TPU v7x, 512 devices: a whole 4x4x16 slice. The times are simulated.
512 devices in a mesh: tm: 64 (over y, z), rows: 8 (over x, core).
Axes of the slice: x: 4, y: 4, z: 16, core: 2. Of those that a mesh axis runs over, the one named last changes fastest.
Arguments:
- states: float32 [128, 64, 640], P('tm'), may hold values from -6 to 6
- ancestors: int32 [128, 640], P('tm'), may hold values from 0 to 639
- tracer_obs: float32 [128, 32], P('tm'), may hold values from -6 to 6
- jitter: float32 [128], P('tm'), may hold values from 0.00390625 to 0.0390625
- fingerprints: float32 [64, 32], replicated, may hold values from -0.75 to 0.75
- tracer_scale: float32 [32], replicated, may hold values from 0.15 to 0.45
- prior_weights: float32 [640], replicated, may hold values from 0.25 to 4
Outputs:
- filtered: float32 [128, 640], P('tm', 'rows')
All inputs are finite; a program needn't handle non-finite values.
Results may differ from a plain program's by a relative error of at most 0.0003.
Values sent between devices are 32-bit elements; how exact they have to be, the bound alone decides.
A program may use at most 64 MiB of HBM per device.

v0:
```python
import jax
import jax.numpy as jnp
from jax import lax
from jax.sharding import PartitionSpec as P


def shifted(block, axis, distance):
    devices = range(lax.axis_size(axis))
    route = [(i - distance, i) for i in devices if i - distance in devices]
    return lax.ppermute(block, axis, route)


def transition(previous, current, parent_ids, observed, mixing, fingerprints, tracer_scale):
    count = current.shape[1]
    highest = lax.Precision.HIGHEST
    inner_prod = lax.dot_general(
        previous,
        current,
        (((0,), (0,)), ((), ())),
        precision=highest,
        preferred_element_type=jnp.float32,
    )
    distance = (
        jnp.sum(previous * previous, axis=0)[:, None]
        + jnp.sum(current * current, axis=0)[None, :]
        - 2.0 * inner_prod
    )
    kernel = jnp.exp(-2.0 * distance / current.shape[0])
    predicted = lax.dot_general(
        fingerprints,
        current,
        (((0,), (0,)), ((), ())),
        precision=highest,
        preferred_element_type=jnp.float32,
    )
    misfit = tracer_scale[:, None] * (observed[:, None] - predicted)
    likelihood = jnp.exp(-0.5 * jnp.sum(misfit * misfit, axis=0))
    parent = (parent_ids[None, :] == jnp.arange(count, dtype=jnp.int32)[:, None]).astype(
        jnp.float32
    )
    weight = likelihood[None, :] * (parent + mixing * kernel)
    return weight * (count / jnp.sum(weight))


def shards(states, ancestors, tracer_obs, jitter, fingerprints, tracer_scale, prior_weights):
    highest = lax.Precision.HIGHEST
    count = states.shape[2]
    own_rows = count // lax.axis_size("rows")
    row_start = lax.axis_index("rows") * own_rows
    time_index = lax.axis_index("tm")
    rim = shifted(states[-1], "tm", 1)
    local_ids = row_start + lax.broadcasted_iota(jnp.int32, (own_rows, count), 0)
    column_ids = lax.broadcasted_iota(jnp.int32, (own_rows, count), 1)
    block_init = (local_ids == column_ids).astype(jnp.float32)

    def accumulate(carry, inputs):
        running, previous = carry
        current, parent_ids, observed, mixing = inputs
        matrix = transition(
            previous, current, parent_ids, observed, mixing, fingerprints, tracer_scale
        )
        running = jnp.dot(running, matrix, precision=highest, preferred_element_type=jnp.float32)
        kept = lax.dynamic_slice_in_dim(matrix, row_start, own_rows, 0)
        return ((running, current), kept)

    (block_part, unused), kept_rows = lax.scan(
        accumulate, (block_init, rim), (states, ancestors, tracer_obs, jitter)
    )
    full_block = lax.all_gather(block_part, "rows", axis=0, tiled=True)
    start = prior_weights / jnp.sum(prior_weights)

    def turn(turn_index, incoming):
        moved = jnp.dot(incoming, full_block, precision=highest, preferred_element_type=jnp.float32)
        moved = moved / jnp.sum(moved)
        received = shifted(moved, "tm", 1)
        return jnp.where(time_index == 0, start, received)

    incoming = lax.fori_loop(0, lax.axis_size("tm") - 1, turn, start)

    def propagate(weights_now, kept):
        mine = lax.dynamic_slice_in_dim(weights_now, row_start, own_rows, 0)
        partial_term = jnp.dot(mine, kept, precision=highest, preferred_element_type=jnp.float32)
        moved = lax.psum(partial_term, "rows")
        moved = moved / jnp.sum(moved)
        return (moved, count * lax.dynamic_slice_in_dim(moved, row_start, own_rows, 0))

    unused_last, filtered = lax.scan(propagate, incoming, kept_rows)
    return filtered


def solution(mesh):
    return jax.shard_map(
        shards,
        mesh=mesh,
        in_specs=(P("tm", None, None), P("tm", None), P("tm", None), P("tm"), P(), P(), P()),
        out_specs=P("tm", "rows"),
        check_vma=False,
    )
```

profile of v0, /device:TPU:25, one launch (start us, length us, event | category | flops | bytes accessed | tf_op | source)
XLA Modules:
  0.0 808.5 jit_solution(13679982750202817545)
XLA Ops:
  11.1 11.5 %collective-permute-done.1 = f32[64,640]{1,0:T(8,128)S(1)} collective-permute-done((f32[64,640]{1,0:T(8,128)S(1)}, f32[64,640]{1,0:T(8,128)S(1)}, u32[]{:S(2)}, u32[]{:S(2)}) %collective-permute-start.1) | collective-permute-done | bytes 163872 | tf_op jit(solution)/shard_map/ppermute | solution.py:10
  22.7 20.1 %while.42 = (s32[]{:T(128)}, f32[80,640]{1,0:T(8,128)S(1)}, f32[64,640]{1,0:T(8,128)S(1)}, f32[2,80,640]{2,1,0:T(8,128)S(1)}, f32[32]{0:T(128)}, /*index=5*/f32[...) while((s32[]{:T(128)}, f32[80,640]{1,0:T(8,128)S(1)}, ...), condition=%wide.region_6.7_spmd, body=%wide.region_1.6_spmd.sunk | while | flops 728267520 | bytes 9130165 | solution.py:66
  44.9 29.3 %all-gather.2.cloned.1.call-done = f32[640,640]{1,0:T(8,128)} async-done(((f32[80,640]{1,0:T(8,128)}), f32[640,640]{1,0:T(8,128)}) %all-gather.2.cloned.1.call-update) | async-done | bytes 1638416 | tf_op jit(solution)/shard_map/all_gather | solution.py:69
  74.2 626.8 %while.43 = (s32[]{:T(128)}, f32[640]{0:T(1024)S(1)}, pred[]{:T(512)}, f32[640,640]{1,0:T(8,128)}, f32[640]{0:T(1024)S(1)}, /*index=5*/s32[]{:T(128)}, f32[]{:T(128)}) while((s32[]{:T(128)}, f32[640]{0:T(1024)S(1)}, pred[]{:T(512)}, f32[640,640]{1,0:T(8,128)}, f32[640]{0:T(1024)S(1)}, /*index=5*/s32[]{:T(128)}, f32[]{:T(128)}) %tuple.76), condition=%wide.region_9.10_spmd, body=%wide.region_7.9_spmd.sunk | while | flops 4917121 | bytes 1674370 | solution.py:78
  90.0 4.5 collective-permute-done
  100.0 4.5 collective-permute-done
  109.9 4.5 collective-permute-done
  119.8 4.5 collective-permute-done
  129.8 4.5 collective-permute-done
  139.7 4.5 collective-permute-done
  149.7 4.5 collective-permute-done
  159.6 4.5 collective-permute-done
  169.5 4.5 collective-permute-done
  179.5 4.5 collective-permute-done
  189.4 4.5 collective-permute-done
  199.4 4.5 collective-permute-done
  209.3 4.5 collective-permute-done
  219.2 4.5 collective-permute-done
  229.2 4.5 collective-permute-done
  239.1 4.5 collective-permute-done
  249.1 4.5 collective-permute-done
  259.0 4.5 collective-permute-done
  269.0 4.5 collective-permute-done
  278.9 4.5 collective-permute-done
  288.8 4.5 collective-permute-done
  298.8 4.5 collective-permute-done
  308.7 4.5 collective-permute-done
  318.7 4.5 collective-permute-done
  328.6 4.5 collective-permute-done
  338.5 4.5 collective-permute-done
  348.5 4.5 collective-permute-done
  358.4 4.5 collective-permute-done
  368.4 4.5 collective-permute-done
  378.3 4.5 collective-permute-done
  388.2 4.5 collective-permute-done
  398.2 4.5 collective-permute-done
  408.1 4.5 collective-permute-done
  418.1 4.5 collective-permute-done
  428.0 4.5 collective-permute-done
  437.9 4.5 collective-permute-done
  447.9 4.5 collective-permute-done
  457.8 4.6 collective-permute-done
  467.8 4.5 collective-permute-done
  477.8 4.5 collective-permute-done
  487.7 4.5 collective-permute-done
  497.6 4.5 collective-permute-done
  507.6 4.5 collective-permute-done
  517.5 4.5 collective-permute-done
  527.5 4.5 collective-permute-done
  537.4 4.5 collective-permute-done
  547.3 4.5 collective-permute-done
  557.3 4.5 collective-permute-done
  567.2 4.5 collective-permute-done
  587.1 4.5 collective-permute-done
  607.0 4.5 collective-permute-done
  616.9 4.5 collective-permute-done
  636.8 4.5 collective-permute-done
  646.8 4.5 collective-permute-done
  666.6 4.5 collective-permute-done
  686.5 4.5 collective-permute-done
  696.5 4.5 collective-permute-done
  701.0 100.1 %while.44 = (s32[]{:T(128)}, f32[640]{0:T(1024)S(1)}, f32[2,80]{1,0:T(2,128)S(1)}, s32[]{:T(128)}, f32[2,80,640]{2,1,0:T(8,128)S(1)}, /*index=5*/s32[]{:T(128)}, f32[]{:T(128)}, s32[]{:T(128)}) while((s32[]{:T(128)}, f32[640]{0:T(1024)S(1)}, f32[2,80]{1,0:T(2,128)S(1)}, s32[]{:T(128)}, f32[2,80,640]{2,1,0:T(8,128)S(1)}, ...), condition=%wide.region_13.14_spmd, body=%wide.region_10.13_spmd.sunk | while | flops 616401 | bytes 222065 | solution.py:87
  701.3 84.1 %psum.10 = f32[640]{0:T(1024)S(1)} all-reduce(f32[640]{0:T(1024)S(1)} %convolution_reduce_fusion.5), channel_id=1, replica_groups=mesh['tm'=64,'rows'=8] {'rows'}, use_global_device_ids=true, to_apply=%region_11.11 | all-reduce | flops 640 | bytes 5120 | tf_op jit(solution)/shard_map/while/body/eval_jaxpr/psum | solution.py:83
  787.2 12.4 %psum.10 = f32[640]{0:T(1024)S(1)} all-reduce(f32[640]{0:T(1024)S(1)} %convolution_reduce_fusion.5), channel_id=1, replica_groups=mesh['tm'=64,'rows'=8] {'rows'}, use_global_device_ids=true, to_apply=%region_11.11 | all-reduce | flops 640 | bytes 5120 | tf_op jit(solution)/shard_map/while/body/eval_jaxpr/psum | solution.py:83
  (435 shorter events, 396.8 us)
Async XLA Ops:
  6.5 67.7 %all-gather.2.cloned.1.call-start = ((), (), s32[]{:S(2)}) async-start(), calls=%async_computation | async-start | bytes 1843200 | tf_op jit(solution)/shard_map/all_gather | solution.py:69
  7.5 15.2 %collective-permute-start.1 = (f32[64,640]{1,0:T(8,128)S(1)}, f32[64,640]{1,0:T(8,128)S(1)}, u32[]{:S(2)}, u32[]{:S(2)}) collective-permute-start(f32[64,640]{1,0:T(8,128)S(1)} %slice_bitcast_fusion), channel_id=1, source_target_pairs={{0,8},{8,16},{16,24},{24,32},{32,40},{40,48},{48,56},{56,64},{64,7... | collective-permute-start | bytes 491528 | tf_op jit(solution)/shard_map/ppermute | solution.py:10
  77.7 6.9 collective-permute-start
  88.1 6.5 collective-permute-start
  98.0 6.5 collective-permute-start
  108.0 6.5 collective-permute-start
  117.9 6.5 collective-permute-start
  127.8 6.5 collective-permute-start
  137.8 6.5 collective-permute-start
  147.7 6.5 collective-permute-start
  157.7 6.5 collective-permute-start
  167.6 6.5 collective-permute-start
  177.6 6.5 collective-permute-start
  187.5 6.5 collective-permute-start
  197.4 6.5 collective-permute-start
  207.4 6.5 collective-permute-start
  217.3 6.5 collective-permute-start
  227.3 6.5 collective-permute-start
  237.2 6.5 collective-permute-start
  247.1 6.5 collective-permute-start
  257.1 6.5 collective-permute-start
  267.0 6.5 collective-permute-start
  277.0 6.5 collective-permute-start
  286.9 6.5 collective-permute-start
  296.8 6.5 collective-permute-start
  306.8 6.5 collective-permute-start
  316.7 6.5 collective-permute-start
  326.7 6.5 collective-permute-start
  336.6 6.5 collective-permute-start
  346.6 6.5 collective-permute-start
  356.5 6.5 collective-permute-start
  366.4 6.5 collective-permute-start
  376.4 6.5 collective-permute-start
  386.3 6.5 collective-permute-start
  396.3 6.5 collective-permute-start
  406.2 6.5 collective-permute-start
  416.1 6.5 collective-permute-start
  426.1 6.5 collective-permute-start
  436.0 6.5 collective-permute-start
  446.0 6.5 collective-permute-start
  455.9 6.5 collective-permute-start
  465.9 6.5 collective-permute-start
  475.8 6.5 collective-permute-start
  485.8 6.5 collective-permute-start
  495.7 6.5 collective-permute-start
  505.7 6.5 collective-permute-start
  515.6 6.5 collective-permute-start
  525.5 6.5 collective-permute-start
  535.5 6.5 collective-permute-start
  545.4 6.5 collective-permute-start
  555.4 6.5 collective-permute-start
  565.3 6.5 collective-permute-start
  575.2 6.5 collective-permute-start
  585.2 6.5 collective-permute-start
  595.1 6.5 collective-permute-start
  605.1 6.5 collective-permute-start
  615.0 6.5 collective-permute-start
  624.9 6.5 collective-permute-start
  634.9 6.5 collective-permute-start
  644.8 6.5 collective-permute-start
  654.8 6.5 collective-permute-start
  664.7 6.5 collective-permute-start
  684.6 6.5 collective-permute-start
  694.5 6.5 collective-permute-start
  (4 other events, 28.6 us)
Sparse Core Ops, SparseCore 0:
  43.6 30.5 all-gather.1
where the time goes:
time: 813 us; the launch traced here: 809 us
  waiting for transfers between devices  326 us (40%)
  matrix products  159 us (20%)
  starting transfers between devices  126 us (15%)
  blocking collectives  96.5 us (12%)
  other arithmetic  77.8 us (10%)
  between operations  13.5 us (2%)
  local copies, waits for them, and re-layouts  8.18 us (1%)
    ppermute x64, waiting for transfers between devices, shifted(): return lax.ppermute(block, axis, route)  296 us
    dot_general x63, matrix products, turn(): jnp.dot(incoming, full_block, precision=highest, preferred_element_type=j...  147 us
    ppermute x64, starting transfers between devices, shifted(): return lax.ppermute(block, axis, route)  126 us
    psum x2, blocking collectives, propagate(): moved = lax.psum(partial_term, 'rows')  96.5 us
    reduce_sum x63, other arithmetic, turn(): moved = moved / jnp.sum(moved)  36.5 us
    div x63, other arithmetic, turn(): moved = moved / jnp.sum(moved)  34.5 us
    all_gather x1, waiting for transfers between devices, shards(): full_block = lax.all_gather(block_part, 'rows', axis=0, tiled=True)  29.3 us
  transfers between devices with their start and end apart: 65, of which 65 were waited for; matrix products, arithmetic and copies ran while one was open for 0% of the time, Pallas kernels for 0%

commit v1 on v0

v1 whole, which is shorter than its diff:
```python
import functools

import jax
import jax.numpy as jnp
from jax import lax
from jax.experimental import pallas as pl
from jax.experimental.pallas import tpu as pltpu
from jax.sharding import PartitionSpec as P

MESH = pl.DeviceIdType.MESH


def shifted(block, axis, distance):
    devices = range(lax.axis_size(axis))
    route = [(i - distance, i) for i in devices if i - distance in devices]
    return lax.ppermute(block, axis, route)


def transition(previous, current, parent_ids, observed, mixing, fingerprints, tracer_scale):
    count = current.shape[1]
    highest = lax.Precision.HIGHEST
    inner_prod = lax.dot_general(
        previous,
        current,
        (((0,), (0,)), ((), ())),
        precision=highest,
        preferred_element_type=jnp.float32,
    )
    distance = (
        jnp.sum(previous * previous, axis=0)[:, None]
        + jnp.sum(current * current, axis=0)[None, :]
        - 2.0 * inner_prod
    )
    kernel = jnp.exp(-2.0 * distance / current.shape[0])
    predicted = lax.dot_general(
        fingerprints,
        current,
        (((0,), (0,)), ((), ())),
        precision=highest,
        preferred_element_type=jnp.float32,
    )
    misfit = tracer_scale[:, None] * (observed[:, None] - predicted)
    likelihood = jnp.exp(-0.5 * jnp.sum(misfit * misfit, axis=0))
    parent = (parent_ids[None, :] == jnp.arange(count, dtype=jnp.int32)[:, None]).astype(
        jnp.float32
    )
    weight = likelihood[None, :] * (parent + mixing * kernel)
    return weight * (count / jnp.sum(weight))


def vec_mat(u_row, mat):
    n = mat.shape[0]
    u_col = jnp.transpose(jnp.broadcast_to(u_row[0:1, :], (128, n)))
    parts = []
    for g in range(n // 128):
        block = mat[:, g * 128:(g + 1) * 128]
        parts.append(jnp.sum(block * u_col, axis=0, keepdims=True))
    return jnp.concatenate(parts, axis=1)


def chain_kernel(steps, b_ref, start_ref, out_ref, recv_buf, send_buf, send_sem, recv_sem):
    me = lax.axis_index("tm")
    row = lax.axis_index("rows")
    last = steps - 1

    barrier = pltpu.get_barrier_semaphore()

    @pl.when(me > 0)
    def _():
        pl.semaphore_signal(barrier, 1, device_id=(me - 1, row), device_id_type=MESH)

    @pl.when(me < last)
    def _():
        pl.semaphore_signal(barrier, 1, device_id=(me + 1, row), device_id_type=MESH)

    @pl.when(jnp.logical_or(me == 0, me == last))
    def _():
        pl.semaphore_wait(barrier, 1)

    @pl.when(jnp.logical_and(me > 0, me < last))
    def _():
        pl.semaphore_wait(barrier, 2)

    copy = pltpu.make_async_remote_copy(
        src_ref=send_buf,
        dst_ref=recv_buf,
        send_sem=send_sem,
        recv_sem=recv_sem,
        device_id=(jnp.minimum(me + 1, last), row),
        device_id_type=MESH,
    )

    @pl.when(me == 0)
    def _():
        out_ref[...] = start_ref[...]

    @pl.when(me > 0)
    def _():
        copy.wait_recv()
        out_ref[...] = recv_buf[...]

    @pl.when(me < last)
    def _():
        v = vec_mat(out_ref[...], b_ref[...])
        v = v / jnp.sum(v)
        send_buf[...] = jnp.broadcast_to(v, send_buf.shape)
        copy.start()
        copy.wait_send()


def chain(block, start, steps):
    count = block.shape[0]
    return pl.pallas_call(
        functools.partial(chain_kernel, steps),
        out_shape=jax.ShapeDtypeStruct((8, count), jnp.float32),
        in_specs=[pl.BlockSpec(memory_space=pltpu.VMEM)] * 2,
        out_specs=pl.BlockSpec(memory_space=pltpu.VMEM),
        scratch_shapes=[
            pltpu.VMEM((8, count), jnp.float32),
            pltpu.VMEM((8, count), jnp.float32),
            pltpu.SemaphoreType.DMA,
            pltpu.SemaphoreType.DMA,
        ],
        compiler_params=pltpu.CompilerParams(collective_id=0, has_side_effects=True),
    )(block, start)


def shards(states, ancestors, tracer_obs, jitter, fingerprints, tracer_scale, prior_weights):
    highest = lax.Precision.HIGHEST
    count = states.shape[2]
    own_rows = count // lax.axis_size("rows")
    row_start = lax.axis_index("rows") * own_rows
    steps = lax.axis_size("tm")
    rim = shifted(states[-1], "tm", 1)

    previous = jnp.concatenate([rim[None], states[:-1]], axis=0)
    matrices = [
        transition(
            previous[s], states[s], ancestors[s], tracer_obs[s], jitter[s], fingerprints, tracer_scale
        )
        for s in range(states.shape[0])
    ]
    block = matrices[0]
    for matrix in matrices[1:]:
        block = jnp.dot(block, matrix, precision=highest, preferred_element_type=jnp.float32)

    start = prior_weights / jnp.sum(prior_weights)
    start8 = jnp.broadcast_to(start[None, :], (8, count))
    incoming = chain(block, start8, steps)[0]

    weights_now = incoming
    rows_out = []
    for matrix in matrices:
        moved = jnp.dot(weights_now, matrix, precision=highest, preferred_element_type=jnp.float32)
        moved = moved / jnp.sum(moved)
        weights_now = moved
        rows_out.append(count * lax.dynamic_slice_in_dim(moved, row_start, own_rows, 0))
    return jnp.stack(rows_out, axis=0)


def solution(mesh):
    return jax.shard_map(
        shards,
        mesh=mesh,
        in_specs=(P("tm", None, None), P("tm", None), P("tm", None), P("tm"), P(), P(), P()),
        out_specs=P("tm", "rows"),
        check_vma=False,
    )
```

time: 813 us -> 236 us (0.29)
  the two profiles are of different devices: /device:TPU:25 before, /device:TPU:504 now
where the time goes in v1:
time: 236 us
  Pallas kernels  204 us (86%)
  matrix products  19.4 us (8%)
  other arithmetic  5.49 us (2%)
  local copies, waits for them, and re-layouts  4.43 us (2%)
    pallas_call x1, Pallas kernels, chain(): pl.pallas_call(functools.partial(chain_kernel, steps), out_shape=jax.Shap...  204 us
    dot_general x2, matrix products, transition(): lax.dot_general(previous, current, (((0,), (0,)), ((), ())), precision=hi...  8.71 us
    dot_general x1, matrix products, shards(): jnp.dot(block, matrix, precision=highest, preferred_element_type=jnp.floa...  5.79 us
  transfers between devices with their start and end apart: 1, of which 0 were waited for; matrix products, arithmetic and copies ran while one was open for 5% of the time, Pallas kernels for 0%

profile of v1, /device:TPU:504, one launch (start us, length us, event | category | flops | bytes accessed | tf_op | source)
XLA Modules:
  0.0 236.0 jit_solution(8792848908651128260)
XLA Ops:
  0.0 0.0 copy-start
  0.0 0.9 slice_bitcast_fusion
  0.9 1.3 collective-permute-start
  2.2 1.0 multiply_reduce_fusion
  3.3 0.8 slice_bitcast_fusion.1
  4.0 0.0 copy-done
  4.0 1.1 fusion.11
  5.2 0.8 slice_reduce_fusion
  6.0 1.3 fusion.32
  7.3 1.1 fusion.12
  8.5 0.0 copy-start.1
  8.5 4.4 %fusion.34 = (f32[]{:T(128)}, f32[640,640]{1,0:T(8,128)S(1)}) fusion(f32[2,64,640]{2,1,0:T(8,128)} %param.7, f32[640]{0:T(1024)S(1)} %get-tuple-element.5, f32[640]{0:T(1024)S(1)} %get-tuple-element.6, f32[]{:T(128)} %bitcast.5, s32[640]{0:T(1024)S(1)} %get-tuple-element.7, f32[640]{0:T(1024)S(1)} %multiply_exponential_fusion), kind=kOutput, calls=%fused_computation.52 | convolution fusion | flops 318668800 | bytes 1976328 | tf_op jit(solution)/shard_map/dot_general | solution.py:22
  13.5 0.0 copy-done.1
  13.5 0.6 reduce_sum.101
  14.1 0.6 broadcast_divide_fusion.2
  14.8 0.0 collective-permute-done
  14.8 4.3 %fusion.33 = (f32[]{:T(128)}, f32[640,640]{1,0:T(8,128)S(1)}) fusion(f32[64,640]{1,0:T(8,128)S(1)} %collective-permute-done, f32[2,64,640]{2,1,0:T(8,128)} %param.7, f32[640]{0:T(1024)S(1)} %get-tuple-element.6, f32[640]{0:T(1024)S(1)} %multiply_reduce_fusion.1, f32[]{:T(128)} %bitcast.2, s32[640]{0:T(1024)S(1)} %get-tuple-element.8, ...), kind=kOutput, calls=%fused_computation.51 | convolution fusion | flops 318668800 | bytes 1976836 | tf_op jit(solution)/shard_map/dot_general | solution.py:22
  19.8 5.8 %fusion.2.b_ref = f32[640,640]{1,0:T(8,128)} fusion(f32[640,640]{1,0:T(8,128)S(1)} %get-tuple-element.16, f32[640,640]{1,0:T(8,128)S(1)} %get-tuple-element.14, f32[]{:T(128)S(6)} %div.36, f32[]{:T(128)S(6)} %div.34), kind=kOutput, calls=%fused_computation.6 | convolution fusion | flops 3146547200 | bytes 4915208 | tf_op jit(solution)/shard_map/dot_general | solution.py:145
  25.6 0.6 broadcast_in_dim.2.start_ref
  26.2 204.0 %shard_map.73 = f32[8,640]{1,0:T(8,128)} custom-call(f32[640,640]{1,0:T(8,128)} %fusion.2.b_ref, f32[8,640]{1,0:T(8,128)} %broadcast_in_dim.2.start_ref), custom_call_target="tpu_custom_call" | custom-call | tf_op jit(solution)/shard_map/pallas_call | solution.py:113
  230.2 1.7 fusion.13
  231.9 0.6 reduce_sum.102
  232.5 0.6 broadcast_divide_fusion.1
  233.1 1.0 fusion.16
  234.1 0.6 reduce_sum.103
  234.7 0.6 broadcast_divide_fusion
  235.4 0.1 multiply_bitcast_fusion
  235.4 0.6 pad_maximum_fusion
  (4 shorter events, 0.0 us)
Async XLA Ops:
  0.0 4.0 %copy-start = (f32[64,32]{0,1:T(8,128)S(1)}, f32[64,32]{0,1:T(8,128)}, u32[]{:S(2)}) copy-start(f32[64,32]{0,1:T(8,128)} %param.11) | copy-start | bytes 24580
  0.9 13.8 %collective-permute-start = (f32[64,640]{1,0:T(8,128)S(1)}, f32[64,640]{1,0:T(8,128)S(1)}, u32[]{:S(2)}, u32[]{:S(2)}) collective-permute-start(f32[64,640]{1,0:T(8,128)S(1)} %slice_bitcast_fusion), channel_id=1, source_target_pairs={{0,8},{8,16},{16,24},{24,32},{32,40},{40,48},{48,56},{56,64},{64,7... | collective-permute-start | bytes 491528 | tf_op jit(solution)/shard_map/ppermute | solution.py:16
  8.5 5.0 %copy-start.1 = (f32[640]{0:T(1024)S(1)}, f32[640]{0:T(1024)}, u32[]{:S(2)}) copy-start(f32[640]{0:T(1024)} %param.13) | copy-start | bytes 7684

commit v2 on v1

v2 whole, which is shorter than its diff:
```python
import functools

import jax
import jax.numpy as jnp
from jax import lax
from jax.experimental import pallas as pl
from jax.experimental.pallas import tpu as pltpu
from jax.sharding import PartitionSpec as P

MESH = pl.DeviceIdType.MESH


def shifted(block, axis, distance):
    devices = range(lax.axis_size(axis))
    route = [(i - distance, i) for i in devices if i - distance in devices]
    return lax.ppermute(block, axis, route)


def transition(previous, current, parent_ids, observed, mixing, fingerprints, tracer_scale):
    count = current.shape[1]
    highest = lax.Precision.HIGHEST
    inner_prod = lax.dot_general(
        previous,
        current,
        (((0,), (0,)), ((), ())),
        precision=highest,
        preferred_element_type=jnp.float32,
    )
    distance = (
        jnp.sum(previous * previous, axis=0)[:, None]
        + jnp.sum(current * current, axis=0)[None, :]
        - 2.0 * inner_prod
    )
    kernel = jnp.exp(-2.0 * distance / current.shape[0])
    predicted = lax.dot_general(
        fingerprints,
        current,
        (((0,), (0,)), ((), ())),
        precision=highest,
        preferred_element_type=jnp.float32,
    )
    misfit = tracer_scale[:, None] * (observed[:, None] - predicted)
    likelihood = jnp.exp(-0.5 * jnp.sum(misfit * misfit, axis=0))
    parent = (parent_ids[None, :] == jnp.arange(count, dtype=jnp.int32)[:, None]).astype(
        jnp.float32
    )
    weight = likelihood[None, :] * (parent + mixing * kernel)
    return weight * (count / jnp.sum(weight))


def vec_mat(u_row, mat):
    n = mat.shape[0]
    u_col = jnp.transpose(jnp.broadcast_to(u_row[0:1, :], (128, n)))
    parts = []
    for g in range(n // 128):
        block = mat[:, g * 128:(g + 1) * 128]
        parts.append(jnp.sum(block * u_col, axis=0, keepdims=True))
    return jnp.concatenate(parts, axis=1)


def normalized(v):
    return v / jnp.sum(v)


def chain_kernel(
    steps, before_ref, block_ref, first_ref, second_ref, start_ref,
    out_ref, recv_buf, send_buf, send_sem, recv_sem,
):
    me = lax.axis_index("tm")
    row = lax.axis_index("rows")
    last = steps - 1
    even = me % 2 == 0

    barrier = pltpu.get_barrier_semaphore()

    def greet(other):
        pl.semaphore_signal(barrier, 1, device_id=(other, row), device_id_type=MESH)

    @pl.when(even)
    def _():
        greet(me + 1)

        @pl.when(me + 2 <= last)
        def _():
            greet(me + 2)

        @pl.when(me >= 2)
        def _():
            greet(me - 2)

    @pl.when(jnp.logical_not(even))
    def _():
        greet(me - 1)

    partners = jnp.where(
        even, 1 + (me + 2 <= last).astype(jnp.int32) + (me >= 2).astype(jnp.int32), 1
    )

    @pl.when(partners == 1)
    def _():
        pl.semaphore_wait(barrier, 1)

    @pl.when(partners == 2)
    def _():
        pl.semaphore_wait(barrier, 2)

    @pl.when(partners == 3)
    def _():
        pl.semaphore_wait(barrier, 3)

    def copy_to(other, slot):
        return pltpu.make_async_remote_copy(
            src_ref=send_buf,
            dst_ref=recv_buf,
            send_sem=send_sem.at[slot],
            recv_sem=recv_sem,
            device_id=(other, row),
            device_id_type=MESH,
        )

    near = copy_to(jnp.minimum(me + 1, last), 0)
    far = copy_to(jnp.minimum(me + 2, last), 1)

    @pl.when(me == 0)
    def _():
        out_ref[...] = start_ref[...]

    @pl.when(jnp.logical_and(even, me > 0))
    def _():
        near.wait_recv()
        u = normalized(vec_mat(recv_buf[...], before_ref[...]))
        out_ref[...] = jnp.broadcast_to(u, out_ref.shape)

    @pl.when(jnp.logical_not(even))
    def _():
        near.wait_recv()
        out_ref[...] = recv_buf[...]

    @pl.when(even)
    def _():
        v = normalized(vec_mat(out_ref[...], block_ref[...]))
        send_buf[...] = jnp.broadcast_to(v, send_buf.shape)
        near.start()

        @pl.when(me + 2 <= last)
        def _():
            far.start()

    incoming = out_ref[...]
    w_first = normalized(vec_mat(incoming, first_ref[...]))
    w_second = normalized(vec_mat(jnp.broadcast_to(w_first, incoming.shape), second_ref[...]))
    out_ref[...] = jnp.concatenate(
        [w_first, w_second, jnp.zeros((incoming.shape[0] - 2, incoming.shape[1]), jnp.float32)],
        axis=0,
    )

    @pl.when(even)
    def _():
        near.wait_send()

        @pl.when(me + 2 <= last)
        def _():
            far.wait_send()


def chain(before, block, first, second, start, steps):
    count = block.shape[0]
    return pl.pallas_call(
        functools.partial(chain_kernel, steps),
        out_shape=jax.ShapeDtypeStruct((8, count), jnp.float32),
        in_specs=[pl.BlockSpec(memory_space=pltpu.VMEM)] * 5,
        out_specs=pl.BlockSpec(memory_space=pltpu.VMEM),
        scratch_shapes=[
            pltpu.VMEM((8, count), jnp.float32),
            pltpu.VMEM((8, count), jnp.float32),
            pltpu.SemaphoreType.DMA((2,)),
            pltpu.SemaphoreType.DMA,
        ],
        compiler_params=pltpu.CompilerParams(collective_id=0, has_side_effects=True),
    )(before, block, first, second, start)


def block_product(matrices):
    block = matrices[0]
    for matrix in matrices[1:]:
        block = jnp.dot(
            block, matrix, precision=lax.Precision.HIGHEST, preferred_element_type=jnp.float32
        )
    return block


def shards(states, ancestors, tracer_obs, jitter, fingerprints, tracer_scale, prior_weights):
    count = states.shape[2]
    own_rows = count // lax.axis_size("rows")
    row_start = lax.axis_index("rows") * own_rows
    steps = lax.axis_size("tm")
    local = states.shape[0]

    states_before = shifted(states, "tm", 1)
    ancestors_before = shifted(ancestors, "tm", 1)
    obs_before = shifted(tracer_obs, "tm", 1)
    jitter_before = shifted(jitter, "tm", 1)
    rim_before = shifted(states[-1], "tm", 2)

    def matrices_of(rim, block_states, parents, observed, mixing):
        previous = jnp.concatenate([rim[None], block_states[:-1]], axis=0)
        return [
            transition(
                previous[s], block_states[s], parents[s], observed[s], mixing[s],
                fingerprints, tracer_scale,
            )
            for s in range(local)
        ]

    own = matrices_of(states_before[-1], states, ancestors, tracer_obs, jitter)
    before = matrices_of(rim_before, states_before, ancestors_before, obs_before, jitter_before)

    start = prior_weights / jnp.sum(prior_weights)
    start8 = jnp.broadcast_to(start[None, :], (8, count))
    weights = chain(block_product(before), block_product(own), own[0], own[1], start8, steps)
    mine = lax.dynamic_slice_in_dim(weights[:local], row_start, own_rows, 1)
    return count * mine


def solution(mesh):
    return jax.shard_map(
        shards,
        mesh=mesh,
        in_specs=(P("tm", None, None), P("tm", None), P("tm", None), P("tm"), P(), P(), P()),
        out_specs=P("tm", "rows"),
        check_vma=False,
    )
```

time: 236 us -> 213 us (0.903)
  Pallas kernels: 204 us -> 155 us
  matrix products: 19.4 us -> 34.3 us
  starting transfers between devices: 1.29 us -> 6.58 us
    pallas_call x1, Pallas kernels: 204 us -> 155 us  [chain(): pl.pallas_call(functools.partial(chain_kernel, steps), out_shape=jax.Shap...]
    dot_general x2 -> x4, matrix products: 8.71 us -> 17.3 us  [transition(): lax.dot_general(previous, current, (((0,), (0,)), ((), ())), precision=hi...]
    dot_general x3 -> x2, matrix products: 8.43 us -> 14.3 us  [block_product(): jnp.dot(block, matrix, precision=lax.Precision.HIGHEST, preferred_element...]
    ppermute x1 -> x5, starting transfers between devices: 1.29 us -> 6.58 us  [shifted(): return lax.ppermute(block, axis, route)]
    mul x0 -> x3, other arithmetic: none -> 3.72 us  [the longest x2 3.08 us: transition(): return weight * (count / jnp.sum(weight))]
  transfers between devices with their start and end apart: 1 -> 5, of which waited for: 0 -> 0; matrix products, arithmetic and copies ran while one was open for 5% -> 8% of each run, Pallas kernels for 0% -> 0%
where the time goes in v2:
time: 213 us; the launch traced here: 212 us
  Pallas kernels  155 us (73%)
  matrix products  34.3 us (16%)
  other arithmetic  7.58 us (4%)
  starting transfers between devices  6.58 us (3%)
  local copies, waits for them, and re-layouts  5.86 us (3%)
  between operations  2.79 us (1%)
    pallas_call x1, Pallas kernels, chain(): pl.pallas_call(functools.partial(chain_kernel, steps), out_shape=jax.Shap...  155 us
    dot_general x4, matrix products, transition(): lax.dot_general(previous, current, (((0,), (0,)), ((), ())), precision=hi...  17.3 us
    dot_general x2, matrix products, block_product(): jnp.dot(block, matrix, precision=lax.Precision.HIGHEST, preferred_element...  14.3 us
    ppermute x5, starting transfers between devices, shifted(): return lax.ppermute(block, axis, route)  6.58 us
  transfers between devices with their start and end apart: 5, of which 0 were waited for; matrix products, arithmetic and copies ran while one was open for 8% of the time, Pallas kernels for 0%

profile of v2, /device:TPU:504, one launch (start us, length us, event | category | flops | bytes accessed | tf_op | source)
XLA Modules:
  0.0 212.1 jit_solution(3328889970522824964)
XLA Ops:
  0.0 0.0 copy-start
  0.0 1.4 collective-permute-start.1
  1.4 1.3 collective-permute-start
  2.7 0.9 slice_bitcast_fusion.2
  3.7 1.3 collective-permute-start.4
  5.0 1.3 collective-permute-start.2
  6.3 1.3 collective-permute-start.3
  7.6 1.0 multiply_reduce_fusion
  8.6 0.8 slice_bitcast_fusion.9
  9.4 0.8 slice_reduce_fusion.2
  10.1 1.3 fusion.26
  11.5 0.0 copy-done
  11.5 1.1 fusion.7
  12.6 1.2 fusion.8
  13.8 1.4 reduce_sum.151
  15.2 1.4 broadcast_divide_fusion
  16.5 5.5 %fusion.29 = (f32[]{:T(128)}, f32[640,640]{1,0:T(8,128)}) fusion(f32[2,64,640]{2,1,0:T(8,128)} %param.7, f32[640]{0:T(1024)S(1)} %get-tuple-element.5, f32[640]{0:T(1024)S(1)} %get-tuple-element.6, f32[]{:T(128)} %bitcast.11, s32[640]{0:T(1024)S(1)} %get-tuple-element.9, f32[640]{0:T(1024)S(1)} %multiply_exponential_fusion), kind=kOutput, calls=%fused_computation.65 | convolution fusion | flops 318668800 | bytes 1976328 | tf_op jit(solution)/shard_map/dot_general | solution.py:22
  22.7 0.0 copy-start.6
  22.7 1.5 broadcast_multiply_fusion.second_ref
  24.2 0.0 copy-start.1
  24.2 0.0 collective-permute-done.3
  24.2 0.7 fusion.27
  24.9 0.0 collective-permute-done
  24.9 0.0 collective-permute-done.2
  25.0 0.0 collective-permute-done.4
  25.0 0.0 collective-permute-done.1
  25.0 0.2 fusion.20
  25.2 0.0 copy-done.6
  25.3 0.2 multiply_reduce_fusion.5
  25.6 1.5 fusion.17
  27.0 0.0 copy-start.4
  27.1 0.0 copy-start.3
  27.1 5.6 %fusion.11 = (f32[]{:T(128)}, f32[]{:T(128)}, f32[640,640]{1,0:T(8,128)}) fusion(f32[640]{0:T(1024)S(1)} %get-tuple-element.7, f32[640]{0:T(1024)S(1)} %multiply_reduce_fusion.3, f32[]{:T(128)} %bitcast.2, s32[640]{0:T(1024)S(1)} %get-tuple-element.11, f32[640]{0:T(1024)S(1)} %get-tuple-element.31, f32[640,640]{1,0:T(8,128)S(1)} %fusion.17, ...), kind=kOutput, calls=%fused_computation.23 | convolution fusion | flops 322764800 | bytes 3637264 | tf_op jit(solution)/shard_map/dot_general | solution.py:22
  32.7 0.0 copy-done.4
  34.0 0.0 copy-done.3
  34.0 4.6 %fusion.28 = (f32[]{:T(128)}, f32[640,640]{1,0:T(8,128)}) fusion(f32[2,64,640]{2,1,0:T(8,128)S(1)} %copy-done.3, f32[2,64,640]{2,1,0:T(8,128)S(1)} %collective-permute-done.1, f32[640]{0:T(1024)S(1)} %get-tuple-element.6, f32[640]{0:T(1024)S(1)} %get-tuple-element.8, f32[]{:T(128)} %bitcast.9, s32[640]{0:T(1024)S(1)} %get-tuple-element.10, ...), kind=kOutput, calls=%fused_computation.64 | convolution fusion | flops 318668800 | bytes 1982472 | tf_op jit(solution)/shard_map/dot_general | solution.py:22
  39.3 1.5 broadcast_multiply_fusion.1.first_ref
  40.8 0.0 copy-done.1
  40.8 0.0 copy-start.2
  40.9 0.0 copy-start.5
  40.9 0.0 copy-start.7
  40.9 6.0 %fusion.30.block_ref = f32[640,640]{1,0:T(8,128)} fusion(f32[640,640]{1,0:T(8,128)S(1)} %broadcast_multiply_fusion.1.first_ref, f32[640,640]{1,0:T(8,128)S(1)} %broadcast_multiply_fusion.second_ref), kind=kOutput, calls=%fused_computation.66 | convolution fusion | flops 3145728000 | bytes 4915200 | tf_op jit(solution)/shard_map/dot_general | solution.py:186
  46.9 0.0 copy-done.2
  46.9 0.0 copy-done.5
  46.9 0.0 copy-done.7
  46.9 8.3 %fusion.before_ref = f32[640,640]{1,0:T(8,128)} fusion(f32[]{:T(128)S(6)} %div.36, f32[]{:T(128)S(6)} %div.34, f32[640,640]{1,0:T(8,128)S(1)} %copy-done.7, f32[640]{0:T(1024)S(1)} %get-tuple-element.7, f32[640]{0:T(1024)S(1)} %multiply_reduce_fusion.3, f32[]{:T(128)} %bitcast.2, s32[640]{0:T(1024)S(1)} %get-tuple-element.11, ...), kind=kOutput, calls=%fused_computation.4 | convolution fusion | flops 3153920000 | bytes 4933136 | tf_op jit(solution)/shard_map/dot_general | solution.py:186
  55.2 0.6 broadcast_in_dim.2.start_ref
  55.8 155.0 %shard_map.73 = f32[8,640]{1,0:T(8,128)} custom-call(f32[640,640]{1,0:T(8,128)} %fusion.before_ref, f32[640,640]{1,0:T(8,128)} %fusion.30.block_ref, f32[640,640]{1,0:T(8,128)} %copy-done.2, f32[640,640]{1,0:T(8,128)} %copy-done.1, f32[8,640]{1,0:T(8,128)} %broadcast_in_dim.2.start_ref), custom_call_target="tpu_custom_call" | custom-call | tf_op jit(solution)/shard_map/pallas_call | solution.py:168
  210.8 0.7 slice.71
  211.5 0.6 dynamic-slice_multiply_fusion
  (7 shorter events, 0.1 us)
Async XLA Ops:
  0.0 11.5 %copy-start = (f32[64,32]{0,1:T(8,128)S(1)}, f32[64,32]{0,1:T(8,128)}, u32[]{:S(2)}) copy-start(f32[64,32]{0,1:T(8,128)} %param.11) | copy-start | bytes 24580
  0.0 25.0 %collective-permute-start.1 = (f32[2,64,640]{2,1,0:T(8,128)}, f32[2,64,640]{2,1,0:T(8,128)S(1)}, u32[]{:S(2)}, u32[]{:S(2)}) collective-permute-start(f32[2,64,640]{2,1,0:T(8,128)} %param.7), channel_id=1, source_target_pairs={{0,8},{8,16},{16,24},{24,32},{32,40},{40,48},{48,56},{56,64},{64,7... | collective-permute-start | bytes 983048 | tf_op jit(solution)/shard_map/ppermute | solution.py:16
  1.4 23.5 %collective-permute-start = (f32[2,32]{1,0:T(2,128)}, f32[2,32]{1,0:T(2,128)S(1)}, u32[]{:S(2)}, u32[]{:S(2)}) collective-permute-start(f32[2,32]{1,0:T(2,128)} %param.9), channel_id=1, source_target_pairs={{0,8},{8,16},{16,24},{24,32},{32,40},{40,48},{48,56},{56,64},{64,7... | collective-permute-start | bytes 776 | tf_op jit(solution)/shard_map/ppermute | solution.py:16
  3.7 21.3 %collective-permute-start.4 = (f32[64,640]{1,0:T(8,128)S(1)}, f32[64,640]{1,0:T(8,128)S(1)}, u32[]{:S(2)}, u32[]{:S(2)}) collective-permute-start(f32[64,640]{1,0:T(8,128)S(1)} %slice_bitcast_fusion.2), channel_id=1, source_target_pairs={{0,16},{8,24},{16,32},{24,40},{32,48},{40,56},{48,64},{56,72},{64,... | collective-permute-start | bytes 491528 | tf_op jit(solution)/shard_map/ppermute | solution.py:16
  5.0 20.0 %collective-permute-start.2 = (s32[2,640]{1,0:T(2,128)}, s32[2,640]{1,0:T(2,128)S(1)}, u32[]{:S(2)}, u32[]{:S(2)}) collective-permute-start(s32[2,640]{1,0:T(2,128)} %param.8), channel_id=1, source_target_pairs={{0,8},{8,16},{16,24},{24,32},{32,40},{40,48},{48,56},{56,64},{64,7... | collective-permute-start | bytes 15368 | tf_op jit(solution)/shard_map/ppermute | solution.py:16
  6.3 18.0 %collective-permute-start.3 = (f32[2]{0:T(128)}, f32[2]{0:T(128)S(1)}, u32[]{:S(2)}, u32[]{:S(2)}) collective-permute-start(f32[2]{0:T(128)} %param.10), channel_id=1, source_target_pairs={{0,8},{8,16},{16,24},{24,32},{32,40},{40,48},{48,56},{56,64},{64,7... | collective-permute-start | bytes 32 | tf_op jit(solution)/shard_map/ppermute | solution.py:16
  22.7 2.6 %copy-start.6 = (f32[32]{0:T(128)S(1)}, f32[32]{0:T(128)}, u32[]{:S(2)}) copy-start(f32[32]{0:T(128)} %param.12) | copy-start | bytes 388
  24.2 16.6 %copy-start.1 = (f32[640,640]{1,0:T(8,128)}, f32[640,640]{1,0:T(8,128)S(1)}, u32[]{:S(2)}) copy-start(f32[640,640]{1,0:T(8,128)S(1)} %broadcast_multiply_fusion.second_ref) | copy-start | bytes 4915204
  27.0 5.7 %copy-start.4 = (f32[640,640]{1,0:T(8,128)}, f32[640,640]{1,0:T(8,128)S(1)}, u32[]{:S(2)}) copy-start(f32[640,640]{1,0:T(8,128)S(1)} %fusion.17) | copy-start | bytes 4915204
  27.1 6.9 %copy-start.3 = (f32[2,64,640]{2,1,0:T(8,128)S(1)}, f32[2,64,640]{2,1,0:T(8,128)}, u32[]{:S(2)}) copy-start(f32[2,64,640]{2,1,0:T(8,128)} %param.7) | copy-start | bytes 983044
  40.8 6.0 %copy-start.2 = (f32[640,640]{1,0:T(8,128)}, f32[640,640]{1,0:T(8,128)S(1)}, u32[]{:S(2)}) copy-start(f32[640,640]{1,0:T(8,128)S(1)} %broadcast_multiply_fusion.1.first_ref) | copy-start | bytes 4915204
  40.9 6.0 %copy-start.5 = (f32[640,640]{1,0:T(8,128)S(1)}, f32[640,640]{1,0:T(8,128)}, u32[]{:S(2)}) copy-start(f32[640,640]{1,0:T(8,128)} %copy-done.4) | copy-start | bytes 4915204
  40.9 6.0 %copy-start.7 = (f32[640,640]{1,0:T(8,128)S(1)}, f32[640,640]{1,0:T(8,128)}, u32[]{:S(2)}) copy-start(f32[640,640]{1,0:T(8,128)} %get-tuple-element.25) | copy-start | bytes 4915204

commit v3 on v2

--- a/solution.py
+++ b/solution.py
@@ -63,7 +63,7 @@
 
 
 def chain_kernel(
-    steps, before_ref, block_ref, first_ref, second_ref, start_ref,
+    steps, before_ref, block_ref, combined_ref, first_ref, second_ref, start_ref,
     out_ref, recv_buf, send_buf, send_sem, recv_sem,
 ):
     me = lax.axis_index("tm")
@@ -124,27 +124,30 @@
     @pl.when(me == 0)
     def _():
         out_ref[...] = start_ref[...]
+        v = normalized(vec_mat(start_ref[...], block_ref[...]))
+        send_buf[...] = jnp.broadcast_to(v, send_buf.shape)
+        near.start()
+        far.start()
 
     @pl.when(jnp.logical_and(even, me > 0))
     def _():
         near.wait_recv()
-        u = normalized(vec_mat(recv_buf[...], before_ref[...]))
+        received = recv_buf[...]
+        v = normalized(vec_mat(received, combined_ref[...]))
+        send_buf[...] = jnp.broadcast_to(v, send_buf.shape)
+        near.start()
+
+        @pl.when(me + 2 <= last)
+        def _():
+            far.start()
+
+        u = normalized(vec_mat(received, before_ref[...]))
         out_ref[...] = jnp.broadcast_to(u, out_ref.shape)
 
     @pl.when(jnp.logical_not(even))
     def _():
         near.wait_recv()
         out_ref[...] = recv_buf[...]
-
-    @pl.when(even)
-    def _():
-        v = normalized(vec_mat(out_ref[...], block_ref[...]))
-        send_buf[...] = jnp.broadcast_to(v, send_buf.shape)
-        near.start()
-
-        @pl.when(me + 2 <= last)
-        def _():
-            far.start()
 
     incoming = out_ref[...]
     w_first = normalized(vec_mat(incoming, first_ref[...]))
@@ -163,12 +166,12 @@
             far.wait_send()
 
 
-def chain(before, block, first, second, start, steps):
+def chain(before, block, combined, first, second, start, steps):
     count = block.shape[0]
     return pl.pallas_call(
         functools.partial(chain_kernel, steps),
         out_shape=jax.ShapeDtypeStruct((8, count), jnp.float32),
-        in_specs=[pl.BlockSpec(memory_space=pltpu.VMEM)] * 5,
+        in_specs=[pl.BlockSpec(memory_space=pltpu.VMEM)] * 6,
         out_specs=pl.BlockSpec(memory_space=pltpu.VMEM),
         scratch_shapes=[
             pltpu.VMEM((8, count), jnp.float32),
@@ -177,14 +180,14 @@
             pltpu.SemaphoreType.DMA,
         ],
         compiler_params=pltpu.CompilerParams(collective_id=0, has_side_effects=True),
-    )(before, block, first, second, start)
+    )(before, block, combined, first, second, start)
 
 
 def block_product(matrices):
     block = matrices[0]
     for matrix in matrices[1:]:
         block = jnp.dot(
-            block, matrix, precision=lax.Precision.HIGHEST, preferred_element_type=jnp.float32
+            block, matrix, precision=lax.Precision.HIGH, preferred_element_type=jnp.float32
         )
     return block
 
@@ -196,10 +199,20 @@
     steps = lax.axis_size("tm")
     local = states.shape[0]
 
-    states_before = shifted(states, "tm", 1)
-    ancestors_before = shifted(ancestors, "tm", 1)
-    obs_before = shifted(tracer_obs, "tm", 1)
-    jitter_before = shifted(jitter, "tm", 1)
+    count_pad = jnp.zeros((local, count - tracer_obs.shape[1] - 1), jnp.float32)
+    extra = jnp.concatenate(
+        [
+            ancestors.astype(jnp.float32)[:, None, :],
+            jnp.concatenate([tracer_obs, jitter[:, None], count_pad], axis=1)[:, None, :],
+        ],
+        axis=1,
+    )
+    packed_before = shifted(jnp.concatenate([states, extra], axis=1), "tm", 1)
+    dims = states.shape[1]
+    states_before = packed_before[:, :dims, :]
+    ancestors_before = packed_before[:, dims, :].astype(jnp.int32)
+    obs_before = packed_before[:, dims + 1, : tracer_obs.shape[1]]
+    jitter_before = packed_before[:, dims + 1, tracer_obs.shape[1]]
     rim_before = shifted(states[-1], "tm", 2)
 
     def matrices_of(rim, block_states, parents, observed, mixing):
@@ -217,7 +230,10 @@
 
     start = prior_weights / jnp.sum(prior_weights)
     start8 = jnp.broadcast_to(start[None, :], (8, count))
-    weights = chain(block_product(before), block_product(own), own[0], own[1], start8, steps)
+    block_before = block_product(before)
+    block_own = block_product(own)
+    combined = block_product([block_before, block_own])
+    weights = chain(block_before, block_own, combined, own[0], own[1], start8, steps)
     mine = lax.dynamic_slice_in_dim(weights[:local], row_start, own_rows, 1)
     return count * mine
 

time: 213 us -> 188 us (0.88)
  Pallas kernels: 155 us -> 134 us
  matrix products: 34.3 us -> 30.2 us
  starting transfers between devices: 6.58 us -> 2.58 us
  waiting for transfers between devices: 0.01 us -> 2.76 us
    pallas_call x1, Pallas kernels: 155 us -> 134 us  [chain(): pl.pallas_call(functools.partial(chain_kernel, steps), out_shape=jax.Shap...]
    dot_general x2 -> x3, matrix products: 14.3 us -> 10 us  [block_product(): jnp.dot(block, matrix, precision=lax.Precision.HIGH, preferred_element_ty...]
    ppermute x5 -> x2, starting transfers between devices: 6.58 us -> 2.58 us  [shifted(): return lax.ppermute(block, axis, route)]
    ppermute x5 -> x2, waiting for transfers between devices: 0.01 us -> 2.76 us  [shifted(): return lax.ppermute(block, axis, route)]
  transfers between devices with their start and end apart: 5 -> 2, of which waited for: 0 -> 1; matrix products, arithmetic and copies ran while one was open for 8% -> 7% of each run, Pallas kernels for 0% -> 0%
where the time goes in v3:
time: 188 us
  Pallas kernels  134 us (71%)
  matrix products  30.2 us (16%)
  other arithmetic  8.41 us (4%)
  local copies, waits for them, and re-layouts  6.65 us (4%)
  between operations  3.15 us (2%)
  waiting for transfers between devices  2.76 us (1%)
  starting transfers between devices  2.58 us (1%)
    pallas_call x1, Pallas kernels, chain(): pl.pallas_call(functools.partial(chain_kernel, steps), out_shape=jax.Shap...  134 us
    dot_general x4, matrix products, transition(): lax.dot_general(previous, current, (((0,), (0,)), ((), ())), precision=hi...  18.4 us
    dot_general x3, matrix products, block_product(): jnp.dot(block, matrix, precision=lax.Precision.HIGH, preferred_element_ty...  10 us
  transfers between devices with their start and end apart: 2, of which 1 were waited for; matrix products, arithmetic and copies ran while one was open for 7% of the time, Pallas kernels for 0%

profile of v3, /device:TPU:504, one launch (start us, length us, event | category | flops | bytes accessed | tf_op | source)
XLA Modules:
  0.0 187.9 jit_solution(8169002345433085378)
XLA Ops:
  0.0 0.0 copy-start
  0.0 0.0 copy-start.5
  0.0 0.0 copy-start.7
  0.0 0.0 copy-start.6
  0.0 0.8 copy.11
  0.8 0.1 pad.5.clone
  0.9 0.8 maximum_bitcast_fusion
  1.7 0.7 convert_bitcast_fusion
  2.4 1.0 pad_maximum_fusion
  3.4 1.3 collective-permute-start
  4.7 0.9 slice_bitcast_fusion.2
  5.6 1.3 collective-permute-start.1
  6.9 1.0 multiply_reduce_fusion
  7.9 0.8 slice_bitcast_fusion.13
  8.7 0.8 slice_reduce_fusion.2
  9.5 1.3 fusion.31
  10.8 0.0 copy-done
  10.8 1.1 fusion.12
  12.0 0.0 copy-done.5
  12.0 0.0 copy-done.7
  12.0 0.2 fusion.13
  12.2 0.0 copy-done.6
  12.2 0.6 reduce_sum.151
  12.8 4.6 %fusion.34 = (f32[]{:T(128)}, f32[640,640]{1,0:T(8,128)}) fusion(f32[2,64,640]{2,1,0:T(8,128)S(1)} %copy-done.5, f32[640]{0:T(1024)S(1)} %get-tuple-element.7, f32[640]{0:T(1024)S(1)} %get-tuple-element.8, f32[]{:T(128)} %bitcast.15, s32[640]{0:T(1024)S(1)} %get-tuple-element.9, f32[640]{0:T(1024)S(1)} %multiply_exponential_fusion), kind=kOutput, calls=%fused_computation.74 | convolution fusion | flops 318668800 | bytes 1976328 | tf_op jit(solution)/shard_map/dot_general | solution.py:22
  18.2 1.5 broadcast_multiply_fusion.second_ref
  19.7 0.0 copy-start.2
  19.7 0.5 broadcast_divide_fusion
  20.3 2.8 %collective-permute-done.1 = f32[64,640]{1,0:T(8,128)S(1)} collective-permute-done((f32[64,640]{1,0:T(8,128)S(1)}, f32[64,640]{1,0:T(8,128)S(1)}, u32[]{:S(2)}, u32[]{:S(2)}) %collective-permute-start.1) | collective-permute-done | bytes 163872 | tf_op jit(solution)/shard_map/ppermute | solution.py:16
  23.1 0.0 collective-permute-done
  23.1 0.2 fusion.23
  23.4 0.2 multiply_reduce_fusion.4
  23.7 0.6 fusion.30
  24.2 4.6 %fusion.16 = (f32[]{:T(128)}, f32[640,640]{1,0:T(8,128)}) fusion(f32[640]{0:T(1024)S(1)} %get-tuple-element.5, f32[640]{0:T(1024)S(1)} %get-tuple-element.6, f32[]{:T(128)} %bitcast.10, s32[640]{0:T(1024)S(1)} %get-tuple-element.11, f32[640]{0:T(1024)S(1)} %get-tuple-element.31, f32[2,66,640]{2,1,0:T(8,128)S(1)} %collective-permute-done), kind=kOutput, calls=%fused_computation.28 | convolution fusion | flops 318668800 | bytes 1982472 | tf_op jit(solution)/shard_map/dot_general | solution.py:22
  29.6 4.5 %fusion.32 = (f32[]{:T(128)}, f32[640,640]{0,1:T(8,128)}) fusion(f32[64,640]{1,0:T(8,128)S(1)} %collective-permute-done.1, f32[2,66,640]{2,1,0:T(8,128)S(1)} %collective-permute-done, f32[640]{0:T(1024)S(1)} %get-tuple-element.6, f32[640]{0:T(1024)S(1)} %multiply_reduce_fusion.3, f32[]{:T(128)} %bitcast.5, s32[640]{0:T(1024)S(1)} %get-tuple-element.12, ...), kind=kOutput, calls=%fused_computation.72 | convolution fusion | flops 318668800 | bytes 1982472 | tf_op jit(solution)/shard_map/dot_general | solution.py:22
  34.8 4.6 %fusion.33 = (f32[]{:T(128)}, f32[640,640]{1,0:T(8,128)}) fusion(f32[2,64,640]{2,1,0:T(8,128)S(1)} %copy-done.5, f32[2,66,640]{2,1,0:T(8,128)S(1)} %collective-permute-done, f32[640]{0:T(1024)S(1)} %get-tuple-element.8, f32[640]{0:T(1024)S(1)} %get-tuple-element.5, f32[]{:T(128)} %bitcast.13, s32[640]{0:T(1024)S(1)} %get-tuple-element.10, ...), kind=kOutput, calls=%fused_computation.73 | convolution fusion | flops 318668800 | bytes 1982472 | tf_op jit(solution)/shard_map/dot_general | solution.py:22
  40.1 1.5 broadcast_multiply_fusion.1.first_ref
  41.7 0.0 copy-done.2
  41.7 0.0 copy-start.3
  41.7 0.0 copy-start.8
  41.7 0.0 copy-start.9
  41.7 2.5 %fusion.35.block_ref = f32[640,640]{1,0:T(8,128)S(1)} fusion(f32[640,640]{1,0:T(8,128)S(1)} %broadcast_multiply_fusion.1.first_ref, f32[640,640]{1,0:T(8,128)S(1)} %broadcast_multiply_fusion.second_ref), kind=kOutput, calls=%fused_computation.75 | convolution fusion | flops 1572864000 | bytes 4915200 | tf_op jit(solution)/shard_map/dot_general | solution.py:189
  44.2 0.0 copy-done.3
  44.2 0.0 copy-start.1
  44.2 0.0 copy-done.8
  44.2 0.0 copy-done.9
  44.3 4.0 %fusion.5.before_ref = f32[640,640]{1,0:T(8,128)S(1)} fusion(f32[640,640]{0,1:T(8,128)S(1)} %copy-done.9, f32[]{:T(128)S(6)} %div.36, f32[]{:T(128)S(6)} %div.34, f32[640,640]{1,0:T(8,128)S(1)} %copy-done.8, f32[640]{0:T(1024)S(1)} %get-tuple-element.5, f32[640]{0:T(1024)S(1)} %get-tuple-element.6, f32[]{:T(128)} %bitcast.10, ...), kind=kOutput, calls=%fused_computation.10 | convolution fusion | flops 1577369600 | bytes 4925452 | tf_op jit(solution)/shard_map/dot_general | solution.py:189
  48.2 0.0 copy-done.1
  48.2 0.0 copy-start.4
  48.2 3.6 %fusion.36.combined_ref = f32[640,640]{1,0:T(8,128)} fusion(f32[640,640]{1,0:T(8,128)S(1)} %fusion.5.before_ref, f32[640,640]{1,0:T(8,128)S(1)} %fusion.35.block_ref), kind=kOutput, calls=%fused_computation.76 | convolution fusion | flops 1572864000 | bytes 4915200 | tf_op jit(solution)/shard_map/dot_general | solution.py:189
  51.8 0.0 copy-done.4
  51.8 0.6 broadcast_in_dim.14.start_ref
  52.4 134.1 %shard_map.73 = f32[8,640]{1,0:T(8,128)} custom-call(f32[640,640]{1,0:T(8,128)} %copy-done.4, f32[640,640]{1,0:T(8,128)} %copy-done.1, f32[640,640]{1,0:T(8,128)} %fusion.36.combined_ref, f32[640,640]{1,0:T(8,128)} %copy-done.3, f32[640,640]{1,0:T(8,128)} %copy-done.2, f32[8,640]{1,0:T(8,128)} %broadcast_in_dim.14.start_ref), custom_call_target="tpu_custom_call" | custom-call | tf_op jit(solution)/shard_map/pallas_call | solution.py:171
  186.5 0.7 slice.90
  187.2 0.6 dynamic-slice_multiply_fusion
  (11 shorter events, 0.1 us)
Async XLA Ops:
  0.0 10.8 %copy-start = (f32[64,32]{0,1:T(8,128)S(1)}, f32[64,32]{0,1:T(8,128)}, u32[]{:S(2)}) copy-start(f32[64,32]{0,1:T(8,128)} %param.11) | copy-start | bytes 24580
  0.0 12.0 %copy-start.5 = (f32[2,64,640]{2,1,0:T(8,128)S(1)}, f32[2,64,640]{2,1,0:T(8,128)}, u32[]{:S(2)}) copy-start(f32[2,64,640]{2,1,0:T(8,128)} %param.7) | copy-start | bytes 983044
  0.0 12.0 %copy-start.7 = (f32[32]{0:T(128)S(1)}, f32[32]{0:T(128)}, u32[]{:S(2)}) copy-start(f32[32]{0:T(128)} %param.12) | copy-start | bytes 388
  0.0 12.2 %copy-start.6 = (f32[640]{0:T(1024)S(1)}, f32[640]{0:T(1024)}, u32[]{:S(2)}) copy-start(f32[640]{0:T(1024)} %param.13) | copy-start | bytes 7684
  3.4 19.7 %collective-permute-start = (f32[2,66,640]{2,1,0:T(8,128)S(1)}, f32[2,66,640]{2,1,0:T(8,128)S(1)}, u32[]{:S(2)}, u32[]{:S(2)}) collective-permute-start(f32[2,66,640]{2,1,0:T(8,128)S(1)} %pad_maximum_fusion), channel_id=1, source_target_pairs={{0,8},{8,16},{16,24},{24,32},{32,40},{40,48},{48,56},{56,64},{64,7... | collective-permute-start | bytes 1013768 | tf_op jit(solution)/shard_map/ppermute | solution.py:16
  5.6 17.5 %collective-permute-start.1 = (f32[64,640]{1,0:T(8,128)S(1)}, f32[64,640]{1,0:T(8,128)S(1)}, u32[]{:S(2)}, u32[]{:S(2)}) collective-permute-start(f32[64,640]{1,0:T(8,128)S(1)} %slice_bitcast_fusion.2), channel_id=1, source_target_pairs={{0,16},{8,24},{16,32},{24,40},{32,48},{40,56},{48,64},{56,72},{64,... | collective-permute-start | bytes 491528 | tf_op jit(solution)/shard_map/ppermute | solution.py:16
  19.7 21.9 %copy-start.2 = (f32[640,640]{1,0:T(8,128)}, f32[640,640]{1,0:T(8,128)S(1)}, u32[]{:S(2)}) copy-start(f32[640,640]{1,0:T(8,128)S(1)} %broadcast_multiply_fusion.second_ref) | copy-start | bytes 4915204
  41.7 2.5 %copy-start.3 = (f32[640,640]{1,0:T(8,128)}, f32[640,640]{1,0:T(8,128)S(1)}, u32[]{:S(2)}) copy-start(f32[640,640]{1,0:T(8,128)S(1)} %broadcast_multiply_fusion.1.first_ref) | copy-start | bytes 4915204
  41.7 2.5 %copy-start.8 = (f32[640,640]{1,0:T(8,128)S(1)}, f32[640,640]{1,0:T(8,128)}, u32[]{:S(2)}) copy-start(f32[640,640]{1,0:T(8,128)} %get-tuple-element.24) | copy-start | bytes 4915204
  41.7 2.5 %copy-start.9 = (f32[640,640]{0,1:T(8,128)S(1)}, f32[640,640]{0,1:T(8,128)}, u32[]{:S(2)}) copy-start(f32[640,640]{0,1:T(8,128)} %get-tuple-element.26) | copy-start | bytes 4915204
  44.2 4.0 %copy-start.1 = (f32[640,640]{1,0:T(8,128)}, f32[640,640]{1,0:T(8,128)S(1)}, u32[]{:S(2)}) copy-start(f32[640,640]{1,0:T(8,128)S(1)} %fusion.35.block_ref) | copy-start | bytes 4915204
  48.2 3.6 %copy-start.4 = (f32[640,640]{1,0:T(8,128)}, f32[640,640]{1,0:T(8,128)S(1)}, u32[]{:S(2)}) copy-start(f32[640,640]{1,0:T(8,128)S(1)} %fusion.5.before_ref) | copy-start | bytes 4915204

commit v4 on v2

v4 whole, which is shorter than its diff:
```python
import functools

import jax
import jax.numpy as jnp
from jax import lax
from jax.experimental import pallas as pl
from jax.experimental.pallas import tpu as pltpu
from jax.sharding import PartitionSpec as P

MESH = pl.DeviceIdType.MESH
STRIDE = 3


def shifted(block, axis, distance):
    devices = range(lax.axis_size(axis))
    route = [(i - distance, i) for i in devices if i - distance in devices]
    return lax.ppermute(block, axis, route)


def transition(previous, current, parent_ids, observed, mixing, fingerprints, tracer_scale):
    count = current.shape[1]
    highest = lax.Precision.HIGHEST
    inner_prod = lax.dot_general(
        previous,
        current,
        (((0,), (0,)), ((), ())),
        precision=highest,
        preferred_element_type=jnp.float32,
    )
    distance = (
        jnp.sum(previous * previous, axis=0)[:, None]
        + jnp.sum(current * current, axis=0)[None, :]
        - 2.0 * inner_prod
    )
    kernel = jnp.exp(-2.0 * distance / current.shape[0])
    predicted = lax.dot_general(
        fingerprints,
        current,
        (((0,), (0,)), ((), ())),
        precision=highest,
        preferred_element_type=jnp.float32,
    )
    misfit = tracer_scale[:, None] * (observed[:, None] - predicted)
    likelihood = jnp.exp(-0.5 * jnp.sum(misfit * misfit, axis=0))
    likelihood = likelihood / jnp.max(likelihood)
    parent = (parent_ids[None, :] == jnp.arange(count, dtype=jnp.int32)[:, None]).astype(
        jnp.float32
    )
    return likelihood[None, :] * (parent + mixing * kernel)


def vec_mat(u_row, mat):
    n = mat.shape[0]
    u_col = jnp.transpose(jnp.broadcast_to(u_row[0:1, :], (128, n)))
    parts = []
    for g in range(n // 128):
        block = mat[:, g * 128:(g + 1) * 128]
        parts.append(jnp.sum(block * u_col, axis=0, keepdims=True))
    return jnp.concatenate(parts, axis=1)


def normalized(v):
    return v / jnp.sum(v)


def spread(v, like):
    return jnp.broadcast_to(v, like.shape)


def chain_kernel(
    steps, stride, before_ref, block_ref, combined_ref, first_ref, second_ref, start_ref,
    out_ref, recv_buf, send_buf, send_sem, recv_sem,
):
    me = lax.axis_index("tm")
    row = lax.axis_index("rows")
    last = steps - 1
    phase = me % stride
    node = phase == 0

    barrier = pltpu.get_barrier_semaphore()

    def greet(other):
        pl.semaphore_signal(barrier, 1, device_id=(other, row), device_id_type=MESH)

    @pl.when(node)
    def _():
        for d in range(1, stride + 1):
            @pl.when(me + d <= last)
            def _():
                greet(me + d)

        @pl.when(me >= stride)
        def _():
            greet(me - stride)

    @pl.when(jnp.logical_not(node))
    def _():
        greet(me - phase)

    partners = jnp.where(
        node,
        jnp.minimum(last - me, stride) + (me >= stride).astype(jnp.int32),
        1,
    )
    for amount in range(1, stride + 2):
        @pl.when(partners == amount)
        def _():
            pl.semaphore_wait(barrier, amount)

    def copy_to(d):
        return pltpu.make_async_remote_copy(
            src_ref=send_buf,
            dst_ref=recv_buf,
            send_sem=send_sem.at[d - 1],
            recv_sem=recv_sem,
            device_id=(jnp.minimum(me + d, last), row),
            device_id_type=MESH,
        )

    copies = [copy_to(d) for d in range(1, stride + 1)]

    def send_all(v):
        send_buf[...] = spread(v, send_buf)
        for d in range(1, stride + 1):
            @pl.when(me + d <= last)
            def _():
                copies[d - 1].start()

    @pl.when(me == 0)
    def _():
        out_ref[...] = start_ref[...]
        send_all(normalized(vec_mat(start_ref[...], block_ref[...])))

    @pl.when(me > 0)
    def _():
        copies[0].wait_recv()
        out_ref[...] = recv_buf[...]

    @pl.when(jnp.logical_and(node, me > 0))
    def _():
        send_all(normalized(vec_mat(out_ref[...], combined_ref[...])))

    lag = jnp.where(node, jnp.where(me > 0, stride - 1, 0), phase - 1)
    for amount in range(1, stride):
        @pl.when(lag == amount)
        def _():
            u = out_ref[...]
            for d in range(amount, 0, -1):
                u = spread(normalized(vec_mat(u, before_ref[d - 1])), out_ref)
            out_ref[...] = u

    incoming = out_ref[...]
    w_first = normalized(vec_mat(incoming, first_ref[...]))
    w_second = normalized(vec_mat(spread(w_first, incoming), second_ref[...]))
    out_ref[...] = jnp.concatenate(
        [w_first, w_second, jnp.zeros((incoming.shape[0] - 2, incoming.shape[1]), jnp.float32)],
        axis=0,
    )

    @pl.when(node)
    def _():
        for d in range(1, stride + 1):
            @pl.when(me + d <= last)
            def _():
                copies[d - 1].wait_send()


def chain(befores, block, combined, first, second, start, steps, stride):
    count = block.shape[0]
    return pl.pallas_call(
        functools.partial(chain_kernel, steps, stride),
        out_shape=jax.ShapeDtypeStruct((8, count), jnp.float32),
        in_specs=[pl.BlockSpec(memory_space=pltpu.VMEM)] * 6,
        out_specs=pl.BlockSpec(memory_space=pltpu.VMEM),
        scratch_shapes=[
            pltpu.VMEM((8, count), jnp.float32),
            pltpu.VMEM((8, count), jnp.float32),
            pltpu.SemaphoreType.DMA((stride,)),
            pltpu.SemaphoreType.DMA,
        ],
        compiler_params=pltpu.CompilerParams(
            collective_id=0, has_side_effects=True, vmem_limit_bytes=48 * 1024 * 1024
        ),
    )(befores, block, combined, first, second, start)


def block_product(matrices):
    block = matrices[0]
    for matrix in matrices[1:]:
        block = jnp.dot(
            block, matrix, precision=lax.Precision.HIGH, preferred_element_type=jnp.float32
        )
    return block


def shards(states, ancestors, tracer_obs, jitter, fingerprints, tracer_scale, prior_weights):
    count = states.shape[2]
    own_rows = count // lax.axis_size("rows")
    row_start = lax.axis_index("rows") * own_rows
    steps = lax.axis_size("tm")
    stride = STRIDE
    local = states.shape[0]
    dims = states.shape[1]
    tracers = tracer_obs.shape[1]

    count_pad = jnp.zeros((local, count - tracers - 1), jnp.float32)
    extra = jnp.concatenate(
        [
            ancestors.astype(jnp.float32)[:, None, :],
            jnp.concatenate([tracer_obs, jitter[:, None], count_pad], axis=1)[:, None, :],
        ],
        axis=1,
    )
    packed = jnp.concatenate([states, extra], axis=1)
    packs = [packed] + [shifted(packed, "tm", d) for d in range(1, stride)]
    rims = [pack[-1, :dims, :] for pack in packs[1:]] + [shifted(states[-1], "tm", stride)]

    def matrices_of(rim, pack):
        block_states = pack[:, :dims, :]
        parents = pack[:, dims, :].astype(jnp.int32)
        observed = pack[:, dims + 1, :tracers]
        mixing = pack[:, dims + 1, tracers]
        previous = jnp.concatenate([rim[None], block_states[:-1]], axis=0)
        return [
            transition(
                previous[s], block_states[s], parents[s], observed[s], mixing[s],
                fingerprints, tracer_scale,
            )
            for s in range(local)
        ]

    own = matrices_of(rims[0], packs[0])
    blocks = [block_product(own)] + [
        block_product(matrices_of(rims[d], packs[d])) for d in range(1, stride)
    ]
    combined = block_product(blocks[::-1])
    befores = jnp.stack(blocks[1:], axis=0)

    start = prior_weights / jnp.sum(prior_weights)
    start8 = jnp.broadcast_to(start[None, :], (8, count))
    weights = chain(befores, blocks[0], combined, own[0], own[1], start8, steps, stride)
    mine = lax.dynamic_slice_in_dim(weights[:local], row_start, own_rows, 1)
    return count * mine


def solution(mesh):
    return jax.shard_map(
        shards,
        mesh=mesh,
        in_specs=(P("tm", None, None), P("tm", None), P("tm", None), P("tm"), P(), P(), P()),
        out_specs=P("tm", "rows"),
        check_vma=False,
    )
```

time: 213 us -> 183 us (0.86)
  Pallas kernels: 155 us -> 103 us
  waiting for transfers between devices: 0.01 us -> 25.8 us
  other arithmetic: 7.58 us -> 14.6 us
  matrix products: 34.3 us -> 30.5 us
  starting transfers between devices: 6.58 us -> 3.88 us
  between operations: 2.79 us -> 0.35 us
    pallas_call x1, Pallas kernels: 155 us -> 103 us  [chain(): pl.pallas_call(functools.partial(chain_kernel, steps, stride), out_shape=...]
    ppermute x5 -> x3, waiting for transfers between devices: 0.01 us -> 25.8 us  [shifted(): return lax.ppermute(block, axis, route)]
    dot_general x4 -> x6, matrix products: 17.3 us -> 11.5 us  [transition(): lax.dot_general(previous, current, (((0,), (0,)), ((), ())), precision=hi...]
    reduce_max x0 -> x6, other arithmetic: none -> 3.71 us  [transition(): likelihood = likelihood / jnp.max(likelihood)]
    div x0 -> x4, other arithmetic: none -> 3.61 us  [transition(): likelihood = likelihood / jnp.max(likelihood)]
    mul x2 -> x0, other arithmetic: 3.08 us -> none  [transition(): return weight * (count / jnp.sum(weight))]
    ppermute x5 -> x3, starting transfers between devices: 6.58 us -> 3.88 us  [shifted(): return lax.ppermute(block, axis, route)]
    dot_general x2 -> x5, matrix products: 14.3 us -> 16.7 us  [block_product(): jnp.dot(block, matrix, precision=lax.Precision.HIGH, preferred_element_ty...]
  transfers between devices with their start and end apart: 5 -> 3, of which waited for: 0 -> 1; matrix products, arithmetic and copies ran while one was open for 8% -> 6% of each run, Pallas kernels for 0% -> 0%
where the time goes in v4:
time: 183 us; the launch traced here: 182 us
  Pallas kernels  103 us (56%)
  matrix products  30.5 us (17%)
  waiting for transfers between devices  25.8 us (14%)
  other arithmetic  14.6 us (8%)
  starting transfers between devices  3.88 us (2%)
  local copies, waits for them, and re-layouts  3.75 us (2%)
    pallas_call x1, Pallas kernels, chain(): pl.pallas_call(functools.partial(chain_kernel, steps, stride), out_shape=...  103 us
    ppermute x3, waiting for transfers between devices, shifted(): return lax.ppermute(block, axis, route)  25.8 us
    dot_general x5, matrix products, block_product(): jnp.dot(block, matrix, precision=lax.Precision.HIGH, preferred_element_ty...  16.7 us
    dot_general x6, matrix products, transition(): lax.dot_general(previous, current, (((0,), (0,)), ((), ())), precision=hi...  11.5 us
    ppermute x3, starting transfers between devices, shifted(): return lax.ppermute(block, axis, route)  3.88 us
    reduce_max x6, other arithmetic, transition(): likelihood = likelihood / jnp.max(likelihood)  3.71 us
  transfers between devices with their start and end apart: 3, of which 1 were waited for; matrix products, arithmetic and copies ran while one was open for 6% of the time, Pallas kernels for 0%

profile of v4, /device:TPU:504, one launch (start us, length us, event | category | flops | bytes accessed | tf_op | source)
XLA Modules:
  0.0 182.4 jit_solution(8628501804273437290)
XLA Ops:
  0.0 0.0 copy-start
  0.0 0.0 copy-start.2
  0.0 0.0 copy-start.4
  0.0 0.0 copy-start.3
  0.0 0.8 copy.11
  0.8 0.1 pad.7.clone
  0.9 0.8 maximum_bitcast_fusion
  1.7 0.7 convert_convert_fusion
  2.4 1.0 pad_maximum_fusion.1
  3.4 1.3 collective-permute-start.1
  4.7 1.3 collective-permute-start
  6.0 0.9 slice_bitcast_fusion.4
  6.9 1.3 collective-permute-start.2
  8.2 0.7 fusion.102
  8.9 1.0 multiply_reduce_fusion
  9.9 0.0 copy-done
  9.9 1.2 fusion.42
  11.1 0.6 fusion.93
  11.7 0.6 fusion.92
  12.3 0.0 copy-done.2
  12.3 0.0 copy-done.4
  12.3 0.2 fusion.43
  12.5 0.6 fusion.95
  13.1 0.6 fusion.94
  13.7 0.0 copy-done.3
  13.7 0.6 reduce_sum.159
  14.3 2.6 %add_multiply_fusion.second_ref = f32[640,640]{1,0:T(8,128)S(1)} fusion(f32[640]{0:T(1024)S(1)} %get-tuple-element.9, f32[640]{0:T(1024)S(1)} %get-tuple-element.10, f32[]{:T(128)} %bitcast.23, s32[640]{0:T(1024)S(1)} %get-tuple-element.11, f32[640]{0:T(1024)S(1)} %fusion.94, f32[2,64,640]{2,1,0:T(8,128)S(1)} %copy-done.2), kind=kOutput, calls=%fused_computation.8 | convolution fusion | flops 318259200 | bytes 1976324 | tf_op jit(solution)/shard_map/dot_general | solution.py:23
  17.0 0.0 copy-start.1
  17.0 0.6 broadcast_divide_fusion
  17.5 25.8 %collective-permute-done.2 = f32[64,640]{1,0:T(8,128)S(1)} collective-permute-done((f32[64,640]{1,0:T(8,128)S(1)}, f32[64,640]{1,0:T(8,128)S(1)}, u32[]{:S(2)}, u32[]{:S(2)}) %collective-permute-start.2) | collective-permute-done | bytes 163872 | tf_op jit(solution)/shard_map/ppermute | solution.py:17
  43.4 0.0 collective-permute-done.1
  43.4 0.2 fusion.77
  43.6 0.0 collective-permute-done
  43.6 0.2 fusion.78
  43.9 0.2 fusion.80
  44.1 0.2 multiply_reduce_fusion.9
  44.3 0.6 fusion.85
  45.0 0.7 fusion.87
  45.7 0.6 fusion.89
  46.3 0.6 fusion.91
  46.9 1.3 fusion.84
  48.2 1.2 fusion.88
  49.4 1.5 fusion.74
  51.0 0.6 fusion.100
  51.6 1.5 fusion.73
  53.1 4.6 %fusion.19 = f32[640,640]{1,0:T(8,128)S(1)} fusion(f32[640,640]{1,0:T(8,128)S(1)} %fusion.73, f32[640,640]{1,0:T(8,128)S(1)} %fusion.74, f32[640]{0:T(1024)S(1)} %get-tuple-element.6, f32[640]{0:T(1024)S(1)} %get-tuple-element.5, f32[]{:T(128)} %bitcast.9, s32[640]{0:T(1024)S(1)} %get-tuple-element.14, f32[640]{0:T(1024)S(1)} %get-tuple-element.36, ...), kind=kOutput, calls=%fused_computation.26 | convolution fusion | flops 1580236800 | bytes 4933128 | tf_op jit(solution)/shard_map/dot_general | solution.py:190
  57.7 1.5 fusion.79
  59.2 0.6 fusion.101
  59.8 1.7 fusion.76
  61.5 4.8 %fusion.5 = f32[640,640]{1,0:T(8,128)S(1)} fusion(f32[640,640]{1,0:T(8,128)S(1)} %fusion.76, f32[640,640]{1,0:T(8,128)S(1)} %fusion.79, f32[640]{0:T(1024)S(1)} %get-tuple-element.8, f32[640]{0:T(1024)S(1)} %get-tuple-element.7, f32[]{:T(128)} %bitcast.17, s32[640]{0:T(1024)S(1)} %get-tuple-element.16, f32[640]{0:T(1024)S(1)} %get-tuple-element.38, ...), kind=kOutput, calls=%fused_computation.7 | convolution fusion | flops 1580236800 | bytes 4933128 | tf_op jit(solution)/shard_map/dot_general | solution.py:190
  66.3 2.4 %fusion.104 = f32[640,640]{1,0:T(8,128)S(1)} fusion(f32[640,640]{1,0:T(8,128)S(1)} %fusion.5, f32[640,640]{1,0:T(8,128)S(1)} %fusion.19), kind=kOutput, calls=%fused_computation.157 | convolution fusion | flops 1572864000 | bytes 4915200 | tf_op jit(solution)/shard_map/dot_general | solution.py:190
  68.7 2.7 %add_multiply_fusion.1.first_ref = f32[640,640]{1,0:T(8,128)S(1)} fusion(f32[640]{0:T(1024)S(1)} %get-tuple-element.10, f32[640]{0:T(1024)S(1)} %get-tuple-element.6, f32[]{:T(128)} %bitcast.21, s32[640]{0:T(1024)S(1)} %get-tuple-element.12, f32[640]{0:T(1024)S(1)} %fusion.92, f32[2,66,640]{2,1,0:T(8,128)S(1)} %collective-permute-done, ...), kind=kOutput, calls=%fused_computation.10 | convolution fusion | flops 318259200 | bytes 1982468 | tf_op jit(solution)/shard_map/dot_general | solution.py:23
  71.4 0.0 copy-done.1
  71.4 2.5 %fusion.103.block_ref = f32[640,640]{1,0:T(8,128)S(1)} fusion(f32[640,640]{1,0:T(8,128)S(1)} %add_multiply_fusion.1.first_ref, f32[640,640]{1,0:T(8,128)S(1)} %add_multiply_fusion.second_ref), kind=kOutput, calls=%fused_computation.156 | convolution fusion | flops 1572864000 | bytes 4915200 | tf_op jit(solution)/shard_map/dot_general | solution.py:190
  73.9 2.4 %fusion.105.combined_ref = f32[640,640]{1,0:T(8,128)S(1)} fusion(f32[640,640]{1,0:T(8,128)S(1)} %fusion.104, f32[640,640]{1,0:T(8,128)S(1)} %fusion.103.block_ref), kind=kOutput, calls=%fused_computation.158 | convolution fusion | flops 1572864000 | bytes 4915200 | tf_op jit(solution)/shard_map/dot_general | solution.py:190
  76.3 1.9 %pad_maximum_fusion.before_ref = f32[2,640,640]{2,1,0:T(8,128)} fusion(f32[1,640,640]{2,1,0:T(8,128)S(1)} %bitcast.98, f32[1,640,640]{2,1,0:T(8,128)S(1)} %bitcast.97), kind=kLoop, calls=%fused_computation | loop fusion | flops 819200 | bytes 6553600 | tf_op jit(solution)/shard_map/stack | solution.py:237
  78.2 103.5 %shard_map.73 = f32[8,640]{1,0:T(8,128)S(1)} custom-call(f32[2,640,640]{2,1,0:T(8,128)} %pad_maximum_fusion.before_ref, f32[640,640]{1,0:T(8,128)S(1)} %fusion.103.block_ref, f32[640,640]{1,0:T(8,128)S(1)} %fusion.105.combined_ref, f32[640,640]{1,0:T(8,128)S(1)} %add_multiply_fusion.1.first_ref, f32[640,640]{1,0:T(8,128)} %copy-done.1, ...), custom_call_target="tpu_custom_call" | custom-call | tf_op jit(solution)/shard_map/pallas_call | solution.py:170
  181.7 0.6 dynamic-slice_multiply_fusion
  (16 shorter events, 0.2 us)
Async XLA Ops:
  0.0 9.9 %copy-start = (f32[64,32]{0,1:T(8,128)S(1)}, f32[64,32]{0,1:T(8,128)}, u32[]{:S(2)}) copy-start(f32[64,32]{0,1:T(8,128)} %param.11) | copy-start | bytes 24580
  0.0 12.3 %copy-start.2 = (f32[2,64,640]{2,1,0:T(8,128)S(1)}, f32[2,64,640]{2,1,0:T(8,128)}, u32[]{:S(2)}) copy-start(f32[2,64,640]{2,1,0:T(8,128)} %param.7) | copy-start | bytes 983044
  0.0 12.3 %copy-start.4 = (f32[32]{0:T(128)S(1)}, f32[32]{0:T(128)}, u32[]{:S(2)}) copy-start(f32[32]{0:T(128)} %param.12) | copy-start | bytes 388
  0.0 13.7 %copy-start.3 = (f32[640]{0:T(1024)S(1)}, f32[640]{0:T(1024)}, u32[]{:S(2)}) copy-start(f32[640]{0:T(1024)} %param.13) | copy-start | bytes 7684
  3.4 40.0 %collective-permute-start.1 = (f32[2,66,640]{2,1,0:T(8,128)S(1)}, f32[2,66,640]{2,1,0:T(8,128)S(1)}, u32[]{:S(2)}, u32[]{:S(2)}) collective-permute-start(f32[2,66,640]{2,1,0:T(8,128)S(1)} %pad_maximum_fusion.1), channel_id=1, source_target_pairs={{0,16},{8,24},{16,32},{24,40},{32,48},{40,56},{48,64},{56,72},{64,... | collective-permute-start | bytes 1013768 | tf_op jit(solution)/shard_map/ppermute | solution.py:17
  4.7 39.0 %collective-permute-start = (f32[2,66,640]{2,1,0:T(8,128)S(1)}, f32[2,66,640]{2,1,0:T(8,128)S(1)}, u32[]{:S(2)}, u32[]{:S(2)}) collective-permute-start(f32[2,66,640]{2,1,0:T(8,128)S(1)} %pad_maximum_fusion.1), channel_id=1, source_target_pairs={{0,8},{8,16},{16,24},{24,32},{32,40},{40,48},{48,56},{56,64},{64,7... | collective-permute-start | bytes 1013768 | tf_op jit(solution)/shard_map/ppermute | solution.py:17
  6.9 36.5 %collective-permute-start.2 = (f32[64,640]{1,0:T(8,128)S(1)}, f32[64,640]{1,0:T(8,128)S(1)}, u32[]{:S(2)}, u32[]{:S(2)}) collective-permute-start(f32[64,640]{1,0:T(8,128)S(1)} %slice_bitcast_fusion.4), channel_id=1, source_target_pairs={{0,24},{8,32},{16,40},{24,48},{32,56},{40,64},{48,72},{56,80},{64,... | collective-permute-start | bytes 491528 | tf_op jit(solution)/shard_map/ppermute | solution.py:17
  17.0 54.5 %copy-start.1 = (f32[640,640]{1,0:T(8,128)}, f32[640,640]{1,0:T(8,128)S(1)}, u32[]{:S(2)}) copy-start(f32[640,640]{1,0:T(8,128)S(1)} %add_multiply_fusion.second_ref) | copy-start | bytes 4915204

commit v5 on v4

--- a/solution.py
+++ b/solution.py
@@ -68,14 +68,26 @@
 
 
 def chain_kernel(
-    steps, stride, before_ref, block_ref, combined_ref, first_ref, second_ref, start_ref,
-    out_ref, recv_buf, send_buf, send_sem, recv_sem,
+    steps, stride, *refs,
 ):
+    n_in = stride + 4
+    hbm = refs[:n_in - 1]
+    start_ref = refs[n_in - 1]
+    out_ref, recv_buf, send_buf, send_sem, recv_sem, load_sem = refs[n_in:n_in + 6]
+    local = refs[n_in + 6:]
     me = lax.axis_index("tm")
     row = lax.axis_index("rows")
     last = steps - 1
     phase = me % stride
     node = phase == 0
+
+    loads = [
+        pltpu.make_async_copy(hbm[i], local[i], load_sem.at[i]) for i in range(len(hbm))
+    ]
+    for load in loads:
+        load.start()
+    block_ref, combined_ref, first_ref, second_ref = local[:4]
+    befores = local[4:]
 
     barrier = pltpu.get_barrier_semaphore()
 
@@ -120,12 +132,15 @@
     copies = [copy_to(d) for d in range(1, stride + 1)]
 
     def send_all(v):
-        send_buf[...] = spread(v, send_buf)
+        send_buf[...] = v
         for d in range(1, stride + 1):
             @pl.when(me + d <= last)
             def _():
                 copies[d - 1].start()
 
+    loads[0].wait()
+    loads[1].wait()
+
     @pl.when(me == 0)
     def _():
         out_ref[...] = start_ref[...]
@@ -134,21 +149,25 @@
     @pl.when(me > 0)
     def _():
         copies[0].wait_recv()
-        out_ref[...] = recv_buf[...]
+        out_ref[...] = spread(recv_buf[...], out_ref)
 
     @pl.when(jnp.logical_and(node, me > 0))
     def _():
         send_all(normalized(vec_mat(out_ref[...], combined_ref[...])))
 
+    for load in loads[4:]:
+        load.wait()
     lag = jnp.where(node, jnp.where(me > 0, stride - 1, 0), phase - 1)
     for amount in range(1, stride):
         @pl.when(lag == amount)
         def _():
             u = out_ref[...]
             for d in range(amount, 0, -1):
-                u = spread(normalized(vec_mat(u, before_ref[d - 1])), out_ref)
+                u = spread(normalized(vec_mat(u, befores[d - 1][...])), out_ref)
             out_ref[...] = u
 
+    loads[2].wait()
+    loads[3].wait()
     incoming = out_ref[...]
     w_first = normalized(vec_mat(incoming, first_ref[...]))
     w_second = normalized(vec_mat(spread(w_first, incoming), second_ref[...]))
@@ -165,23 +184,27 @@
                 copies[d - 1].wait_send()
 
 
-def chain(befores, block, combined, first, second, start, steps, stride):
+def chain(block, combined, first, second, befores, start, steps, stride):
     count = block.shape[0]
+    matrices = [block, combined, first, second] + list(befores)
     return pl.pallas_call(
         functools.partial(chain_kernel, steps, stride),
         out_shape=jax.ShapeDtypeStruct((8, count), jnp.float32),
-        in_specs=[pl.BlockSpec(memory_space=pltpu.VMEM)] * 6,
+        in_specs=[pl.BlockSpec(memory_space=pl.ANY)] * len(matrices)
+        + [pl.BlockSpec(memory_space=pltpu.VMEM)],
         out_specs=pl.BlockSpec(memory_space=pltpu.VMEM),
         scratch_shapes=[
-            pltpu.VMEM((8, count), jnp.float32),
-            pltpu.VMEM((8, count), jnp.float32),
+            pltpu.VMEM((1, count), jnp.float32),
+            pltpu.VMEM((1, count), jnp.float32),
             pltpu.SemaphoreType.DMA((stride,)),
             pltpu.SemaphoreType.DMA,
-        ],
+            pltpu.SemaphoreType.DMA((len(matrices),)),
+        ]
+        + [pltpu.VMEM((count, count), jnp.float32) for _ in matrices],
         compiler_params=pltpu.CompilerParams(
             collective_id=0, has_side_effects=True, vmem_limit_bytes=48 * 1024 * 1024
         ),
-    )(befores, block, combined, first, second, start)
+    )(*matrices, start)
 
 
 def block_product(matrices):
@@ -234,11 +257,10 @@
         block_product(matrices_of(rims[d], packs[d])) for d in range(1, stride)
     ]
     combined = block_product(blocks[::-1])
-    befores = jnp.stack(blocks[1:], axis=0)
 
     start = prior_weights / jnp.sum(prior_weights)
     start8 = jnp.broadcast_to(start[None, :], (8, count))
-    weights = chain(befores, blocks[0], combined, own[0], own[1], start8, steps, stride)
+    weights = chain(blocks[0], combined, own[0], own[1], blocks[1:], start8, steps, stride)
     mine = lax.dynamic_slice_in_dim(weights[:local], row_start, own_rows, 1)
     return count * mine
 

time: 183 us -> 168 us (0.918)
  Pallas kernels: 103 us -> 90.3 us
    pallas_call x1, Pallas kernels: 103 us -> 90.3 us  [chain(): pl.pallas_call(functools.partial(chain_kernel, steps, stride), out_shape=...]
    another operation x1 -> x0, other arithmetic: 1.9 us -> none  [shards(): befores = jnp.stack(blocks[1:], axis=0)]
where the time goes in v5:
time: 168 us; the launch traced here: 167 us
  Pallas kernels  90.3 us (54%)
  matrix products  30.4 us (18%)
  waiting for transfers between devices  25.5 us (15%)
  other arithmetic  13.1 us (8%)
  starting transfers between devices  3.88 us (2%)
  local copies, waits for them, and re-layouts  3.68 us (2%)
    pallas_call x1, Pallas kernels, chain(): pl.pallas_call(functools.partial(chain_kernel, steps, stride), out_shape=...  90.3 us
    ppermute x3, waiting for transfers between devices, shifted(): return lax.ppermute(block, axis, route)  25.5 us
    dot_general x5, matrix products, block_product(): jnp.dot(block, matrix, precision=lax.Precision.HIGH, preferred_element_ty...  16.8 us
    dot_general x6, matrix products, transition(): lax.dot_general(previous, current, (((0,), (0,)), ((), ())), precision=hi...  11.3 us
    div x4, other arithmetic, transition(): likelihood = likelihood / jnp.max(likelihood)  3.9 us
    ppermute x3, starting transfers between devices, shifted(): return lax.ppermute(block, axis, route)  3.88 us
    reduce_max x6, other arithmetic, transition(): likelihood = likelihood / jnp.max(likelihood)  3.87 us
  transfers between devices with their start and end apart: 3, of which 1 were waited for; matrix products, arithmetic and copies ran while one was open for 6% of the time, Pallas kernels for 0%

profile of v5, /device:TPU:504, one launch (start us, length us, event | category | flops | bytes accessed | tf_op | source)
XLA Modules:
  0.0 167.3 jit_solution(7879494773825237035)
XLA Ops:
  0.0 0.0 copy-start
  0.0 0.0 copy-start.4
  0.0 0.0 copy-start.6
  0.0 0.0 copy-start.5
  0.0 0.8 copy.11
  0.8 0.1 pad.5.clone
  0.9 0.8 maximum_bitcast_fusion
  1.7 0.7 convert_convert_fusion
  2.4 1.0 pad_maximum_fusion
  3.4 1.3 collective-permute-start.1
  4.7 1.3 collective-permute-start
  6.0 0.9 slice_bitcast_fusion.4
  6.9 1.3 collective-permute-start.2
  8.2 0.6 fusion.102
  8.8 1.0 multiply_reduce_fusion.4
  9.8 0.0 copy-done
  9.8 1.1 fusion.42
  11.0 0.7 fusion.85
  11.7 0.7 fusion.84
  12.4 0.0 copy-done.4
  12.4 0.0 copy-done.6
  12.4 0.2 fusion.43
  12.7 0.7 fusion.87
  13.4 0.7 fusion.86
  14.1 0.0 copy-done.5
  14.1 0.6 reduce_sum.159
  14.6 2.6 %add_multiply_fusion.refs_3_ = f32[640,640]{1,0:T(8,128)S(1)} fusion(f32[640]{0:T(1024)S(1)} %get-tuple-element.9, f32[640]{0:T(1024)S(1)} %get-tuple-element.10, f32[]{:T(128)} %bitcast.9, s32[640]{0:T(1024)S(1)} %get-tuple-element.15, f32[640]{0:T(1024)S(1)} %fusion.86, f32[2,64,640]{2,1,0:T(8,128)S(1)} %copy-done.4), kind=kOutput, calls=%fused_computation.42 | convolution fusion | flops 318259200 | bytes 1976324 | tf_op jit(solution)/shard_map/dot_general | solution.py:23
  17.3 0.0 copy-start.1
  17.3 0.5 broadcast_divide_fusion
  17.8 25.5 %collective-permute-done.2 = f32[64,640]{1,0:T(8,128)S(1)} collective-permute-done((f32[64,640]{1,0:T(8,128)S(1)}, f32[64,640]{1,0:T(8,128)S(1)}, u32[]{:S(2)}, u32[]{:S(2)}) %collective-permute-start.2) | collective-permute-done | bytes 163872 | tf_op jit(solution)/shard_map/ppermute | solution.py:17
  43.4 0.0 collective-permute-done
  43.4 0.2 fusion.74
  43.6 0.0 collective-permute-done.1
  43.6 0.2 fusion.77
  43.9 0.2 fusion.79
  44.1 0.2 multiply_reduce_fusion.7
  44.3 0.7 fusion.93
  45.0 0.6 fusion.95
  45.7 0.6 fusion.89
  46.3 0.6 fusion.91
  46.9 1.3 fusion.92
  48.2 1.2 fusion.88
  49.4 1.5 fusion.78
  51.0 0.6 fusion.100
  51.6 1.5 fusion.73
  53.1 4.7 %fusion.7.refs_4_ = f32[640,640]{1,0:T(8,128)S(1)} fusion(f32[640,640]{1,0:T(8,128)S(1)} %fusion.73, f32[640,640]{1,0:T(8,128)S(1)} %fusion.78, f32[640]{0:T(1024)S(1)} %get-tuple-element.6, f32[640]{0:T(1024)S(1)} %get-tuple-element.5, f32[]{:T(128)} %bitcast.21, s32[640]{0:T(1024)S(1)} %get-tuple-element.12, f32[640]{0:T(1024)S(1)} %get-tuple-element.38, ...), kind=kOutput, calls=%fused_computation.7 | convolution fusion | flops 1580236800 | bytes 4933128 | tf_op jit(solution)/shard_map/dot_general | solution.py:213
  57.8 0.0 copy-start.2
  57.8 1.5 fusion.76
  59.3 0.6 fusion.101
  59.9 1.7 %fusion.75 = f32[640,640]{1,0:T(8,128)S(1)} fusion(f32[2,66,640]{2,1,0:T(8,128)S(1)} %collective-permute-done.1), kind=kOutput, calls=%fused_computation.98 | convolution fusion | flops 314572800 | bytes 1966080 | tf_op jit(solution)/shard_map/dot_general | solution.py:23
  61.6 4.8 %fusion.5.refs_5_ = f32[640,640]{1,0:T(8,128)S(1)} fusion(f32[640,640]{1,0:T(8,128)S(1)} %fusion.75, f32[640,640]{1,0:T(8,128)S(1)} %fusion.76, f32[640]{0:T(1024)S(1)} %get-tuple-element.8, f32[640]{0:T(1024)S(1)} %get-tuple-element.7, f32[]{:T(128)} %bitcast.16, s32[640]{0:T(1024)S(1)} %get-tuple-element.14, f32[640]{0:T(1024)S(1)} %get-tuple-element.36, ...), kind=kOutput, calls=%fused_computation.6 | convolution fusion | flops 1580236800 | bytes 4933128 | tf_op jit(solution)/shard_map/dot_general | solution.py:213
  66.4 0.0 copy-done.2
  66.4 0.0 copy-start.3
  66.4 2.4 %fusion.104 = f32[640,640]{1,0:T(8,128)S(1)} fusion(f32[640,640]{1,0:T(8,128)S(1)} %fusion.5.refs_5_, f32[640,640]{1,0:T(8,128)S(1)} %fusion.7.refs_4_), kind=kOutput, calls=%fused_computation.156 | convolution fusion | flops 1572864000 | bytes 4915200 | tf_op jit(solution)/shard_map/dot_general | solution.py:213
  68.8 0.0 copy-done.3
  68.8 2.5 %add_multiply_fusion.1.refs_2_ = f32[640,640]{1,0:T(8,128)S(1)} fusion(f32[640]{0:T(1024)S(1)} %get-tuple-element.10, f32[640]{0:T(1024)S(1)} %get-tuple-element.6, f32[]{:T(128)} %bitcast.4, s32[640]{0:T(1024)S(1)} %get-tuple-element.16, f32[640]{0:T(1024)S(1)} %fusion.84, f32[2,66,640]{2,1,0:T(8,128)S(1)} %collective-permute-done, ...), kind=kOutput, calls=%fused_computation.44 | convolution fusion | flops 318259200 | bytes 1982468 | tf_op jit(solution)/shard_map/dot_general | solution.py:23
  71.4 0.0 copy-done.1
  71.4 2.5 %fusion.103.refs_0_ = f32[640,640]{1,0:T(8,128)S(1)} fusion(f32[640,640]{1,0:T(8,128)S(1)} %add_multiply_fusion.1.refs_2_, f32[640,640]{1,0:T(8,128)S(1)} %add_multiply_fusion.refs_3_), kind=kOutput, calls=%fused_computation.155 | convolution fusion | flops 1572864000 | bytes 4915200 | tf_op jit(solution)/shard_map/dot_general | solution.py:213
  73.8 2.4 %fusion.105.refs_1_ = f32[640,640]{1,0:T(8,128)S(1)} fusion(f32[640,640]{1,0:T(8,128)S(1)} %fusion.104, f32[640,640]{1,0:T(8,128)S(1)} %fusion.103.refs_0_), kind=kOutput, calls=%fused_computation.157 | convolution fusion | flops 1572864000 | bytes 4915200 | tf_op jit(solution)/shard_map/dot_general | solution.py:213
  76.3 90.3 %shard_map.73 = f32[8,640]{1,0:T(8,128)S(1)} custom-call(f32[640,640]{1,0:T(8,128)S(1)} %fusion.103.refs_0_, f32[640,640]{1,0:T(8,128)S(1)} %fusion.105.refs_1_, f32[640,640]{1,0:T(8,128)S(1)} %add_multiply_fusion.1.refs_2_, f32[640,640]{1,0:T(8,128)} %copy-done.1, f32[640,640]{1,0:T(8,128)} %copy-done.2, f32[640,640]{1,0:T(8,128)} %copy-done.3, ...), custom_call_target="tpu_custom_call" | custom-call | tf_op jit(solution)/shard_map/pallas_call | solution.py:190
  166.6 0.6 dynamic-slice_multiply_fusion
  (16 shorter events, 0.2 us)
Async XLA Ops:
  0.0 9.8 %copy-start = (f32[64,32]{0,1:T(8,128)S(1)}, f32[64,32]{0,1:T(8,128)}, u32[]{:S(2)}) copy-start(f32[64,32]{0,1:T(8,128)} %param.11) | copy-start | bytes 24580
  0.0 12.4 %copy-start.4 = (f32[2,64,640]{2,1,0:T(8,128)S(1)}, f32[2,64,640]{2,1,0:T(8,128)}, u32[]{:S(2)}) copy-start(f32[2,64,640]{2,1,0:T(8,128)} %param.7) | copy-start | bytes 983044
  0.0 12.4 %copy-start.6 = (f32[32]{0:T(128)S(1)}, f32[32]{0:T(128)}, u32[]{:S(2)}) copy-start(f32[32]{0:T(128)} %param.12) | copy-start | bytes 388
  0.0 14.1 %copy-start.5 = (f32[640]{0:T(1024)S(1)}, f32[640]{0:T(1024)}, u32[]{:S(2)}) copy-start(f32[640]{0:T(1024)} %param.13) | copy-start | bytes 7684
  3.4 40.3 %collective-permute-start.1 = (f32[2,66,640]{2,1,0:T(8,128)S(1)}, f32[2,66,640]{2,1,0:T(8,128)S(1)}, u32[]{:S(2)}, u32[]{:S(2)}) collective-permute-start(f32[2,66,640]{2,1,0:T(8,128)S(1)} %pad_maximum_fusion), channel_id=1, source_target_pairs={{0,16},{8,24},{16,32},{24,40},{32,48},{40,56},{48,64},{56,72},{64,... | collective-permute-start | bytes 1013768 | tf_op jit(solution)/shard_map/ppermute | solution.py:17
  4.7 38.7 %collective-permute-start = (f32[2,66,640]{2,1,0:T(8,128)S(1)}, f32[2,66,640]{2,1,0:T(8,128)S(1)}, u32[]{:S(2)}, u32[]{:S(2)}) collective-permute-start(f32[2,66,640]{2,1,0:T(8,128)S(1)} %pad_maximum_fusion), channel_id=1, source_target_pairs={{0,8},{8,16},{16,24},{24,32},{32,40},{40,48},{48,56},{56,64},{64,7... | collective-permute-start | bytes 1013768 | tf_op jit(solution)/shard_map/ppermute | solution.py:17
  6.9 36.5 %collective-permute-start.2 = (f32[64,640]{1,0:T(8,128)S(1)}, f32[64,640]{1,0:T(8,128)S(1)}, u32[]{:S(2)}, u32[]{:S(2)}) collective-permute-start(f32[64,640]{1,0:T(8,128)S(1)} %slice_bitcast_fusion.4), channel_id=1, source_target_pairs={{0,24},{8,32},{16,40},{24,48},{32,56},{40,64},{48,72},{56,80},{64,... | collective-permute-start | bytes 491528 | tf_op jit(solution)/shard_map/ppermute | solution.py:17
  17.3 54.1 %copy-start.1 = (f32[640,640]{1,0:T(8,128)}, f32[640,640]{1,0:T(8,128)S(1)}, u32[]{:S(2)}) copy-start(f32[640,640]{1,0:T(8,128)S(1)} %add_multiply_fusion.refs_3_) | copy-start | bytes 4915204
  57.8 8.6 %copy-start.2 = (f32[640,640]{1,0:T(8,128)}, f32[640,640]{1,0:T(8,128)S(1)}, u32[]{:S(2)}) copy-start(f32[640,640]{1,0:T(8,128)S(1)} %fusion.7.refs_4_) | copy-start | bytes 4915204
  66.4 2.4 %copy-start.3 = (f32[640,640]{1,0:T(8,128)}, f32[640,640]{1,0:T(8,128)S(1)}, u32[]{:S(2)}) copy-start(f32[640,640]{1,0:T(8,128)S(1)} %fusion.5.refs_5_) | copy-start | bytes 4915204

commit v6 on v5

--- a/solution.py
+++ b/solution.py
@@ -235,8 +235,42 @@
         axis=1,
     )
     packed = jnp.concatenate([states, extra], axis=1)
-    packs = [packed] + [shifted(packed, "tm", d) for d in range(1, stride)]
-    rims = [pack[-1, :dims, :] for pack in packs[1:]] + [shifted(states[-1], "tm", stride)]
+
+    def need(k):
+        if k % stride == 0:
+            return stride - 1 if k > 0 else 0
+        return k % stride - 1
+
+    devices = range(steps)
+
+    def sent(block, distance, wanted):
+        route = [(i - distance, i) for i in devices if i - distance >= 0 and wanted(i)]
+        return lax.ppermute(block, "tm", route)
+
+    core = lax.axis_index("rows") % 2
+    half_rows = dims // 2
+    packed_half = lax.dynamic_index_in_dim(packed, core, 0, keepdims=False)
+    rim_half = lax.dynamic_slice_in_dim(states[-1], core * half_rows, half_rows, 0)
+    fetched = [sent(packed_half, d, lambda i, d=d: need(i) >= d) for d in range(1, stride)]
+    fetched += [sent(rim_half, e, lambda i, e=e: need(i) + 1 == e) for e in range(1, stride + 1)]
+    bundle = jnp.concatenate(fetched, axis=0)
+    pairs = [(r, r ^ 1) for r in range(lax.axis_size("rows"))]
+    other = lax.ppermute(bundle, "rows", pairs)
+    first_half = jnp.where(core == 0, bundle, other)
+    second_half = jnp.where(core == 0, other, bundle)
+    rows_of = [f.shape[0] for f in fetched]
+    offsets = [sum(rows_of[:i]) for i in range(len(rows_of) + 1)]
+
+    def joined(i):
+        lo, hi = offsets[i], offsets[i + 1]
+        return jnp.concatenate([first_half[lo:hi], second_half[lo:hi]], axis=0)
+
+    packs = [packed] + [joined(i).reshape(packed.shape) for i in range(stride - 1)]
+    rim_parts = [joined(stride - 1 + i) for i in range(stride)]
+    rims = [
+        (packs[d + 1][-1, :dims, :] if d + 1 < stride else 0.0) + rim_parts[d]
+        for d in range(stride)
+    ]
 
     def matrices_of(rim, pack):
         block_states = pack[:, :dims, :]

time: 168 us -> 162 us (0.964)
  waiting for transfers between devices: 25.5 us -> 4.41 us
  Pallas kernels: 90.3 us -> 99.8 us
  starting transfers between devices: 3.88 us -> 7.13 us
  matrix products: 30.4 us -> 32.4 us
  local copies, waits for them, and re-layouts: 3.68 us -> 5.53 us
    ppermute x3 -> x6, waiting for transfers between devices: 25.5 us -> 4.41 us  [the longest x5 4.41 us: sent(): return lax.ppermute(block, 'tm', route)]
    pallas_call x1, Pallas kernels: 90.3 us -> 99.8 us  [chain(): pl.pallas_call(functools.partial(chain_kernel, steps, stride), out_shape=...]
    ppermute x3 -> x6, starting transfers between devices: 3.88 us -> 7.13 us  [the longest x5 5.21 us: sent(): return lax.ppermute(block, 'tm', route)]
    div x4 -> x6, other arithmetic: 3.9 us -> 3.49 us  [transition(): likelihood = likelihood / jnp.max(likelihood)]
  transfers between devices with their start and end apart: 3 -> 6, of which waited for: 1 -> 1; matrix products, arithmetic and copies ran while one was open for 6% -> 6% of each run, Pallas kernels for 0% -> 0%
where the time goes in v6:
time: 162 us
  Pallas kernels  99.8 us (62%)
  matrix products  32.4 us (20%)
  other arithmetic  11.7 us (7%)
  starting transfers between devices  7.13 us (4%)
  local copies, waits for them, and re-layouts  5.53 us (3%)
  waiting for transfers between devices  4.41 us (3%)
    pallas_call x1, Pallas kernels, chain(): pl.pallas_call(functools.partial(chain_kernel, steps, stride), out_shape=...  99.8 us
    dot_general x5, matrix products, block_product(): jnp.dot(block, matrix, precision=lax.Precision.HIGH, preferred_element_ty...  16.8 us
    dot_general x6, matrix products, transition(): lax.dot_general(previous, current, (((0,), (0,)), ((), ())), precision=hi...  12.4 us
    ppermute x5, starting transfers between devices, sent(): return lax.ppermute(block, 'tm', route)  5.21 us
    ppermute x5, waiting for transfers between devices, sent(): return lax.ppermute(block, 'tm', route)  4.41 us
    reduce_max x6, other arithmetic, transition(): likelihood = likelihood / jnp.max(likelihood)  3.52 us
    div x6, other arithmetic, transition(): likelihood = likelihood / jnp.max(likelihood)  3.49 us
    dot_general x6, matrix products, transition(): lax.dot_general(fingerprints, current, (((0,), (0,)), ((), ())), precisio...  3.24 us
  transfers between devices with their start and end apart: 6, of which 1 were waited for; matrix products, arithmetic and copies ran while one was open for 6% of the time, Pallas kernels for 0%

profile of v6, /device:TPU:504, one launch (start us, length us, event | category | flops | bytes accessed | tf_op | source)
XLA Modules:
  0.0 161.6 jit_solution(12943037780117407447)
XLA Ops:
  0.0 0.8 copy.10
  0.8 0.1 pad.19.clone
  0.9 0.8 maximum_bitcast_fusion
  1.7 0.7 convert_convert_fusion
  2.4 0.9 fusion.82
  3.3 1.3 collective-permute-start
  4.6 1.3 collective-permute-start.1
  5.9 0.9 slice.161
  6.9 0.7 collective-permute-start.2
  7.5 0.7 collective-permute-start.3
  8.2 1.3 collective-permute-start.4
  9.5 1.2 fusion.50
  10.7 0.6 fusion.122
  11.3 0.7 fusion.121
  12.0 1.2 fusion.51
  13.1 0.6 fusion.124
  13.7 0.7 fusion.123
  14.5 0.7 reduce_sum.171
  15.2 0.0 collective-permute-done.2
  15.2 0.0 collective-permute-done.3
  15.2 4.4 %collective-permute-done.4 = f32[32,640]{1,0:T(8,128)S(1)} collective-permute-done((f32[32,640]{1,0:T(8,128)S(1)}, f32[32,640]{1,0:T(8,128)S(1)}, u32[]{:S(2)}, u32[]{:S(2)}) %collective-permute-start.4) | collective-permute-done | bytes 81952 | tf_op jit(solution)/shard_map/ppermute | solution.py:248
  19.6 0.0 collective-permute-done
  19.6 0.0 collective-permute-done.1
  19.6 0.7 concatenate.40
  20.3 1.9 %collective-permute-start.5 = (f32[228,640]{1,0:T(8,128)S(1)}, f32[228,640]{1,0:T(8,128)S(1)}, u32[]{:S(2)}, u32[]{:S(2)}) collective-permute-start(f32[228,640]{1,0:T(8,128)S(1)} %concatenate.40), channel_id=1, source_target_pairs={{0,1},{1,0},{2,3},{3,2},{4,5},{5,4},{6,7},{7,6},{8,9},{9,8},{10,11... | collective-permute-start | bytes 1751048 | tf_op jit(solution)/shard_map/ppermute | solution.py:258
  22.2 0.6 fusion.147
  22.9 0.7 broadcast_divide_fusion
  23.6 2.6 %add_multiply_fusion.refs_3_ = f32[640,640]{1,0:T(8,128)S(1)} fusion(f32[640]{0:T(1024)S(1)} %get-tuple-element.11, f32[640]{0:T(1024)S(1)} %get-tuple-element.12, f32[]{:T(128)} %bitcast.14, s32[640]{0:T(1024)S(1)} %get-tuple-element.17, f32[640]{0:T(1024)S(1)} %fusion.123, f32[2,64,640]{2,1,0:T(8,128)S(1)} %copy-done.4), kind=kOutput, calls=%fused_computation.42 | convolution fusion | flops 318259200 | bytes 1976324 | tf_op jit(solution)/shard_map/dot_general | solution.py:23
  26.2 0.0 copy-start.1
  26.2 0.0 collective-permute-done.5
  26.2 0.1 broadcast_select_fusion.1
  26.3 0.1 fusion.143
  26.4 0.9 slice_bitcast_fusion.14
  27.4 2.7 %fusion.103 = f32[640,640]{1,0:T(8,128)} fusion(f32[2,66,640]{2,1,0:T(8,128)S(1)} %reshape.97), kind=kOutput, calls=%fused_computation.131 | convolution fusion | flops 314572800 | bytes 1966080 | tf_op jit(solution)/shard_map/dot_general | solution.py:23
  30.1 0.6 fusion.145
  30.7 0.0 copy-start.11
  30.7 1.5 fusion.111
  32.3 1.5 fusion.96
  33.8 0.6 fusion.146
  34.4 0.0 copy-done.11
  34.4 0.2 fusion.54
  34.7 0.6 fusion.130
  35.2 0.5 fusion.129
  35.8 0.2 fusion.55
  36.0 0.6 fusion.132
  36.6 0.5 fusion.131
  37.2 0.2 fusion.52
  37.4 0.6 fusion.126
  38.0 0.5 fusion.125
  38.6 0.2 fusion.53
  38.8 0.0 copy-start.5
  38.8 0.6 fusion.128
  39.4 0.5 fusion.127
  40.0 1.5 fusion.92
  41.5 0.1 fusion.90
  41.6 0.1 multiply_reduce_fusion
  41.6 4.8 %fusion.refs_4_ = f32[640,640]{1,0:T(8,128)S(1)} fusion(f32[640,640]{1,0:T(8,128)S(1)} %copy-done.5, f32[640,640]{1,0:T(8,128)S(1)} %fusion.92, f32[640]{0:T(1024)S(1)} %get-tuple-element.9, f32[640]{0:T(1024)S(1)} %get-tuple-element.8, f32[]{:T(128)} %bitcast.28, s32[640]{0:T(1024)S(1)} %get-tuple-element.14, f32[640]{0:T(1024)S(1)} %fusion.131, ...), kind=kOutput, calls=%fused_computation | convolution fusion | flops 1580236800 | bytes 4933128 | tf_op jit(solution)/shard_map/dot_general | solution.py:213
  46.5 4.8 %fusion.19.refs_5_ = f32[640,640]{1,0:T(8,128)S(1)} fusion(f32[640,640]{1,0:T(8,128)S(1)} %fusion.96, f32[640,640]{1,0:T(8,128)S(1)} %fusion.111, f32[640]{0:T(1024)S(1)} %get-tuple-element.6, f32[640]{0:T(1024)S(1)} %get-tuple-element.7, f32[]{:T(128)} %bitcast.20, s32[640]{0:T(1024)S(1)} %get-tuple-element.16, f32[640]{0:T(1024)S(1)} %fusion.127, ...), kind=kOutput, calls=%fused_computation.21 | convolution fusion | flops 1580236800 | bytes 4933128 | tf_op jit(solution)/shard_map/dot_general | solution.py:213
  51.3 2.5 %fusion.149 = f32[640,640]{1,0:T(8,128)S(1)} fusion(f32[640,640]{1,0:T(8,128)S(1)} %fusion.19.refs_5_, f32[640,640]{1,0:T(8,128)S(1)} %fusion.refs_4_), kind=kOutput, calls=%fused_computation.212 | convolution fusion | flops 1572864000 | bytes 4915200 | tf_op jit(solution)/shard_map/dot_general | solution.py:213
  53.8 2.6 %add_multiply_fusion.1.refs_2_ = f32[640,640]{1,0:T(8,128)S(1)} fusion(f32[640]{0:T(1024)S(1)} %get-tuple-element.12, f32[640]{0:T(1024)S(1)} %get-tuple-element.10, f32[]{:T(128)} %bitcast.4, s32[640]{0:T(1024)S(1)} %get-tuple-element.18, f32[640]{0:T(1024)S(1)} %fusion.121, f32[1,32,640]{2,1,0:T(8,128)S(1)} %copy-done.9, ...), kind=kOutput, calls=%fused_computation.44 | convolution fusion | flops 318341120 | bytes 2146308 | tf_op jit(solution)/shard_map/dot_general | solution.py:23
  56.4 2.3 %fusion.148.refs_0_ = f32[640,640]{1,0:T(8,128)S(1)} fusion(f32[640,640]{1,0:T(8,128)S(1)} %add_multiply_fusion.1.refs_2_, f32[640,640]{1,0:T(8,128)S(1)} %add_multiply_fusion.refs_3_), kind=kOutput, calls=%fused_computation.211 | convolution fusion | flops 1572864000 | bytes 4915200 | tf_op jit(solution)/shard_map/dot_general | solution.py:213
  58.7 2.4 %fusion.150.refs_1_ = f32[640,640]{1,0:T(8,128)S(1)} fusion(f32[640,640]{1,0:T(8,128)S(1)} %fusion.149, f32[640,640]{1,0:T(8,128)S(1)} %fusion.148.refs_0_), kind=kOutput, calls=%fused_computation.213 | convolution fusion | flops 1572864000 | bytes 4915200 | tf_op jit(solution)/shard_map/dot_general | solution.py:213
  61.1 99.8 %shard_map.73 = f32[8,640]{1,0:T(8,128)S(1)} custom-call(f32[640,640]{1,0:T(8,128)S(1)} %fusion.148.refs_0_, f32[640,640]{1,0:T(8,128)S(1)} %fusion.150.refs_1_, f32[640,640]{1,0:T(8,128)S(1)} %add_multiply_fusion.1.refs_2_, f32[640,640]{1,0:T(8,128)} %copy-done.1, f32[640,640]{1,0:T(8,128)} %copy-done.2, f32[640,640]{1,0:T(8,128)} %copy-done.3, ...), custom_call_target="tpu_custom_call" | custom-call | tf_op jit(solution)/shard_map/pallas_call | solution.py:190
  161.0 0.6 fusion.133
  (42 shorter events, 0.4 us)
Async XLA Ops:
  0.0 9.5 %copy-start = (f32[64,32]{0,1:T(8,128)S(1)}, f32[64,32]{0,1:T(8,128)}, u32[]{:S(2)}) copy-start(f32[64,32]{0,1:T(8,128)} %param.11) | copy-start | bytes 24580
  0.0 14.4 %copy-start.4 = (f32[2,64,640]{2,1,0:T(8,128)S(1)}, f32[2,64,640]{2,1,0:T(8,128)}, u32[]{:S(2)}) copy-start(f32[2,64,640]{2,1,0:T(8,128)} %param.7) | copy-start | bytes 983044
  0.0 14.4 %copy-start.12 = (f32[640]{0:T(1024)S(1)}, f32[640]{0:T(1024)}, u32[]{:S(2)}) copy-start(f32[640]{0:T(1024)} %param.13) | copy-start | bytes 7684
  3.3 16.3 %collective-permute-start = (f32[66,640]{1,0:T(8,128)S(1)}, f32[66,640]{1,0:T(8,128)S(1)}, u32[]{:S(2)}, u32[]{:S(2)}) collective-permute-start(f32[66,640]{1,0:T(8,128)S(1)} %fusion.82), channel_id=1, source_target_pairs={{8,16},{16,24},{32,40},{40,48},{56,64},{64,72},{80,88},{88,96},{10... | collective-permute-start | bytes 506888 | tf_op jit(solution)/shard_map/ppermute | solution.py:248
  4.6 15.0 %collective-permute-start.1 = (f32[66,640]{1,0:T(8,128)S(1)}, f32[66,640]{1,0:T(8,128)S(1)}, u32[]{:S(2)}, u32[]{:S(2)}) collective-permute-start(f32[66,640]{1,0:T(8,128)S(1)} %fusion.82), channel_id=1, source_target_pairs={{8,24},{32,48},{56,72},{80,96},{104,120},{128,144},{152,168},{176,... | collective-permute-start | bytes 506888 | tf_op jit(solution)/shard_map/ppermute | solution.py:248
  6.9 8.3 %collective-permute-start.2 = (f32[32,640]{1,0:T(8,128)S(1)}, f32[32,640]{1,0:T(8,128)S(1)}, u32[]{:S(2)}, u32[]{:S(2)}) collective-permute-start(f32[32,640]{1,0:T(8,128)S(1)} %dynamic-slice_bitcast_fusion), channel_id=1, source_target_pairs={{0,8},{24,32},{48,56},{72,80},{96,104},{120,128},{144,152},{168,17... | collective-permute-start | bytes 245768 | tf_op jit(solution)/shard_map/ppermute | solution.py:248
  7.5 7.6 %collective-permute-start.3 = (f32[32,640]{1,0:T(8,128)S(1)}, f32[32,640]{1,0:T(8,128)S(1)}, u32[]{:S(2)}, u32[]{:S(2)}) collective-permute-start(f32[32,640]{1,0:T(8,128)S(1)} %dynamic-slice_bitcast_fusion), channel_id=1, source_target_pairs={{0,16},{24,40},{48,64},{72,88},{96,112},{120,136},{144,160},{168,1... | collective-permute-start | bytes 245768 | tf_op jit(solution)/shard_map/ppermute | solution.py:248
  8.2 11.4 %collective-permute-start.4 = (f32[32,640]{1,0:T(8,128)S(1)}, f32[32,640]{1,0:T(8,128)S(1)}, u32[]{:S(2)}, u32[]{:S(2)}) collective-permute-start(f32[32,640]{1,0:T(8,128)S(1)} %dynamic-slice_bitcast_fusion), channel_id=1, source_target_pairs={{0,24},{24,48},{48,72},{72,96},{96,120},{120,144},{144,168},{168,1... | collective-permute-start | bytes 245768 | tf_op jit(solution)/shard_map/ppermute | solution.py:248
  20.3 5.9 %collective-permute-start.5 = (f32[228,640]{1,0:T(8,128)S(1)}, f32[228,640]{1,0:T(8,128)S(1)}, u32[]{:S(2)}, u32[]{:S(2)}) collective-permute-start(f32[228,640]{1,0:T(8,128)S(1)} %concatenate.40), channel_id=1, source_target_pairs={{0,1},{1,0},{2,3},{3,2},{4,5},{5,4},{6,7},{7,6},{8,9},{9,8},{10,11... | collective-permute-start | bytes 1751048 | tf_op jit(solution)/shard_map/ppermute | solution.py:258
  26.2 30.2 %copy-start.1 = (f32[640,640]{1,0:T(8,128)}, f32[640,640]{1,0:T(8,128)S(1)}, u32[]{:S(2)}) copy-start(f32[640,640]{1,0:T(8,128)S(1)} %add_multiply_fusion.refs_3_) | copy-start | bytes 4915204
  30.7 3.7 %copy-start.11 = (f32[32]{0:T(128)S(1)}, f32[32]{0:T(128)}, u32[]{:S(2)}) copy-start(f32[32]{0:T(128)} %param.12) | copy-start | bytes 388
  33.8 7.7 %copy-start.7 = (f32[32,640]{1,0:T(8,128)S(1)}, f32[32,640]{1,0:T(8,128)}, u32[]{:S(2)}) copy-start(f32[32,640]{1,0:T(8,128)} %get-tuple-element.28) | copy-start | bytes 245764
  33.8 7.7 %copy-start.8 = (f32[32,640]{1,0:T(8,128)S(1)}, f32[32,640]{1,0:T(8,128)}, u32[]{:S(2)}) copy-start(f32[32,640]{1,0:T(8,128)} %get-tuple-element.51) | copy-start | bytes 245764
  35.8 5.8 %copy-start.6 = (f32[32,640]{1,0:T(8,128)S(1)}, f32[32,640]{1,0:T(8,128)}, u32[]{:S(2)}) copy-start(f32[32,640]{1,0:T(8,128)} %get-tuple-element.49) | copy-start | bytes 245764
  38.8 2.8 %copy-start.5 = (f32[640,640]{1,0:T(8,128)S(1)}, f32[640,640]{1,0:T(8,128)}, u32[]{:S(2)}) copy-start(f32[640,640]{1,0:T(8,128)} %fusion.103) | copy-start | bytes 4915204
  46.5 4.8 %copy-start.2 = (f32[640,640]{1,0:T(8,128)}, f32[640,640]{1,0:T(8,128)S(1)}, u32[]{:S(2)}) copy-start(f32[640,640]{1,0:T(8,128)S(1)} %fusion.refs_4_) | copy-start | bytes 4915204
  51.2 2.5 %copy-start.3 = (f32[640,640]{1,0:T(8,128)}, f32[640,640]{1,0:T(8,128)S(1)}, u32[]{:S(2)}) copy-start(f32[640,640]{1,0:T(8,128)S(1)} %fusion.19.refs_5_) | copy-start | bytes 4915204
  51.2 2.5 %copy-start.9 = (f32[1,32,640]{2,1,0:T(8,128)S(1)}, f32[1,32,640]{2,1,0:T(8,128)}, u32[]{:S(2)}) copy-start(f32[1,32,640]{2,1,0:T(8,128)} %get-tuple-element.27) | copy-start | bytes 245764
  51.3 2.5 %copy-start.10 = (f32[1,32,640]{2,1,0:T(8,128)S(1)}, f32[1,32,640]{2,1,0:T(8,128)}, u32[]{:S(2)}) copy-start(f32[1,32,640]{2,1,0:T(8,128)} %get-tuple-element.52) | copy-start | bytes 245764

commit v7 on v6

--- a/solution.py
+++ b/solution.py
@@ -272,25 +272,37 @@
         for d in range(stride)
     ]
 
-    def matrices_of(rim, pack):
-        block_states = pack[:, :dims, :]
-        parents = pack[:, dims, :].astype(jnp.int32)
-        observed = pack[:, dims + 1, :tracers]
-        mixing = pack[:, dims + 1, tracers]
-        previous = jnp.concatenate([rim[None], block_states[:-1]], axis=0)
-        return [
-            transition(
-                previous[s], block_states[s], parents[s], observed[s], mixing[s],
-                fingerprints, tracer_scale,
-            )
-            for s in range(local)
-        ]
-
-    own = matrices_of(rims[0], packs[0])
-    blocks = [block_product(own)] + [
-        block_product(matrices_of(rims[d], packs[d])) for d in range(1, stride)
-    ]
+    previous = []
+    current = []
+    parents = []
+    observed = []
+    mixing = []
+    for d in range(stride):
+        block_states = packs[d][:, :dims, :]
+        previous += [rims[d], block_states[0]]
+        current += [block_states[0], block_states[1]]
+        parents.append(packs[d][:, dims, :])
+        observed.append(packs[d][:, dims + 1, :tracers])
+        mixing.append(packs[d][:, dims + 1, tracers])
+    weights_all = jax.vmap(transition, in_axes=(0, 0, 0, 0, 0, None, None))(
+        jnp.stack(previous),
+        jnp.stack(current),
+        jnp.concatenate(parents).astype(jnp.int32),
+        jnp.concatenate(observed),
+        jnp.concatenate(mixing),
+        fingerprints,
+        tracer_scale,
+    )
+    products = lax.dot_general(
+        weights_all[0::2],
+        weights_all[1::2],
+        (((2,), (1,)), ((0,), (0,))),
+        precision=lax.Precision.HIGH,
+        preferred_element_type=jnp.float32,
+    )
+    blocks = [products[d] for d in range(stride)]
     combined = block_product(blocks[::-1])
+    own = [weights_all[0], weights_all[1]]
 
     start = prior_weights / jnp.sum(prior_weights)
     start8 = jnp.broadcast_to(start[None, :], (8, count))

time: 162 us -> 147 us (0.907)
  matrix products: 32.4 us -> 24.6 us
  Pallas kernels: 99.8 us -> 92.4 us
  other arithmetic: 11.7 us -> 6.44 us
  waiting for transfers between devices: 4.41 us -> 8.52 us
    dot_general x5 -> x2, matrix products: 16.8 us -> 4.92 us  [block_product(): jnp.dot(block, matrix, precision=lax.Precision.HIGH, preferred_element_ty...]
    pallas_call x1, Pallas kernels: 99.8 us -> 92.4 us  [chain(): pl.pallas_call(functools.partial(chain_kernel, steps, stride), out_shape=...]
    dot_general x0 -> x1, matrix products: none -> 7.02 us  [shards(): lax.dot_general(weights_all[0::2], weights_all[1::2], (((2,), (1,)), ((0,...]
    ppermute x5, waiting for transfers between devices: 4.41 us -> 8.52 us  [sent(): return lax.ppermute(block, 'tm', route)]
    div x6 -> x1, other arithmetic: 3.49 us -> 0.07 us  [transition(): likelihood = likelihood / jnp.max(likelihood)]
    reduce_max x6 -> x1, other arithmetic: 3.52 us -> 0.12 us  [transition(): likelihood = likelihood / jnp.max(likelihood)]
    squeeze x0 -> x3, local copies, waits for them, and re-layouts: none -> 3.39 us  [the longest x1 2 us: shards(): blocks = [products[d] for d in range(stride)]]
    dot_general x6 -> x1, matrix products: 3.24 us -> 0.68 us  [transition(): lax.dot_general(fingerprints, current, (((0,), (0,)), ((), ())), precisio...]
  transfers between devices with their start and end apart: 6 -> 6, of which waited for: 1 -> 3; matrix products, arithmetic and copies ran while one was open for 6% -> 3% of each run, Pallas kernels for 0% -> 0%
where the time goes in v7:
time: 147 us; the launch traced here: 146 us
  Pallas kernels  92.4 us (63%)
  matrix products  24.6 us (17%)
  waiting for transfers between devices  8.52 us (6%)
  starting transfers between devices  7.26 us (5%)
  local copies, waits for them, and re-layouts  6.7 us (5%)
  other arithmetic  6.44 us (4%)
    pallas_call x1, Pallas kernels, chain(): pl.pallas_call(functools.partial(chain_kernel, steps, stride), out_shape=...  92.4 us
    dot_general x1, matrix products, transition(): lax.dot_general(previous, current, (((0,), (0,)), ((), ())), precision=hi...  12 us
    ppermute x5, waiting for transfers between devices, sent(): return lax.ppermute(block, 'tm', route)  8.52 us
    dot_general x1, matrix products, shards(): lax.dot_general(weights_all[0::2], weights_all[1::2], (((2,), (1,)), ((0,...  7.02 us
    ppermute x5, starting transfers between devices, sent(): return lax.ppermute(block, 'tm', route)  5.34 us
    dot_general x2, matrix products, block_product(): jnp.dot(block, matrix, precision=lax.Precision.HIGH, preferred_element_ty...  4.92 us
  transfers between devices with their start and end apart: 6, of which 3 were waited for; matrix products, arithmetic and copies ran while one was open for 3% of the time, Pallas kernels for 0%

profile of v7, /device:TPU:504, one launch (start us, length us, event | category | flops | bytes accessed | tf_op | source)
XLA Modules:
  0.0 146.2 jit_solution(12249873918647779859)
XLA Ops:
  0.0 0.0 copy-start
  0.0 0.8 copy.11
  0.8 0.1 pad.27.clone
  0.8 0.8 maximum_bitcast_fusion.1
  1.6 0.7 fusion.24
  2.3 0.9 fusion.8
  3.3 1.3 collective-permute-start.1
  4.6 1.3 collective-permute-start
  5.9 0.9 slice.116
  6.8 0.0 copy-start.1
  6.8 1.4 collective-permute-start.4
  8.3 0.7 collective-permute-start.3
  8.9 0.7 collective-permute-start.2
  9.6 6.0 %collective-permute-done.4 = f32[32,640]{1,0:T(8,128)S(1)} collective-permute-done((f32[32,640]{1,0:T(8,128)S(1)}, f32[32,640]{1,0:T(8,128)S(1)}, u32[]{:S(2)}, u32[]{:S(2)}) %collective-permute-start.4) | collective-permute-done | bytes 81952 | tf_op jit(solution)/shard_map/ppermute | solution.py:248
  15.6 0.0 collective-permute-done.3
  15.6 0.0 collective-permute-done.2
  15.6 0.7 collective-permute-done.1
  16.4 1.8 %collective-permute-done = f32[66,640]{1,0:T(8,128)S(1)} collective-permute-done((f32[66,640]{1,0:T(8,128)S(1)}, f32[66,640]{1,0:T(8,128)S(1)}, u32[]{:S(2)}, u32[]{:S(2)}) %collective-permute-start) | collective-permute-done | bytes 168992 | tf_op jit(solution)/shard_map/ppermute | solution.py:248
  18.1 0.7 concatenate.53
  18.8 1.9 %collective-permute-start.5 = (f32[228,640]{1,0:T(8,128)S(1)}, f32[228,640]{1,0:T(8,128)S(1)}, u32[]{:S(2)}, u32[]{:S(2)}) collective-permute-start(f32[228,640]{1,0:T(8,128)S(1)} %concatenate.53), channel_id=1, source_target_pairs={{0,1},{1,0},{2,3},{3,2},{4,5},{5,4},{6,7},{7,6},{8,9},{9,8},{10,11... | collective-permute-start | bytes 1751048 | tf_op jit(solution)/shard_map/ppermute | solution.py:258
  20.8 1.3 reduce_sum.39
  22.0 0.2 slice_reduce_fusion.2
  22.2 1.3 broadcast_divide_fusion
  23.6 0.0 copy-start.2
  23.6 0.0 collective-permute-done.5
  23.6 0.2 broadcast_select_fusion.1
  23.8 0.1 fusion.22
  23.9 0.2 slice_reduce_fusion.1
  24.2 0.2 slice_reduce_fusion
  24.5 0.0 copy-done.1
  24.5 0.1 multiply_reduce_fusion
  24.6 0.0 copy-done
  24.6 0.0 copy-done.2
  24.6 0.7 fusion.5
  25.3 0.1 fusion.13
  25.4 0.1 fusion.12
  25.7 0.1 multiply_reduce_fusion.1
  25.8 0.1 pad_maximum_fusion.6
  25.8 12.0 %add_multiply_fusion = f32[6,640,640]{2,1,0:T(8,128)S(1)} fusion(f32[6,640]{1,0:T(8,128)S(1)} %multiply_reduce_fusion, f32[6,640]{1,0:T(8,128)S(1)} %multiply_reduce_fusion.1, f32[6]{0:T(128)S(1)} %pad_maximum_fusion.6, s32[6,640]{1,0:T(8,128)S(1)} %maximum_convert_fusion, f32[6,640]{1,0:T(8,128)S(1)} %fusion.12, ...), kind=kOutput, calls=%fused_computation | convolution fusion | flops 1910046720 | bytes 11857944 | tf_op jit(solution)/shard_map/vmap()/dot_general | solution.py:23
  37.8 1.4 slice_bitcast_fusion
  39.2 7.0 %fusion = f32[3,640,640]{2,1,0:T(8,128)S(1)} fusion(f32[6,640,640]{2,1,0:T(8,128)S(1)} %add_multiply_fusion), kind=kOutput, calls=%fused_computation.2 | convolution fusion | flops 4718592000 | bytes 14745600 | tf_op jit(solution)/shard_map/dot_general | solution.py:296
  46.3 2.3 %fusion.19 = f32[640,640]{1,0:T(8,128)S(1)} fusion(f32[3,640,640]{2,1,0:T(8,128)S(1)} %fusion), kind=kOutput, calls=%fused_computation.62 | convolution fusion | flops 1572864000 | bytes 4915200 | tf_op jit(solution)/shard_map/dot_general | solution.py:213
  48.6 2.0 %slice_bitcast_fusion.3 = (f32[640,640]{1,0:T(8,128)}, f32[640,640]{1,0:T(8,128)}, f32[640,640]{1,0:T(8,128)S(1)}) fusion(f32[3,640,640]{2,1,0:T(8,128)S(1)} %fusion), kind=kLoop, calls=%fused_computation.8 | loop fusion | bytes 9830400 | tf_op jit(solution)/shard_map/squeeze | solution.py:303
  50.6 2.6 %fusion.18.refs_1_ = f32[640,640]{1,0:T(8,128)S(1)} fusion(f32[640,640]{1,0:T(8,128)S(1)} %fusion.19, f32[3,640,640]{2,1,0:T(8,128)S(1)} %fusion), kind=kOutput, calls=%fused_computation.61 | convolution fusion | flops 1572864000 | bytes 4915200 | tf_op jit(solution)/shard_map/dot_general | solution.py:213
  53.2 92.4 %shard_map.73 = f32[8,640]{1,0:T(8,128)S(1)} custom-call(f32[640,640]{1,0:T(8,128)S(1)} %get-tuple-element.9.refs_0_, f32[640,640]{1,0:T(8,128)S(1)} %fusion.18.refs_1_, f32[640,640]{1,0:T(8,128)S(1)} %get-tuple-element.6.refs_2_, f32[640,640]{1,0:T(8,128)} %get-tuple-element.5.refs_3_, f32[640,640]{1,0:T(8,128)} %get-tuple-element.8.refs_4_, ...), custom_call_target="tpu_custom_call" | custom-call | tf_op jit(solution)/shard_map/pallas_call | solution.py:190
  145.6 0.6 fusion.15
  (28 shorter events, 0.4 us)
Async XLA Ops:
  0.0 24.6 %copy-start = (f32[64,32]{0,1:T(8,128)S(1)}, f32[64,32]{0,1:T(8,128)}, u32[]{:S(2)}) copy-start(f32[64,32]{0,1:T(8,128)} %param.11) | copy-start | bytes 24580
  3.3 13.1 %collective-permute-start.1 = (f32[66,640]{1,0:T(8,128)S(1)}, f32[66,640]{1,0:T(8,128)S(1)}, u32[]{:S(2)}, u32[]{:S(2)}) collective-permute-start(f32[66,640]{1,0:T(8,128)S(1)} %fusion.8), channel_id=1, source_target_pairs={{8,24},{32,48},{56,72},{80,96},{104,120},{128,144},{152,168},{176,... | collective-permute-start | bytes 506888 | tf_op jit(solution)/shard_map/ppermute | solution.py:248
  4.6 13.6 %collective-permute-start = (f32[66,640]{1,0:T(8,128)S(1)}, f32[66,640]{1,0:T(8,128)S(1)}, u32[]{:S(2)}, u32[]{:S(2)}) collective-permute-start(f32[66,640]{1,0:T(8,128)S(1)} %fusion.8), channel_id=1, source_target_pairs={{8,16},{16,24},{32,40},{40,48},{56,64},{64,72},{80,88},{88,96},{10... | collective-permute-start | bytes 506888 | tf_op jit(solution)/shard_map/ppermute | solution.py:248
  6.8 17.6 %copy-start.1 = (f32[2,64,640]{2,1,0:T(8,128)S(1)}, f32[2,64,640]{2,1,0:T(8,128)}, u32[]{:S(2)}) copy-start(f32[2,64,640]{2,1,0:T(8,128)} %param.7) | copy-start | bytes 983044
  6.8 8.8 %collective-permute-start.4 = (f32[32,640]{1,0:T(8,128)S(1)}, f32[32,640]{1,0:T(8,128)S(1)}, u32[]{:S(2)}, u32[]{:S(2)}) collective-permute-start(f32[32,640]{1,0:T(8,128)S(1)} %dynamic-slice_bitcast_fusion), channel_id=1, source_target_pairs={{0,24},{24,48},{48,72},{72,96},{96,120},{120,144},{144,168},{168,1... | collective-permute-start | bytes 245768 | tf_op jit(solution)/shard_map/ppermute | solution.py:248
  8.3 7.4 %collective-permute-start.3 = (f32[32,640]{1,0:T(8,128)S(1)}, f32[32,640]{1,0:T(8,128)S(1)}, u32[]{:S(2)}, u32[]{:S(2)}) collective-permute-start(f32[32,640]{1,0:T(8,128)S(1)} %dynamic-slice_bitcast_fusion), channel_id=1, source_target_pairs={{0,16},{24,40},{48,64},{72,88},{96,112},{120,136},{144,160},{168,1... | collective-permute-start | bytes 245768 | tf_op jit(solution)/shard_map/ppermute | solution.py:248
  8.9 6.7 %collective-permute-start.2 = (f32[32,640]{1,0:T(8,128)S(1)}, f32[32,640]{1,0:T(8,128)S(1)}, u32[]{:S(2)}, u32[]{:S(2)}) collective-permute-start(f32[32,640]{1,0:T(8,128)S(1)} %dynamic-slice_bitcast_fusion), channel_id=1, source_target_pairs={{0,8},{24,32},{48,56},{72,80},{96,104},{120,128},{144,152},{168,17... | collective-permute-start | bytes 245768 | tf_op jit(solution)/shard_map/ppermute | solution.py:248
  18.8 4.8 %collective-permute-start.5 = (f32[228,640]{1,0:T(8,128)S(1)}, f32[228,640]{1,0:T(8,128)S(1)}, u32[]{:S(2)}, u32[]{:S(2)}) collective-permute-start(f32[228,640]{1,0:T(8,128)S(1)} %concatenate.53), channel_id=1, source_target_pairs={{0,1},{1,0},{2,3},{3,2},{4,5},{5,4},{6,7},{7,6},{8,9},{9,8},{10,11... | collective-permute-start | bytes 1751048 | tf_op jit(solution)/shard_map/ppermute | solution.py:258
  23.6 1.0 copy-start.2

commit v8 on v7

--- a/solution.py
+++ b/solution.py
@@ -70,19 +70,19 @@
 def chain_kernel(
     steps, stride, *refs,
 ):
-    n_in = stride + 4
-    hbm = refs[:n_in - 1]
-    start_ref = refs[n_in - 1]
-    out_ref, recv_buf, send_buf, send_sem, recv_sem, load_sem = refs[n_in:n_in + 6]
-    local = refs[n_in + 6:]
+    weights_hbm, products_hbm, combined_hbm, prior_ref = refs[:4]
+    out_ref, recv_buf, send_buf, send_sem, recv_sem, load_sem = refs[4:10]
+    local = refs[10:]
     me = lax.axis_index("tm")
     row = lax.axis_index("rows")
     last = steps - 1
     phase = me % stride
     node = phase == 0
 
+    sources = [products_hbm.at[0], combined_hbm, weights_hbm.at[0], weights_hbm.at[1]]
+    sources += [products_hbm.at[d] for d in range(1, stride)]
     loads = [
-        pltpu.make_async_copy(hbm[i], local[i], load_sem.at[i]) for i in range(len(hbm))
+        pltpu.make_async_copy(sources[i], local[i], load_sem.at[i]) for i in range(len(sources))
     ]
     for load in loads:
         load.start()
@@ -143,8 +143,9 @@
 
     @pl.when(me == 0)
     def _():
-        out_ref[...] = start_ref[...]
-        send_all(normalized(vec_mat(start_ref[...], block_ref[...])))
+        start = spread(normalized(prior_ref[0:1, :]), out_ref)
+        out_ref[...] = start
+        send_all(normalized(vec_mat(start, block_ref[...])))
 
     @pl.when(me > 0)
     def _():
@@ -184,13 +185,13 @@
                 copies[d - 1].wait_send()
 
 
-def chain(block, combined, first, second, befores, start, steps, stride):
-    count = block.shape[0]
-    matrices = [block, combined, first, second] + list(befores)
+def chain(weights_all, products, combined, prior, steps, stride):
+    count = combined.shape[0]
+    loaded = stride + 3
     return pl.pallas_call(
         functools.partial(chain_kernel, steps, stride),
         out_shape=jax.ShapeDtypeStruct((8, count), jnp.float32),
-        in_specs=[pl.BlockSpec(memory_space=pl.ANY)] * len(matrices)
+        in_specs=[pl.BlockSpec(memory_space=pl.ANY)] * 3
         + [pl.BlockSpec(memory_space=pltpu.VMEM)],
         out_specs=pl.BlockSpec(memory_space=pltpu.VMEM),
         scratch_shapes=[
@@ -198,13 +199,13 @@
             pltpu.VMEM((1, count), jnp.float32),
             pltpu.SemaphoreType.DMA((stride,)),
             pltpu.SemaphoreType.DMA,
-            pltpu.SemaphoreType.DMA((len(matrices),)),
+            pltpu.SemaphoreType.DMA((loaded,)),
         ]
-        + [pltpu.VMEM((count, count), jnp.float32) for _ in matrices],
+        + [pltpu.VMEM((count, count), jnp.float32) for _ in range(loaded)],
         compiler_params=pltpu.CompilerParams(
             collective_id=0, has_side_effects=True, vmem_limit_bytes=48 * 1024 * 1024
         ),
-    )(*matrices, start)
+    )(weights_all, products, combined, prior)
 
 
 def block_product(matrices):
@@ -300,13 +301,10 @@
         precision=lax.Precision.HIGH,
         preferred_element_type=jnp.float32,
     )
-    blocks = [products[d] for d in range(stride)]
-    combined = block_product(blocks[::-1])
-    own = [weights_all[0], weights_all[1]]
-
-    start = prior_weights / jnp.sum(prior_weights)
-    start8 = jnp.broadcast_to(start[None, :], (8, count))
-    weights = chain(blocks[0], combined, own[0], own[1], blocks[1:], start8, steps, stride)
+    combined = block_product([products[d] for d in range(stride - 1, -1, -1)])
+
+    prior8 = jnp.broadcast_to(prior_weights[None, :], (8, count))
+    weights = chain(weights_all, products, combined, prior8, steps, stride)
     mine = lax.dynamic_slice_in_dim(weights[:local], row_start, own_rows, 1)
     return count * mine
 

time: 147 us -> 148 us (level)
  Pallas kernels: 92.4 us -> 96 us
  local copies, waits for them, and re-layouts: 6.7 us -> 3.34 us
  waiting for transfers between devices: 8.52 us -> 11.8 us
  other arithmetic: 6.44 us -> 3.73 us
    pallas_call x1, Pallas kernels: 92.4 us -> 96 us  [chain(): pl.pallas_call(functools.partial(chain_kernel, steps, stride), out_shape=...]
    squeeze x2 -> x0, local copies, waits for them, and re-layouts: 3.38 us -> none  [the longest x1 2 us: shards(): blocks = [products[d] for d in range(stride)]]
    ppermute x1, waiting for transfers between devices: 0.01 us -> 1.77 us  [shards(): other = lax.ppermute(bundle, 'rows', pairs)]
    ppermute x5, waiting for transfers between devices: 8.52 us -> 10.1 us  [sent(): return lax.ppermute(block, 'tm', route)]
  transfers between devices with their start and end apart: 6 -> 6, of which waited for: 3 -> 2; matrix products, arithmetic and copies ran while one was open for 3% -> 1% of each run, Pallas kernels for 0% -> 0%
where the time goes in v8:
time: 148 us; the launch traced here: 147 us
  Pallas kernels  96 us (65%)
  matrix products  24.8 us (17%)
  waiting for transfers between devices  11.8 us (8%)
  starting transfers between devices  7.26 us (5%)
  other arithmetic  3.73 us (3%)
  local copies, waits for them, and re-layouts  3.34 us (2%)
    pallas_call x1, Pallas kernels, chain(): pl.pallas_call(functools.partial(chain_kernel, steps, stride), out_shape=...  96 us
    dot_general x1, matrix products, transition(): lax.dot_general(previous, current, (((0,), (0,)), ((), ())), precision=hi...  12 us
    ppermute x5, waiting for transfers between devices, sent(): return lax.ppermute(block, 'tm', route)  10.1 us
    dot_general x1, matrix products, shards(): lax.dot_general(weights_all[0::2], weights_all[1::2], (((2,), (1,)), ((0,...  7.28 us
    ppermute x5, starting transfers between devices, sent(): return lax.ppermute(block, 'tm', route)  5.34 us
    dot_general x2, matrix products, block_product(): jnp.dot(block, matrix, precision=lax.Precision.HIGH, preferred_element_ty...  4.9 us
  transfers between devices with their start and end apart: 6, of which 2 were waited for; matrix products, arithmetic and copies ran while one was open for 1% of the time, Pallas kernels for 0%

profile of v8, /device:TPU:504, one launch (start us, length us, event | category | flops | bytes accessed | tf_op | source)
XLA Modules:
  0.0 147.4 jit_solution(3111661798896805822)
XLA Ops:
  0.0 0.0 copy-start
  0.0 0.8 copy.11
  0.8 0.1 pad.27.clone
  0.8 0.8 maximum_bitcast_fusion.1
  1.6 0.7 fusion.24
  2.3 0.9 fusion.10
  3.3 1.3 collective-permute-start
  4.6 1.3 collective-permute-start.1
  5.9 0.9 slice.110
  6.8 0.0 copy-start.3
  6.8 0.8 collective-permute-start.2
  7.6 0.7 collective-permute-start.3
  8.3 1.3 collective-permute-start.4
  9.6 0.0 collective-permute-done.2
  9.6 0.0 collective-permute-done.3
  9.6 10.0 %collective-permute-done.4 = f32[32,640]{1,0:T(8,128)S(1)} collective-permute-done((f32[32,640]{1,0:T(8,128)S(1)}, f32[32,640]{1,0:T(8,128)S(1)}, u32[]{:S(2)}, u32[]{:S(2)}) %collective-permute-start.4) | collective-permute-done | bytes 81952 | tf_op jit(solution)/shard_map/ppermute | solution.py:249
  19.7 0.0 collective-permute-done
  19.7 0.0 collective-permute-done.1
  19.7 0.7 concatenate.53
  20.4 1.9 %collective-permute-start.5 = (f32[228,640]{1,0:T(8,128)S(1)}, f32[228,640]{1,0:T(8,128)S(1)}, u32[]{:S(2)}, u32[]{:S(2)}) collective-permute-start(f32[228,640]{1,0:T(8,128)S(1)} %concatenate.53), channel_id=1, source_target_pairs={{0,1},{1,0},{2,3},{3,2},{4,5},{5,4},{6,7},{7,6},{8,9},{9,8},{10,11... | collective-permute-start | bytes 1751048 | tf_op jit(solution)/shard_map/ppermute | solution.py:259
  22.3 0.2 slice_reduce_fusion.2
  22.5 0.0 copy-start.5
  22.5 1.8 %collective-permute-done.5 = f32[228,640]{1,0:T(8,128)S(1)} collective-permute-done((f32[228,640]{1,0:T(8,128)S(1)}, f32[228,640]{1,0:T(8,128)S(1)}, u32[]{:S(2)}, u32[]{:S(2)}) %collective-permute-start.5) | collective-permute-done | bytes 583712 | tf_op jit(solution)/shard_map/ppermute | solution.py:259
  24.3 0.1 broadcast_select_fusion.1
  24.4 0.1 fusion.22
  24.8 0.2 slice_reduce_fusion.1
  24.9 0.2 slice_reduce_fusion
  25.1 0.0 copy-done.3
  25.1 0.1 multiply_reduce_fusion
  25.2 0.0 copy-done
  25.2 0.0 copy-done.5
  25.2 0.7 fusion.7
  25.9 0.1 fusion.15
  26.1 0.1 fusion.14
  26.3 0.1 multiply_reduce_fusion.1
  26.4 0.1 pad_maximum_fusion.6
  26.5 12.0 %add_multiply_fusion.refs_0_ = f32[6,640,640]{2,1,0:T(8,128)S(1)} fusion(f32[6,640]{1,0:T(8,128)S(1)} %multiply_reduce_fusion, f32[6,640]{1,0:T(8,128)S(1)} %multiply_reduce_fusion.1, f32[6]{0:T(128)S(1)} %pad_maximum_fusion.6, s32[6,640]{1,0:T(8,128)S(1)} %maximum_convert_fusion, f32[6,640]{1,0:T(8,128)S(1)} %fusion.14, ...), kind=kOutput, calls=%fused_computation | convolution fusion | flops 1910046720 | bytes 11857944 | tf_op jit(solution)/shard_map/vmap()/dot_general | solution.py:23
  38.5 0.0 copy-start.2
  38.5 7.3 %fusion.refs_1_ = f32[3,640,640]{2,1,0:T(8,128)S(1)} fusion(f32[6,640,640]{2,1,0:T(8,128)S(1)} %add_multiply_fusion.refs_0_), kind=kOutput, calls=%fused_computation.2 | convolution fusion | flops 4718592000 | bytes 14745600 | tf_op jit(solution)/shard_map/dot_general | solution.py:297
  45.8 0.0 copy-done.2
  45.8 0.0 copy-start.1
  45.8 0.0 copy-start.4
  45.8 2.5 %fusion.4 = f32[640,640]{1,0:T(8,128)S(1)} fusion(f32[3,640,640]{2,1,0:T(8,128)S(1)} %fusion.refs_1_), kind=kOutput, calls=%fused_computation.8 | convolution fusion | flops 1572864000 | bytes 4915200 | tf_op jit(solution)/shard_map/dot_general | solution.py:214
  48.3 2.4 %fusion.3.refs_2_ = f32[640,640]{1,0:T(8,128)S(1)} fusion(f32[640,640]{1,0:T(8,128)S(1)} %fusion.4, f32[3,640,640]{2,1,0:T(8,128)S(1)} %fusion.refs_1_), kind=kOutput, calls=%fused_computation.6 | convolution fusion | flops 1572864000 | bytes 4915200 | tf_op jit(solution)/shard_map/dot_general | solution.py:214
  50.7 0.0 copy-done.4
  50.7 0.0 copy-done.1
  50.7 96.0 %shard_map.73 = f32[8,640]{1,0:T(8,128)S(1)} custom-call(f32[6,640,640]{2,1,0:T(8,128)} %copy-done.2, f32[3,640,640]{2,1,0:T(8,128)} %copy-done.1, f32[640,640]{1,0:T(8,128)S(1)} %fusion.3.refs_2_, f32[8,640]{1,0:T(8,128)S(1)} %broadcast_in_dim.14.refs_3_), custom_call_target="tpu_custom_call" | custom-call | tf_op jit(solution)/shard_map/pallas_call | solution.py:191
  146.8 0.6 fusion.17
  (28 shorter events, 0.4 us)
Async XLA Ops:
  0.0 25.2 %copy-start = (f32[64,32]{0,1:T(8,128)S(1)}, f32[64,32]{0,1:T(8,128)}, u32[]{:S(2)}) copy-start(f32[64,32]{0,1:T(8,128)} %param.11) | copy-start | bytes 24580
  3.3 16.4 %collective-permute-start = (f32[66,640]{1,0:T(8,128)S(1)}, f32[66,640]{1,0:T(8,128)S(1)}, u32[]{:S(2)}, u32[]{:S(2)}) collective-permute-start(f32[66,640]{1,0:T(8,128)S(1)} %fusion.10), channel_id=1, source_target_pairs={{8,16},{16,24},{32,40},{40,48},{56,64},{64,72},{80,88},{88,96},{10... | collective-permute-start | bytes 506888 | tf_op jit(solution)/shard_map/ppermute | solution.py:249
  4.6 15.1 %collective-permute-start.1 = (f32[66,640]{1,0:T(8,128)S(1)}, f32[66,640]{1,0:T(8,128)S(1)}, u32[]{:S(2)}, u32[]{:S(2)}) collective-permute-start(f32[66,640]{1,0:T(8,128)S(1)} %fusion.10), channel_id=1, source_target_pairs={{8,24},{32,48},{56,72},{80,96},{104,120},{128,144},{152,168},{176,... | collective-permute-start | bytes 506888 | tf_op jit(solution)/shard_map/ppermute | solution.py:249
  6.8 18.3 %copy-start.3 = (f32[2,64,640]{2,1,0:T(8,128)S(1)}, f32[2,64,640]{2,1,0:T(8,128)}, u32[]{:S(2)}) copy-start(f32[2,64,640]{2,1,0:T(8,128)} %param.7) | copy-start | bytes 983044
  6.8 2.8 %collective-permute-start.2 = (f32[32,640]{1,0:T(8,128)S(1)}, f32[32,640]{1,0:T(8,128)S(1)}, u32[]{:S(2)}, u32[]{:S(2)}) collective-permute-start(f32[32,640]{1,0:T(8,128)S(1)} %dynamic-slice_bitcast_fusion), channel_id=1, source_target_pairs={{0,8},{24,32},{48,56},{72,80},{96,104},{120,128},{144,152},{168,17... | collective-permute-start | bytes 245768 | tf_op jit(solution)/shard_map/ppermute | solution.py:249
  7.6 2.0 %collective-permute-start.3 = (f32[32,640]{1,0:T(8,128)S(1)}, f32[32,640]{1,0:T(8,128)S(1)}, u32[]{:S(2)}, u32[]{:S(2)}) collective-permute-start(f32[32,640]{1,0:T(8,128)S(1)} %dynamic-slice_bitcast_fusion), channel_id=1, source_target_pairs={{0,16},{24,40},{48,64},{72,88},{96,112},{120,136},{144,160},{168,1... | collective-permute-start | bytes 245768 | tf_op jit(solution)/shard_map/ppermute | solution.py:249
  8.3 11.4 %collective-permute-start.4 = (f32[32,640]{1,0:T(8,128)S(1)}, f32[32,640]{1,0:T(8,128)S(1)}, u32[]{:S(2)}, u32[]{:S(2)}) collective-permute-start(f32[32,640]{1,0:T(8,128)S(1)} %dynamic-slice_bitcast_fusion), channel_id=1, source_target_pairs={{0,24},{24,48},{48,72},{72,96},{96,120},{120,144},{144,168},{168,1... | collective-permute-start | bytes 245768 | tf_op jit(solution)/shard_map/ppermute | solution.py:249
  20.4 3.9 %collective-permute-start.5 = (f32[228,640]{1,0:T(8,128)S(1)}, f32[228,640]{1,0:T(8,128)S(1)}, u32[]{:S(2)}, u32[]{:S(2)}) collective-permute-start(f32[228,640]{1,0:T(8,128)S(1)} %concatenate.53), channel_id=1, source_target_pairs={{0,1},{1,0},{2,3},{3,2},{4,5},{5,4},{6,7},{7,6},{8,9},{9,8},{10,11... | collective-permute-start | bytes 1751048 | tf_op jit(solution)/shard_map/ppermute | solution.py:259
  22.5 2.7 %copy-start.5 = (f32[32]{0:T(128)S(1)}, f32[32]{0:T(128)}, u32[]{:S(2)}) copy-start(f32[32]{0:T(128)} %param.12) | copy-start | bytes 388
  38.5 7.3 %copy-start.2 = (f32[6,640,640]{2,1,0:T(8,128)}, f32[6,640,640]{2,1,0:T(8,128)S(1)}, u32[]{:S(2)}) copy-start(f32[6,640,640]{2,1,0:T(8,128)S(1)} %add_multiply_fusion.refs_0_) | copy-start | bytes 29491204
  45.8 5.0 %copy-start.1 = (f32[3,640,640]{2,1,0:T(8,128)}, f32[3,640,640]{2,1,0:T(8,128)S(1)}, u32[]{:S(2)}) copy-start(f32[3,640,640]{2,1,0:T(8,128)S(1)} %fusion.refs_1_) | copy-start | bytes 14745604
  45.8 4.9 %copy-start.4 = (f32[640]{0:T(1024)S(1)}, f32[640]{0:T(1024)}, u32[]{:S(2)}) copy-start(f32[640]{0:T(1024)} %param.13) | copy-start | bytes 7684

commit v9 on v5

--- a/solution.py
+++ b/solution.py
@@ -9,6 +9,7 @@
 
 MESH = pl.DeviceIdType.MESH
 STRIDE = 3
+HEAD = 10
 
 
 def shifted(block, axis, distance):
@@ -67,53 +68,47 @@
     return jnp.broadcast_to(v, like.shape)
 
 
-def chain_kernel(
-    steps, stride, *refs,
-):
-    n_in = stride + 4
-    hbm = refs[:n_in - 1]
-    start_ref = refs[n_in - 1]
-    out_ref, recv_buf, send_buf, send_sem, recv_sem, load_sem = refs[n_in:n_in + 6]
-    local = refs[n_in + 6:]
+def chain_kernel(steps, stride, head, *refs):
+    weights_hbm, block_hbm, befores_hbm, combined_hbm, prior_ref = refs[:5]
+    out_ref, recv_buf, send_buf, send_sem, recv_sem, load_sem = refs[5:11]
+    local = refs[11:]
     me = lax.axis_index("tm")
     row = lax.axis_index("rows")
     last = steps - 1
-    phase = me % stride
-    node = phase == 0
-
+    offset = me - head
+    phase = jnp.maximum(offset, 0) % stride
+    tail = me > head
+    tail_node = jnp.logical_and(tail, phase == 0)
+    fans = jnp.logical_or(me == head, tail_node)
+
+    sources = [block_hbm, combined_hbm, weights_hbm.at[0], weights_hbm.at[1]]
+    sources += [befores_hbm.at[d] for d in range(stride - 1)]
     loads = [
-        pltpu.make_async_copy(hbm[i], local[i], load_sem.at[i]) for i in range(len(hbm))
+        pltpu.make_async_copy(sources[i], local[i], load_sem.at[i]) for i in range(len(sources))
     ]
     for load in loads:
         load.start()
     block_ref, combined_ref, first_ref, second_ref = local[:4]
     befores = local[4:]
 
+    source_gap = jnp.where(me <= head, 1, jnp.where(phase == 0, stride, phase))
+    sends = jnp.where(me < head, 1, jnp.where(fans, jnp.minimum(last - me, stride), 0))
+
     barrier = pltpu.get_barrier_semaphore()
 
     def greet(other):
         pl.semaphore_signal(barrier, 1, device_id=(other, row), device_id_type=MESH)
 
-    @pl.when(node)
-    def _():
-        for d in range(1, stride + 1):
-            @pl.when(me + d <= last)
-            def _():
-                greet(me + d)
-
-        @pl.when(me >= stride)
+    @pl.when(me > 0)
+    def _():
+        greet(me - source_gap)
+
+    for d in range(1, stride + 1):
+        @pl.when(d <= sends)
         def _():
-            greet(me - stride)
-
-    @pl.when(jnp.logical_not(node))
-    def _():
-        greet(me - phase)
-
-    partners = jnp.where(
-        node,
-        jnp.minimum(last - me, stride) + (me >= stride).astype(jnp.int32),
-        1,
-    )
+            greet(me + d)
+
+    partners = sends + (me > 0).astype(jnp.int32)
     for amount in range(1, stride + 2):
         @pl.when(partners == amount)
         def _():
@@ -134,7 +129,7 @@
     def send_all(v):
         send_buf[...] = v
         for d in range(1, stride + 1):
-            @pl.when(me + d <= last)
+            @pl.when(d <= sends)
             def _():
                 copies[d - 1].start()
 
@@ -143,21 +138,24 @@
 
     @pl.when(me == 0)
     def _():
-        out_ref[...] = start_ref[...]
-        send_all(normalized(vec_mat(start_ref[...], block_ref[...])))
+        out_ref[...] = spread(normalized(prior_ref[0:1, :]), out_ref)
 
     @pl.when(me > 0)
     def _():
         copies[0].wait_recv()
         out_ref[...] = spread(recv_buf[...], out_ref)
 
-    @pl.when(jnp.logical_and(node, me > 0))
+    @pl.when(me <= head)
+    def _():
+        send_all(normalized(vec_mat(out_ref[...], block_ref[...])))
+
+    @pl.when(tail_node)
     def _():
         send_all(normalized(vec_mat(out_ref[...], combined_ref[...])))
 
     for load in loads[4:]:
         load.wait()
-    lag = jnp.where(node, jnp.where(me > 0, stride - 1, 0), phase - 1)
+    lag = jnp.where(tail_node, stride - 1, jnp.where(tail, phase - 1, 0))
     for amount in range(1, stride):
         @pl.when(lag == amount)
         def _():
@@ -176,21 +174,19 @@
         axis=0,
     )
 
-    @pl.when(node)
-    def _():
-        for d in range(1, stride + 1):
-            @pl.when(me + d <= last)
-            def _():
-                copies[d - 1].wait_send()
-
-
-def chain(block, combined, first, second, befores, start, steps, stride):
-    count = block.shape[0]
-    matrices = [block, combined, first, second] + list(befores)
+    for d in range(1, stride + 1):
+        @pl.when(d <= sends)
+        def _():
+            copies[d - 1].wait_send()
+
+
+def chain(weights_own, block, befores, combined, prior, steps, stride, head):
+    count = combined.shape[0]
+    loaded = stride + 3
     return pl.pallas_call(
-        functools.partial(chain_kernel, steps, stride),
+        functools.partial(chain_kernel, steps, stride, head),
         out_shape=jax.ShapeDtypeStruct((8, count), jnp.float32),
-        in_specs=[pl.BlockSpec(memory_space=pl.ANY)] * len(matrices)
+        in_specs=[pl.BlockSpec(memory_space=pl.ANY)] * 4
         + [pl.BlockSpec(memory_space=pltpu.VMEM)],
         out_specs=pl.BlockSpec(memory_space=pltpu.VMEM),
         scratch_shapes=[
@@ -198,13 +194,13 @@
             pltpu.VMEM((1, count), jnp.float32),
             pltpu.SemaphoreType.DMA((stride,)),
             pltpu.SemaphoreType.DMA,
-            pltpu.SemaphoreType.DMA((len(matrices),)),
+            pltpu.SemaphoreType.DMA((loaded,)),
         ]
-        + [pltpu.VMEM((count, count), jnp.float32) for _ in matrices],
+        + [pltpu.VMEM((count, count), jnp.float32) for _ in range(loaded)],
         compiler_params=pltpu.CompilerParams(
             collective_id=0, has_side_effects=True, vmem_limit_bytes=48 * 1024 * 1024
         ),
-    )(*matrices, start)
+    )(weights_own, block, befores, combined, prior)
 
 
 def block_product(matrices):
@@ -222,9 +218,11 @@
     row_start = lax.axis_index("rows") * own_rows
     steps = lax.axis_size("tm")
     stride = STRIDE
+    head = min(HEAD, steps - 1)
     local = states.shape[0]
     dims = states.shape[1]
     tracers = tracer_obs.shape[1]
+    me = lax.axis_index("tm")
 
     count_pad = jnp.zeros((local, count - tracers - 1), jnp.float32)
     extra = jnp.concatenate(
@@ -235,32 +233,102 @@
         axis=1,
     )
     packed = jnp.concatenate([states, extra], axis=1)
-    packs = [packed] + [shifted(packed, "tm", d) for d in range(1, stride)]
-    rims = [pack[-1, :dims, :] for pack in packs[1:]] + [shifted(states[-1], "tm", stride)]
-
-    def matrices_of(rim, pack):
-        block_states = pack[:, :dims, :]
-        parents = pack[:, dims, :].astype(jnp.int32)
-        observed = pack[:, dims + 1, :tracers]
-        mixing = pack[:, dims + 1, tracers]
-        previous = jnp.concatenate([rim[None], block_states[:-1]], axis=0)
-        return [
-            transition(
-                previous[s], block_states[s], parents[s], observed[s], mixing[s],
-                fingerprints, tracer_scale,
-            )
-            for s in range(local)
+
+    def need(k):
+        if k <= head:
+            return 0
+        phase = (k - head) % stride
+        return stride - 1 if phase == 0 else phase - 1
+
+    devices = range(steps)
+
+    def sent(block, distance, wanted):
+        route = [(i - distance, i) for i in devices if i - distance >= 0 and wanted(i)]
+        return lax.ppermute(block, "tm", route)
+
+    rim_own = sent(states[-1], 1, lambda i: True)
+
+    core = lax.axis_index("rows") % 2
+    half_rows = dims // 2
+    packed_half = lax.dynamic_index_in_dim(packed, core, 0, keepdims=False)
+    rim_half = lax.dynamic_slice_in_dim(states[-1], core * half_rows, half_rows, 0)
+    fetched = [sent(packed_half, d, lambda i, d=d: need(i) >= d) for d in range(1, stride)]
+    fetched += [sent(rim_half, e, lambda i, e=e: need(i) + 1 == e) for e in range(2, stride + 1)]
+    bundle = jnp.concatenate(fetched, axis=0)
+    pairs = [(r, r ^ 1) for r in range(lax.axis_size("rows"))]
+    other = lax.ppermute(bundle, "rows", pairs)
+
+    def own_matrices():
+        return jax.vmap(transition, in_axes=(0, 0, 0, 0, 0, None, None))(
+            jnp.stack([rim_own, states[0]]),
+            states,
+            ancestors,
+            tracer_obs,
+            jitter,
+            fingerprints,
+            tracer_scale,
+        )
+
+    weights_own = own_matrices()
+    block_own = block_product([weights_own[0], weights_own[1]])
+
+    def earlier(bundle, other):
+        first_half = jnp.where(core == 0, bundle, other)
+        second_half = jnp.where(core == 0, other, bundle)
+        rows_of = [f.shape[0] for f in fetched]
+        offsets = [sum(rows_of[:i]) for i in range(len(rows_of) + 1)]
+
+        def joined(i):
+            lo, hi = offsets[i], offsets[i + 1]
+            return jnp.concatenate([first_half[lo:hi], second_half[lo:hi]], axis=0)
+
+        packs = [packed] + [joined(i).reshape(packed.shape) for i in range(stride - 1)]
+        rim_parts = [joined(stride - 1 + i) for i in range(stride - 1)]
+        rims = [None] + [
+            (packs[d + 1][-1, :dims, :] if d + 1 < stride else 0.0) + rim_parts[d - 1]
+            for d in range(1, stride)
         ]
-
-    own = matrices_of(rims[0], packs[0])
-    blocks = [block_product(own)] + [
-        block_product(matrices_of(rims[d], packs[d])) for d in range(1, stride)
-    ]
-    combined = block_product(blocks[::-1])
-
-    start = prior_weights / jnp.sum(prior_weights)
-    start8 = jnp.broadcast_to(start[None, :], (8, count))
-    weights = chain(blocks[0], combined, own[0], own[1], blocks[1:], start8, steps, stride)
+        previous = []
+        current = []
+        parents = []
+        observed = []
+        mixing = []
+        for d in range(1, stride):
+            block_states = packs[d][:, :dims, :]
+            previous += [rims[d], block_states[0]]
+            current += [block_states[0], block_states[1]]
+            parents.append(packs[d][:, dims, :])
+            observed.append(packs[d][:, dims + 1, :tracers])
+            mixing.append(packs[d][:, dims + 1, tracers])
+        weights_all = jax.vmap(transition, in_axes=(0, 0, 0, 0, 0, None, None))(
+            jnp.stack(previous),
+            jnp.stack(current),
+            jnp.concatenate(parents).astype(jnp.int32),
+            jnp.concatenate(observed),
+            jnp.concatenate(mixing),
+            fingerprints,
+            tracer_scale,
+        )
+        products = lax.dot_general(
+            weights_all[0::2],
+            weights_all[1::2],
+            (((2,), (1,)), ((0,), (0,))),
+            precision=lax.Precision.HIGH,
+            preferred_element_type=jnp.float32,
+        )
+        combined = block_product([products[d] for d in range(stride - 2, -1, -1)] + [block_own])
+        return products, combined
+
+    def skipped(bundle, other):
+        return (
+            jnp.zeros((stride - 1, count, count), jnp.float32),
+            jnp.zeros((count, count), jnp.float32),
+        )
+
+    befores, combined = lax.cond(me > head, earlier, skipped, bundle, other)
+
+    prior8 = jnp.broadcast_to(prior_weights[None, :], (8, count))
+    weights = chain(weights_own, block_own, befores, combined, prior8, steps, stride, head)
     mine = lax.dynamic_slice_in_dim(weights[:local], row_start, own_rows, 1)
     return count * mine
 

time: 168 us -> 162 us (0.964)
  waiting for transfers between devices: 25.5 us -> 5.99 us
  local copies, waits for them, and re-layouts: 3.68 us -> 15.7 us
  starting transfers between devices: 3.88 us -> 7.12 us
  other arithmetic: 13.1 us -> 10.3 us
  matrix products: 30.4 us -> 32.9 us
  Pallas kernels: 90.3 us -> 88.6 us
    ppermute x3 -> x6, waiting for transfers between devices: 25.5 us -> 5.99 us  [the longest x5 5.99 us: sent(): return lax.ppermute(block, 'tm', route)]
    slice x6 -> x11, local copies, waits for them, and re-layouts: 1.82 us -> 9.42 us  [the longest x3 2.93 us: earlier(): current += [block_states[0], block_states[1]]]
    dot_general x0 -> x1, matrix products: none -> 6.65 us  [earlier(): lax.dot_general(weights_all[0::2], weights_all[1::2], (((2,), (1,)), ((0,...]
    dot_general x5 -> x3, matrix products: 16.8 us -> 11.6 us  [block_product(): jnp.dot(block, matrix, precision=lax.Precision.HIGH, preferred_element_ty...]
    div x4 -> x2, other arithmetic: 3.9 us -> 0.15 us  [transition(): likelihood = likelihood / jnp.max(likelihood)]
    reduce_max x6 -> x2, other arithmetic: 3.87 us -> 0.25 us  [transition(): likelihood = likelihood / jnp.max(likelihood)]
    reshape x0 -> x2, local copies, waits for them, and re-layouts: none -> 3.5 us  [earlier(): joined(i).reshape(packed.shape)]
    ppermute x3 -> x6, starting transfers between devices: 3.88 us -> 7.12 us  [the longest x5 5.21 us: sent(): return lax.ppermute(block, 'tm', route)]
  transfers between devices with their start and end apart: 3 -> 6, of which waited for: 1 -> 1; matrix products, arithmetic and copies ran while one was open for 6% -> 9% of each run, Pallas kernels for 0% -> 0%
where the time goes in v9:
time: 162 us; the launch traced here: 161 us
  Pallas kernels  88.6 us (55%)
  matrix products  32.9 us (20%)
  local copies, waits for them, and re-layouts  15.7 us (10%)
  other arithmetic  10.3 us (6%)
  starting transfers between devices  7.12 us (4%)
  waiting for transfers between devices  5.99 us (4%)
    pallas_call x1, Pallas kernels, chain(): pl.pallas_call(functools.partial(chain_kernel, steps, stride, head), out_...  88.6 us
    dot_general x2, matrix products, transition(): lax.dot_general(previous, current, (((0,), (0,)), ((), ())), precision=hi...  12.9 us
    dot_general x3, matrix products, block_product(): jnp.dot(block, matrix, precision=lax.Precision.HIGH, preferred_element_ty...  11.6 us
    dot_general x1, matrix products, earlier(): lax.dot_general(weights_all[0::2], weights_all[1::2], (((2,), (1,)), ((0,...  6.65 us
    ppermute x5, waiting for transfers between devices, sent(): return lax.ppermute(block, 'tm', route)  5.99 us
    ppermute x5, starting transfers between devices, sent(): return lax.ppermute(block, 'tm', route)  5.21 us
    reshape x2, local copies, waits for them, and re-layouts, earlier(): joined(i).reshape(packed.shape)  3.5 us
  transfers between devices with their start and end apart: 6, of which 1 were waited for; matrix products, arithmetic and copies ran while one was open for 9% of the time, Pallas kernels for 0%

profile of v9, /device:TPU:504, one launch (start us, length us, event | category | flops | bytes accessed | tf_op | source)
XLA Modules:
  0.0 161.1 jit_solution(8164808151177531134)
XLA Ops:
  0.0 1.1 fusion.27
  1.1 1.3 collective-permute-start.3
  2.4 0.7 collective-permute-start.4
  3.1 0.7 copy.12
  3.8 0.1 pad.29.clone
  3.9 0.8 maximum_bitcast_fusion.1
  4.7 0.7 convert_bitcast_fusion
  5.4 0.9 fusion.19
  6.3 1.3 collective-permute-start.1
  7.6 0.7 collective-permute-start.2
  8.3 1.3 collective-permute-start
  9.6 1.3 fusion.16
  10.9 0.1 fusion.22
  11.0 0.1 fusion.21
  11.1 1.0 multiply_reduce_fusion.2
  12.1 6.0 %collective-permute-done = f32[64,640]{1,0:T(8,128)S(1)} collective-permute-done((f32[64,640]{1,0:T(8,128)S(1)}, f32[64,640]{1,0:T(8,128)S(1)}, u32[]{:S(2)}, u32[]{:S(2)}) %collective-permute-start) | collective-permute-done | bytes 163872 | tf_op jit(solution)/shard_map/ppermute | solution.py:247
  18.1 0.0 collective-permute-done.3
  18.1 0.0 collective-permute-done.4
  18.2 0.0 collective-permute-done.1
  18.2 0.0 collective-permute-done.2
  18.2 0.8 pad_maximum_fusion.9
  19.0 1.9 %collective-permute-start.5 = (f32[196,640]{1,0:T(8,128)}, f32[196,640]{1,0:T(8,128)}, u32[]{:S(2)}, u32[]{:S(2)}) collective-permute-start(f32[196,640]{1,0:T(8,128)} %pad_maximum_fusion.9), channel_id=1, source_target_pairs={{0,1},{1,0},{2,3},{3,2},{4,5},{5,4},{6,7},{7,6},{8,9},{9,8},{10,11... | collective-permute-start | bytes 1505288 | tf_op jit(solution)/shard_map/ppermute | solution.py:259
  20.9 0.0 copy-done.8
  21.0 0.0 copy-done.5
  21.0 5.0 %add_multiply_fusion.1.refs_0_ = f32[2,640,640]{2,1,0:T(8,128)S(1)} fusion(f32[2,64,640]{2,1,0:T(8,128)} %param.9, f32[2,640]{1,0:T(2,128)S(1)} %multiply_reduce_fusion.2, f32[2,640]{1,0:T(2,128)S(1)} %multiply_reduce_fusion.3, f32[2]{0:T(128)S(1)} %copy-done.8, s32[2,640]{1,0:T(2,128)S(1)} %copy-done.5, f32[2,640]{1,0:T(2,128)S(1)} %fusion.21, ...), kind=kOutput, calls=%fused_computation.37 | convolution fusion | flops 636600320 | bytes 3952648 | tf_op jit(solution)/shard_map/vmap()/dot_general | solution.py:24
  25.9 0.0 copy-start.4
  25.9 0.0 copy-start.7
  26.0 3.5 %fusion.12.refs_1_ = f32[640,640]{1,0:T(8,128)} fusion(f32[2,640,640]{2,1,0:T(8,128)S(1)} %add_multiply_fusion.1.refs_0_), kind=kOutput, calls=%fused_computation.40 | convolution fusion | flops 1572864000 | bytes 4915200 | tf_op jit(solution)/shard_map/dot_general | solution.py:209
  29.5 0.0 collective-permute-done.5
  29.5 0.0 copy-done.7
  29.5 0.0 copy-start.6
  29.5 42.4 %conditional.1 = (f32[2,640,640]{2,1,0:T(8,128)}, f32[640,640]{1,0:T(8,128)}) conditional(s32[]{:T(128)} %convert_element_type.20, () %tuple.13, (f32[32]{0:T(128)S(1)}, s32[]{:T(128)}, f32[196,640]{1,0:T(8,128)}, f32[196,640]{1,0:T(8,128)}, f32[64,32]{0,1:T(8,128)S(1)}, /*index=5*/f32[640,640]{1,0:T(8,128)}) %tuple.30), branch_computations={%region_4.5_spmd, %region_5.10_spmd} | conditional | flops 7630415360 | bytes 49736540 | solution.py:328
  29.7 1.3 broadcast_select_fusion.1
  31.0 0.0 copy-start.1
  31.0 0.0 copy-start.2
  31.0 0.8 copy-done.1
  31.8 0.7 fusion.25
  32.5 0.7 pad_maximum_fusion.5
  33.3 1.8 %reshape.66 = f32[2,66,640]{2,1,0:T(8,128)} reshape(f32[132,640]{1,0:T(8,128)} %pad_maximum_fusion.5) | data formatting | bytes 675840 | tf_op jit(solution)/shard_map/cond/branch_1_fun/reshape | solution.py:285
  35.1 0.7 slice.102
  35.8 1.7 %pad_maximum_fusion.6 = f32[132,640]{1,0:T(8,128)} fusion(f32[66,640]{1,0:T(8,128)} %get-tuple-element.41, f32[66,640]{1,0:T(8,128)S(1)} %get-tuple-element.34), kind=kLoop, calls=%fused_computation.17 | loop fusion | flops 84480 | bytes 675840 | tf_op jit(solution)/shard_map/cond/branch_1_fun/concatenate | solution.py:283
  37.4 1.7 %reshape.67 = f32[2,66,640]{2,1,0:T(8,128)} reshape(f32[132,640]{1,0:T(8,128)} %pad_maximum_fusion.6) | data formatting | bytes 675840 | tf_op jit(solution)/shard_map/cond/branch_1_fun/reshape | solution.py:285
  39.2 0.7 slice.105
  39.9 1.0 slice.106
  40.9 1.0 slice.107
  41.9 0.5 fusion.6
  42.4 0.1 fusion.9
  42.5 0.1 fusion.8
  42.6 1.1 slice_bitcast_fusion.4
  43.7 1.0 slice_add_fusion
  44.7 0.9 slice.115
  45.7 0.1 multiply_reduce_fusion.1
  45.8 0.1 multiply_reduce_fusion
  45.8 0.8 slice.108
  46.6 0.8 slice.109
  47.4 0.9 slice_reduce_fusion.1
  48.3 0.9 slice_reduce_fusion
  49.2 0.1 pad_maximum_fusion.8
  49.2 7.9 %add_multiply_fusion = f32[4,640,640]{2,1,0:T(8,128)S(1)} fusion(f32[4,640]{1,0:T(4,128)S(1)} %multiply_reduce_fusion, f32[4,640]{1,0:T(4,128)S(1)} %multiply_reduce_fusion.1, f32[4]{0:T(128)S(1)} %pad_maximum_fusion.8, s32[4,640]{1,0:T(4,128)S(1)} %maximum_convert_fusion, f32[4,640]{1,0:T(4,128)S(1)} %fusion.8, f32[2,64,640]{2,1,0:T(8,128)S(1)} %slice.107, ...), kind=kOutput, calls=%fused_computation | convolution fusion | flops 1273692160 | bytes 7905296 | tf_op jit(solution)/shard_map/cond/branch_1_fun/vmap()/dot_general | solution.py:24
  57.1 6.7 %fusion = f32[2,640,640]{2,1,0:T(8,128)} fusion(f32[4,640,640]{2,1,0:T(8,128)S(1)} %add_multiply_fusion), kind=kOutput, calls=%fused_computation.2 | convolution fusion | flops 3145728000 | bytes 9830400 | tf_op jit(solution)/shard_map/cond/branch_1_fun/dot_general | solution.py:312
  63.8 4.5 %fusion.3 = f32[640,640]{1,0:T(8,128)S(1)} fusion(f32[2,640,640]{2,1,0:T(8,128)} %fusion), kind=kOutput, calls=%fused_computation.6 | convolution fusion | flops 1572864000 | bytes 4915200 | tf_op jit(solution)/shard_map/cond/branch_1_fun/dot_general | solution.py:209
  68.3 3.6 %fusion.28 = f32[640,640]{1,0:T(8,128)} fusion(f32[640,640]{1,0:T(8,128)S(1)} %fusion.3, f32[640,640]{1,0:T(8,128)S(1)} %copy-done), kind=kOutput, calls=%fused_computation.71 | convolution fusion | flops 1572864000 | bytes 4915200 | tf_op jit(solution)/shard_map/cond/branch_1_fun/dot_general | solution.py:209
  71.9 88.6 %shard_map.73 = f32[8,640]{1,0:T(8,128)S(1)} custom-call(f32[2,640,640]{2,1,0:T(8,128)S(1)} %add_multiply_fusion.1.refs_0_, f32[640,640]{1,0:T(8,128)} %fusion.12.refs_1_, f32[2,640,640]{2,1,0:T(8,128)} %get-tuple-element.25.refs_2_, f32[640,640]{1,0:T(8,128)} %get-tuple-element.26.refs_3_, f32[8,640]{1,0:T(8,128)S(1)} %broadcast_in_dim.14.refs_4_), custom_call_target="tpu_custom_call" | custom-call | tf_op jit(solution)/shard_map/pallas_call | solution.py:186
  160.5 0.6 fusion.23
  (21 shorter events, 0.1 us)
Async XLA Ops:
  0.0 20.9 %copy-start.8 = (f32[2]{0:T(128)S(1)}, f32[2]{0:T(128)}, u32[]{:S(2)}) copy-start(f32[2]{0:T(128)} %param.12) | copy-start | bytes 28
  0.0 21.0 %copy-start.5 = (s32[2,640]{1,0:T(2,128)S(1)}, s32[2,640]{1,0:T(2,128)}, u32[]{:S(2)}) copy-start(s32[2,640]{1,0:T(2,128)} %param.10) | copy-start | bytes 15364
  1.1 17.1 %collective-permute-start.3 = (f32[32,640]{1,0:T(8,128)S(1)}, f32[32,640]{1,0:T(8,128)S(1)}, u32[]{:S(2)}, u32[]{:S(2)}) collective-permute-start(f32[32,640]{1,0:T(8,128)S(1)} %dynamic-slice_bitcast_fusion), channel_id=1, source_target_pairs={{80,96},{104,120},{128,144},{152,168},{176,192},{200,216},{224,240... | collective-permute-start | bytes 245768 | tf_op jit(solution)/shard_map/ppermute | solution.py:247
  2.4 15.8 %collective-permute-start.4 = (f32[32,640]{1,0:T(8,128)S(1)}, f32[32,640]{1,0:T(8,128)S(1)}, u32[]{:S(2)}, u32[]{:S(2)}) collective-permute-start(f32[32,640]{1,0:T(8,128)S(1)} %dynamic-slice_bitcast_fusion), channel_id=1, source_target_pairs={{80,104},{104,128},{128,152},{152,176},{176,200},{200,224},{224,24... | collective-permute-start | bytes 245768 | tf_op jit(solution)/shard_map/ppermute | solution.py:247
  6.3 11.9 %collective-permute-start.1 = (f32[66,640]{1,0:T(8,128)S(1)}, f32[66,640]{1,0:T(8,128)S(1)}, u32[]{:S(2)}, u32[]{:S(2)}) collective-permute-start(f32[66,640]{1,0:T(8,128)S(1)} %fusion.19), channel_id=1, source_target_pairs={{88,96},{96,104},{112,120},{120,128},{136,144},{144,152},{160,168}... | collective-permute-start | bytes 506888 | tf_op jit(solution)/shard_map/ppermute | solution.py:247
  7.6 10.6 %collective-permute-start.2 = (f32[66,640]{1,0:T(8,128)S(1)}, f32[66,640]{1,0:T(8,128)S(1)}, u32[]{:S(2)}, u32[]{:S(2)}) collective-permute-start(f32[66,640]{1,0:T(8,128)S(1)} %fusion.19), channel_id=1, source_target_pairs={{88,104},{112,128},{136,152},{160,176},{184,200},{208,224},{232,24... | collective-permute-start | bytes 506888 | tf_op jit(solution)/shard_map/ppermute | solution.py:247
  8.3 9.8 %collective-permute-start = (f32[64,640]{1,0:T(8,128)S(1)}, f32[64,640]{1,0:T(8,128)S(1)}, u32[]{:S(2)}, u32[]{:S(2)}) collective-permute-start(f32[64,640]{1,0:T(8,128)S(1)} %get-tuple-element.44), channel_id=1, source_target_pairs={{0,8},{8,16},{16,24},{24,32},{32,40},{40,48},{48,56},{56,64},{64,7... | collective-permute-start | bytes 491528 | tf_op jit(solution)/shard_map/ppermute | solution.py:247
  18.1 0.9 copy-start.3
  19.0 10.4 %collective-permute-start.5 = (f32[196,640]{1,0:T(8,128)}, f32[196,640]{1,0:T(8,128)}, u32[]{:S(2)}, u32[]{:S(2)}) collective-permute-start(f32[196,640]{1,0:T(8,128)} %pad_maximum_fusion.9), channel_id=1, source_target_pairs={{0,1},{1,0},{2,3},{3,2},{4,5},{5,4},{6,7},{7,6},{8,9},{9,8},{10,11... | collective-permute-start | bytes 1505288 | tf_op jit(solution)/shard_map/ppermute | solution.py:259
  25.9 3.5 %copy-start.4 = (f32[64,32]{0,1:T(8,128)S(1)}, f32[64,32]{0,1:T(8,128)}, u32[]{:S(2)}) copy-start(f32[64,32]{0,1:T(8,128)} %param.13) | copy-start | bytes 24580
  25.9 3.5 %copy-start.7 = (f32[32]{0:T(128)S(1)}, f32[32]{0:T(128)}, u32[]{:S(2)}) copy-start(f32[32]{0:T(128)} %param.14) | copy-start | bytes 388
  29.5 42.4 %copy-start.6 = (f32[640]{0:T(1024)S(1)}, f32[640]{0:T(1024)}, u32[]{:S(2)}) copy-start(f32[640]{0:T(1024)} %param.15) | copy-start | bytes 7684
  31.0 0.8 copy-start.1
  31.0 1.6 copy-start.2
  63.8 4.5 %copy-start = (f32[640,640]{1,0:T(8,128)S(1)}, f32[640,640]{1,0:T(8,128)}, u32[]{:S(2)}) copy-start(f32[640,640]{1,0:T(8,128)} %get-tuple-element.22) | copy-start | bytes 4915204 | tf_op jit(solution)/shard_map/cond

commit v10 on v9

--- a/solution.py
+++ b/solution.py
@@ -9,7 +9,7 @@
 
 MESH = pl.DeviceIdType.MESH
 STRIDE = 3
-HEAD = 10
+HEAD = 13
 
 
 def shifted(block, axis, distance):
@@ -229,6 +229,7 @@
         [
             ancestors.astype(jnp.float32)[:, None, :],
             jnp.concatenate([tracer_obs, jitter[:, None], count_pad], axis=1)[:, None, :],
+            jnp.zeros((local, 6, count), jnp.float32),
         ],
         axis=1,
     )

time: 162 us -> 143 us (0.88)
  local copies, waits for them, and re-layouts: 15.7 us -> 5.22 us
  other arithmetic: 10.3 us -> 6.2 us
  Pallas kernels: 88.6 us -> 85.6 us
    reshape x2 -> x0, local copies, waits for them, and re-layouts: 3.5 us -> none  [earlier(): joined(i).reshape(packed.shape)]
    pallas_call x1, Pallas kernels: 88.6 us -> 85.6 us  [chain(): pl.pallas_call(functools.partial(chain_kernel, steps, stride, head), out_...]
    slice x3, local copies, waits for them, and re-layouts: 2.93 us -> 0.06 us  [earlier(): current += [block_states[0], block_states[1]]]
    concatenate x2, other arithmetic: 2.42 us -> 0.06 us  [joined(): return jnp.concatenate([first_half[lo:hi], second_half[lo:hi]], axis=0)]
    unnamed x12 -> x15, local copies, waits for them, and re-layouts: 0.03 us -> 2.05 us
  transfers between devices with their start and end apart: 6 -> 6, of which waited for: 1 -> 1; matrix products, arithmetic and copies ran while one was open for 9% -> 10% of each run, Pallas kernels for 0% -> 0%
where the time goes in v10:
time: 143 us; the launch traced here: 142 us
  Pallas kernels  85.6 us (60%)
  matrix products  32.9 us (23%)
  starting transfers between devices  7.12 us (5%)
  other arithmetic  6.2 us (4%)
  local copies, waits for them, and re-layouts  5.22 us (4%)
  waiting for transfers between devices  4.9 us (3%)
    pallas_call x1, Pallas kernels, chain(): pl.pallas_call(functools.partial(chain_kernel, steps, stride, head), out_...  85.6 us
    dot_general x2, matrix products, transition(): lax.dot_general(previous, current, (((0,), (0,)), ((), ())), precision=hi...  12.9 us
    dot_general x3, matrix products, block_product(): jnp.dot(block, matrix, precision=lax.Precision.HIGH, preferred_element_ty...  11.6 us
    dot_general x1, matrix products, earlier(): lax.dot_general(weights_all[0::2], weights_all[1::2], (((2,), (1,)), ((0,...  6.65 us
    ppermute x5, starting transfers between devices, sent(): return lax.ppermute(block, 'tm', route)  5.21 us
    ppermute x5, waiting for transfers between devices, sent(): return lax.ppermute(block, 'tm', route)  4.9 us
  transfers between devices with their start and end apart: 6, of which 1 were waited for; matrix products, arithmetic and copies ran while one was open for 10% of the time, Pallas kernels for 0%

profile of v10, /device:TPU:504, one launch (start us, length us, event | category | flops | bytes accessed | tf_op | source)
XLA Modules:
  0.0 142.5 jit_solution(7381405392737183732)
XLA Ops:
  0.0 0.0 copy-start.6
  0.0 0.0 copy-start.3
  0.0 0.8 copy.12
  0.8 0.1 pad.26.clone
  0.9 0.8 maximum_bitcast_fusion.1
  1.7 0.7 convert_bitcast_fusion
  2.4 0.1 pad.23.clone
  2.4 1.0 fusion.20
  3.4 1.3 collective-permute-start.1
  4.7 0.7 collective-permute-start.2
  5.4 1.0 fusion.28
  6.5 1.3 collective-permute-start.3
  7.8 0.7 collective-permute-start.4
  8.5 1.3 collective-permute-start
  9.8 1.3 fusion.16
  11.1 0.1 fusion.23
  11.2 0.1 fusion.22
  11.3 1.0 multiply_reduce_fusion.2
  12.3 4.9 %collective-permute-done = f32[64,640]{1,0:T(8,128)S(1)} collective-permute-done((f32[64,640]{1,0:T(8,128)S(1)}, f32[64,640]{1,0:T(8,128)S(1)}, u32[]{:S(2)}, u32[]{:S(2)}) %collective-permute-start) | collective-permute-done | bytes 163872 | tf_op jit(solution)/shard_map/ppermute | solution.py:248
  17.2 0.0 copy-start.1
  17.2 0.0 collective-permute-done.1
  17.2 0.7 constant_dynamic-update-slice_fusion.3
  17.9 0.0 collective-permute-done.2
  17.9 0.7 constant_dynamic-update-slice_fusion.2
  18.6 0.0 collective-permute-done.3
  18.6 0.6 constant_dynamic-update-slice_fusion.1
  19.3 0.0 collective-permute-done.4
  19.3 0.6 constant_dynamic-update-slice_fusion
  19.9 0.0 copy-done.1
  19.9 1.9 %collective-permute-start.5 = (f32[208,640]{1,0:T(8,128)}, f32[208,640]{1,0:T(8,128)}, u32[]{:S(2)}, u32[]{:S(2)}) collective-permute-start(f32[208,640]{1,0:T(8,128)} %constant_dynamic-update-slice_fusion), channel_id=1, source_target_pairs={{0,1},{1,0},{2,3},{3,2},{4,5},{5,4},{6,7},{7,6},{8,9},{9,8},{10,11... | collective-permute-start | bytes 1597448 | tf_op jit(solution)/shard_map/ppermute | solution.py:260
  21.8 0.0 copy-done.6
  21.8 0.0 copy-done.3
  21.8 5.0 %add_multiply_fusion.1.refs_0_ = f32[2,640,640]{2,1,0:T(8,128)S(1)} fusion(f32[2,64,640]{2,1,0:T(8,128)} %param.9, f32[2,640]{1,0:T(2,128)S(1)} %multiply_reduce_fusion.2, f32[2,640]{1,0:T(2,128)S(1)} %multiply_reduce_fusion.3, f32[2]{0:T(128)S(1)} %copy-done.6, s32[2,640]{1,0:T(2,128)S(1)} %copy-done.3, f32[2,640]{1,0:T(2,128)S(1)} %fusion.22, ...), kind=kOutput, calls=%fused_computation.37 | convolution fusion | flops 636600320 | bytes 3952648 | tf_op jit(solution)/shard_map/vmap()/dot_general | solution.py:24
  26.8 0.0 copy-start.2
  26.8 0.0 copy-start.5
  26.8 3.5 %fusion.12.refs_1_ = f32[640,640]{1,0:T(8,128)} fusion(f32[2,640,640]{2,1,0:T(8,128)S(1)} %add_multiply_fusion.1.refs_0_), kind=kOutput, calls=%fused_computation.40 | convolution fusion | flops 1572864000 | bytes 4915200 | tf_op jit(solution)/shard_map/dot_general | solution.py:209
  30.4 0.0 collective-permute-done.5
  30.4 0.0 copy-done.2
  30.4 0.0 copy-done.5
  30.4 0.0 copy-start.4
  30.4 25.9 %conditional.1 = (f32[2,640,640]{2,1,0:T(8,128)}, f32[640,640]{1,0:T(8,128)}) conditional(s32[]{:T(128)} %convert_element_type.20, () %tuple.13, (f32[32]{0:T(128)S(1)}, s32[]{:T(128)}, f32[208,640]{1,0:T(8,128)}, f32[208,640]{1,0:T(8,128)}, f32[64,32]{0,1:T(8,128)S(1)}, /*index=5*/f32[640,640]{1,0:T(8,128)}) %tuple.30), branch_computations={%region_4.5_spmd, %region_5.10_spmd} | conditional | flops 7630446080 | bytes 44739368 | solution.py:329
  30.6 1.3 broadcast_select_fusion.1
  31.9 0.1 fusion.26
  32.1 0.5 fusion.6
  32.6 0.1 fusion.9
  32.8 0.1 fusion.8
  33.0 0.1 multiply_reduce_fusion.1
  33.0 0.1 multiply_reduce_fusion
  33.2 0.2 slice_reduce_fusion.1
  33.3 0.2 slice_reduce_fusion
  33.5 0.1 pad_maximum_fusion.8
  33.6 7.9 %add_multiply_fusion = f32[4,640,640]{2,1,0:T(8,128)S(1)} fusion(f32[4,640]{1,0:T(4,128)S(1)} %multiply_reduce_fusion, f32[4,640]{1,0:T(4,128)S(1)} %multiply_reduce_fusion.1, f32[4]{0:T(128)S(1)} %pad_maximum_fusion.8, s32[4,640]{1,0:T(4,128)S(1)} %maximum_convert_fusion, f32[4,640]{1,0:T(4,128)S(1)} %fusion.8, f32[2,64,640]{2,1,0:T(8,128)S(1)} %slice.107, ...), kind=kOutput, calls=%fused_computation | convolution fusion | flops 1273692160 | bytes 7905296 | tf_op jit(solution)/shard_map/cond/branch_1_fun/vmap()/dot_general | solution.py:24
  41.5 6.6 %fusion = f32[2,640,640]{2,1,0:T(8,128)} fusion(f32[4,640,640]{2,1,0:T(8,128)S(1)} %add_multiply_fusion), kind=kOutput, calls=%fused_computation.2 | convolution fusion | flops 3145728000 | bytes 9830400 | tf_op jit(solution)/shard_map/cond/branch_1_fun/dot_general | solution.py:313
  48.1 0.0 copy-start
  48.1 4.5 %fusion.3 = f32[640,640]{1,0:T(8,128)S(1)} fusion(f32[2,640,640]{2,1,0:T(8,128)} %fusion), kind=kOutput, calls=%fused_computation.6 | convolution fusion | flops 1572864000 | bytes 4915200 | tf_op jit(solution)/shard_map/cond/branch_1_fun/dot_general | solution.py:209
  52.6 0.0 copy-done
  52.6 3.6 %fusion.29 = f32[640,640]{1,0:T(8,128)} fusion(f32[640,640]{1,0:T(8,128)S(1)} %fusion.3, f32[640,640]{1,0:T(8,128)S(1)} %copy-done), kind=kOutput, calls=%fused_computation.75 | convolution fusion | flops 1572864000 | bytes 4915200 | tf_op jit(solution)/shard_map/cond/branch_1_fun/dot_general | solution.py:209
  56.2 0.0 copy-done.4
  56.2 85.6 %shard_map.73 = f32[8,640]{1,0:T(8,128)S(1)} custom-call(f32[2,640,640]{2,1,0:T(8,128)S(1)} %add_multiply_fusion.1.refs_0_, f32[640,640]{1,0:T(8,128)} %fusion.12.refs_1_, f32[2,640,640]{2,1,0:T(8,128)} %get-tuple-element.25.refs_2_, f32[640,640]{1,0:T(8,128)} %get-tuple-element.26.refs_3_, f32[8,640]{1,0:T(8,128)S(1)} %broadcast_in_dim.17.refs_4_), custom_call_target="tpu_custom_call" | custom-call | tf_op jit(solution)/shard_map/pallas_call | solution.py:186
  141.8 0.6 fusion.24
  (24 shorter events, 0.3 us)
Async XLA Ops:
  0.0 21.8 %copy-start.6 = (f32[2]{0:T(128)S(1)}, f32[2]{0:T(128)}, u32[]{:S(2)}) copy-start(f32[2]{0:T(128)} %param.12) | copy-start | bytes 28
  0.0 21.8 %copy-start.3 = (s32[2,640]{1,0:T(2,128)S(1)}, s32[2,640]{1,0:T(2,128)}, u32[]{:S(2)}) copy-start(s32[2,640]{1,0:T(2,128)} %param.10) | copy-start | bytes 15364
  3.4 13.8 %collective-permute-start.1 = (f32[72,640]{1,0:T(8,128)S(1)}, f32[72,640]{1,0:T(8,128)S(1)}, u32[]{:S(2)}, u32[]{:S(2)}) collective-permute-start(f32[72,640]{1,0:T(8,128)S(1)} %fusion.20), channel_id=1, source_target_pairs={{112,120},{120,128},{136,144},{144,152},{160,168},{168,176},{184,1... | collective-permute-start | bytes 552968 | tf_op jit(solution)/shard_map/ppermute | solution.py:248
  4.7 13.2 %collective-permute-start.2 = (f32[72,640]{1,0:T(8,128)S(1)}, f32[72,640]{1,0:T(8,128)S(1)}, u32[]{:S(2)}, u32[]{:S(2)}) collective-permute-start(f32[72,640]{1,0:T(8,128)S(1)} %fusion.20), channel_id=1, source_target_pairs={{112,128},{136,152},{160,176},{184,200},{208,224},{232,248},{256,2... | collective-permute-start | bytes 552968 | tf_op jit(solution)/shard_map/ppermute | solution.py:248
  6.5 12.1 %collective-permute-start.3 = (f32[32,640]{1,0:T(8,128)S(1)}, f32[32,640]{1,0:T(8,128)S(1)}, u32[]{:S(2)}, u32[]{:S(2)}) collective-permute-start(f32[32,640]{1,0:T(8,128)S(1)} %dynamic-slice_bitcast_fusion), channel_id=1, source_target_pairs={{104,120},{128,144},{152,168},{176,192},{200,216},{224,240},{248,2... | collective-permute-start | bytes 245768 | tf_op jit(solution)/shard_map/ppermute | solution.py:248
  7.8 11.5 %collective-permute-start.4 = (f32[32,640]{1,0:T(8,128)S(1)}, f32[32,640]{1,0:T(8,128)S(1)}, u32[]{:S(2)}, u32[]{:S(2)}) collective-permute-start(f32[32,640]{1,0:T(8,128)S(1)} %dynamic-slice_bitcast_fusion), channel_id=1, source_target_pairs={{104,128},{128,152},{152,176},{176,200},{200,224},{224,248},{248,2... | collective-permute-start | bytes 245768 | tf_op jit(solution)/shard_map/ppermute | solution.py:248
  8.5 8.7 %collective-permute-start = (f32[64,640]{1,0:T(8,128)S(1)}, f32[64,640]{1,0:T(8,128)S(1)}, u32[]{:S(2)}, u32[]{:S(2)}) collective-permute-start(f32[64,640]{1,0:T(8,128)S(1)} %get-tuple-element.44), channel_id=1, source_target_pairs={{0,8},{8,16},{16,24},{24,32},{32,40},{40,48},{48,56},{56,64},{64,7... | collective-permute-start | bytes 491528 | tf_op jit(solution)/shard_map/ppermute | solution.py:248
  17.2 2.7 %copy-start.1 = (f32[64,640]{1,0:T(8,128)}, f32[64,640]{1,0:T(8,128)S(1)}, u32[]{:S(2)}) copy-start(f32[64,640]{1,0:T(8,128)S(1)} %collective-permute-done) | copy-start | bytes 491524
  19.9 10.5 %collective-permute-start.5 = (f32[208,640]{1,0:T(8,128)}, f32[208,640]{1,0:T(8,128)}, u32[]{:S(2)}, u32[]{:S(2)}) collective-permute-start(f32[208,640]{1,0:T(8,128)} %constant_dynamic-update-slice_fusion), channel_id=1, source_target_pairs={{0,1},{1,0},{2,3},{3,2},{4,5},{5,4},{6,7},{7,6},{8,9},{9,8},{10,11... | collective-permute-start | bytes 1597448 | tf_op jit(solution)/shard_map/ppermute | solution.py:260
  26.8 3.5 %copy-start.2 = (f32[64,32]{0,1:T(8,128)S(1)}, f32[64,32]{0,1:T(8,128)}, u32[]{:S(2)}) copy-start(f32[64,32]{0,1:T(8,128)} %param.13) | copy-start | bytes 24580
  26.8 3.5 %copy-start.5 = (f32[32]{0:T(128)S(1)}, f32[32]{0:T(128)}, u32[]{:S(2)}) copy-start(f32[32]{0:T(128)} %param.14) | copy-start | bytes 388
  30.4 25.9 %copy-start.4 = (f32[640]{0:T(1024)S(1)}, f32[640]{0:T(1024)}, u32[]{:S(2)}) copy-start(f32[640]{0:T(1024)} %param.15) | copy-start | bytes 7684
  48.1 4.5 %copy-start = (f32[640,640]{1,0:T(8,128)S(1)}, f32[640,640]{1,0:T(8,128)}, u32[]{:S(2)}) copy-start(f32[640,640]{1,0:T(8,128)} %get-tuple-element.22) | copy-start | bytes 4915204 | tf_op jit(solution)/shard_map/cond

commit v11 on v10

--- a/solution.py
+++ b/solution.py
@@ -259,21 +259,18 @@
     pairs = [(r, r ^ 1) for r in range(lax.axis_size("rows"))]
     other = lax.ppermute(bundle, "rows", pairs)
 
-    def own_matrices():
+    def batched(previous, current, parents, observed, mixing):
         return jax.vmap(transition, in_axes=(0, 0, 0, 0, 0, None, None))(
-            jnp.stack([rim_own, states[0]]),
-            states,
-            ancestors,
-            tracer_obs,
-            jitter,
+            jnp.stack(previous),
+            jnp.stack(current),
+            jnp.concatenate(parents).astype(jnp.int32),
+            jnp.concatenate(observed),
+            jnp.concatenate(mixing),
             fingerprints,
             tracer_scale,
         )
 
-    weights_own = own_matrices()
-    block_own = block_product([weights_own[0], weights_own[1]])
-
-    def earlier(bundle, other):
+    def earlier(bundle, other, rim_own):
         first_half = jnp.where(core == 0, bundle, other)
         second_half = jnp.where(core == 0, other, bundle)
         rows_of = [f.shape[0] for f in fetched]
@@ -285,7 +282,7 @@
 
         packs = [packed] + [joined(i).reshape(packed.shape) for i in range(stride - 1)]
         rim_parts = [joined(stride - 1 + i) for i in range(stride - 1)]
-        rims = [None] + [
+        rims = [rim_own] + [
             (packs[d + 1][-1, :dims, :] if d + 1 < stride else 0.0) + rim_parts[d - 1]
             for d in range(1, stride)
         ]
@@ -294,22 +291,14 @@
         parents = []
         observed = []
         mixing = []
-        for d in range(1, stride):
+        for d in range(stride):
             block_states = packs[d][:, :dims, :]
             previous += [rims[d], block_states[0]]
             current += [block_states[0], block_states[1]]
             parents.append(packs[d][:, dims, :])
             observed.append(packs[d][:, dims + 1, :tracers])
             mixing.append(packs[d][:, dims + 1, tracers])
-        weights_all = jax.vmap(transition, in_axes=(0, 0, 0, 0, 0, None, None))(
-            jnp.stack(previous),
-            jnp.stack(current),
-            jnp.concatenate(parents).astype(jnp.int32),
-            jnp.concatenate(observed),
-            jnp.concatenate(mixing),
-            fingerprints,
-            tracer_scale,
-        )
+        weights_all = batched(previous, current, parents, observed, mixing)
         products = lax.dot_general(
             weights_all[0::2],
             weights_all[1::2],
@@ -317,16 +306,27 @@
             precision=lax.Precision.HIGH,
             preferred_element_type=jnp.float32,
         )
-        combined = block_product([products[d] for d in range(stride - 2, -1, -1)] + [block_own])
-        return products, combined
-
-    def skipped(bundle, other):
+        combined = block_product([products[d] for d in range(stride - 1, -1, -1)])
+        return weights_all[0:2], products[0], products[1:], combined
+
+    def own_only(bundle, other, rim_own):
+        weights_own = batched(
+            [rim_own, states[0]],
+            [states[0], states[1]],
+            [ancestors],
+            [tracer_obs],
+            [jitter],
+        )
         return (
+            weights_own,
+            block_product([weights_own[0], weights_own[1]]),
             jnp.zeros((stride - 1, count, count), jnp.float32),
             jnp.zeros((count, count), jnp.float32),
         )
 
-    befores, combined = lax.cond(me > head, earlier, skipped, bundle, other)
+    weights_own, block_own, befores, combined = lax.cond(
+        me > head, earlier, own_only, bundle, other, rim_own
+    )
 
     prior8 = jnp.broadcast_to(prior_weights[None, :], (8, count))
     weights = chain(weights_own, block_own, befores, combined, prior8, steps, stride, head)

time: 143 us -> 148 us (1.035)
  waiting for transfers between devices: 4.9 us -> 11.1 us
  matrix products: 32.9 us -> 27.4 us
  local copies, waits for them, and re-layouts: 5.22 us -> 8.71 us
  Pallas kernels: 85.6 us -> 87.4 us
    ppermute x5, waiting for transfers between devices: 4.9 us -> 11.1 us  [sent(): return lax.ppermute(block, 'tm', route)]
    dot_general x3 -> x2, matrix products: 11.6 us -> 7.48 us  [block_product(): jnp.dot(block, matrix, precision=lax.Precision.HIGH, preferred_element_ty...]
    slice x0 -> x2, local copies, waits for them, and re-layouts: none -> 2.11 us  [earlier(): return (weights_all[0:2], products[0], products[1:], combined)]
    pallas_call x1, Pallas kernels: 85.6 us -> 87.4 us  [chain(): pl.pallas_call(functools.partial(chain_kernel, steps, stride, head), out_...]
    dot_general x2 -> x1, matrix products: 12.9 us -> 12 us  [transition(): lax.dot_general(previous, current, (((0,), (0,)), ((), ())), precision=hi...]
  transfers between devices with their start and end apart: 6 -> 6, of which waited for: 1 -> 3; matrix products, arithmetic and copies ran while one was open for 10% -> 2% of each run, Pallas kernels for 0% -> 0%
where the time goes in v11:
time: 148 us; the launch traced here: 147 us
  Pallas kernels  87.4 us (59%)
  matrix products  27.4 us (19%)
  waiting for transfers between devices  11.1 us (8%)
  local copies, waits for them, and re-layouts  8.71 us (6%)
  starting transfers between devices  7.12 us (5%)
  other arithmetic  5 us (3%)
    pallas_call x1, Pallas kernels, chain(): pl.pallas_call(functools.partial(chain_kernel, steps, stride, head), out_...  87.4 us
    dot_general x1, matrix products, transition(): lax.dot_general(previous, current, (((0,), (0,)), ((), ())), precision=hi...  12 us
    ppermute x5, waiting for transfers between devices, sent(): return lax.ppermute(block, 'tm', route)  11.1 us
    dot_general x2, matrix products, block_product(): jnp.dot(block, matrix, precision=lax.Precision.HIGH, preferred_element_ty...  7.48 us
    dot_general x1, matrix products, earlier(): lax.dot_general(weights_all[0::2], weights_all[1::2], (((2,), (1,)), ((0,...  7.27 us
    ppermute x5, starting transfers between devices, sent(): return lax.ppermute(block, 'tm', route)  5.21 us
  transfers between devices with their start and end apart: 6, of which 3 were waited for; matrix products, arithmetic and copies ran while one was open for 2% of the time, Pallas kernels for 0%

profile of v11, /device:TPU:504, one launch (start us, length us, event | category | flops | bytes accessed | tf_op | source)
XLA Modules:
  0.0 147.2 jit_solution(3213794730339845743)
XLA Ops:
  0.0 0.7 copy.20
  0.7 0.7 fusion.33
  1.5 0.1 pad.28.clone
  1.5 0.8 maximum_bitcast_fusion.1
  2.3 0.1 pad.25.clone
  2.4 1.0 fusion.26
  3.4 1.3 collective-permute-start.1
  4.7 0.7 collective-permute-start.2
  5.4 0.9 fusion.32
  6.3 1.3 collective-permute-start.3
  7.6 0.7 collective-permute-start.4
  8.3 3.4 %collective-permute-done.1 = f32[72,640]{1,0:T(8,128)S(1)} collective-permute-done((f32[72,640]{1,0:T(8,128)S(1)}, f32[72,640]{1,0:T(8,128)S(1)}, u32[]{:S(2)}, u32[]{:S(2)}) %collective-permute-start.1) | collective-permute-done | bytes 184352 | tf_op jit(solution)/shard_map/ppermute | solution.py:248
  11.7 0.7 constant_dynamic-update-slice_fusion.3
  12.4 0.0 collective-permute-done.2
  12.4 0.7 constant_dynamic-update-slice_fusion.2
  13.1 0.5 collective-permute-done.3
  13.6 0.6 constant_dynamic-update-slice_fusion.1
  14.2 0.0 collective-permute-done.4
  14.2 0.6 constant_dynamic-update-slice_fusion
  14.8 1.9 %collective-permute-start.5 = (f32[208,640]{1,0:T(8,128)}, f32[208,640]{1,0:T(8,128)}, u32[]{:S(2)}, u32[]{:S(2)}) collective-permute-start(f32[208,640]{1,0:T(8,128)} %constant_dynamic-update-slice_fusion), channel_id=1, source_target_pairs={{0,1},{1,0},{2,3},{3,2},{4,5},{5,4},{6,7},{7,6},{8,9},{9,8},{10,11... | collective-permute-start | bytes 1597448 | tf_op jit(solution)/shard_map/ppermute | solution.py:260
  16.8 1.3 collective-permute-start
  18.1 7.2 %collective-permute-done = f32[64,640]{1,0:T(8,128)S(1)} collective-permute-done((f32[64,640]{1,0:T(8,128)S(1)}, f32[64,640]{1,0:T(8,128)S(1)}, u32[]{:S(2)}, u32[]{:S(2)}) %collective-permute-start) | collective-permute-done | bytes 163872 | tf_op jit(solution)/shard_map/ppermute | solution.py:248
  25.2 0.0 collective-permute-done.5
  25.3 0.0 copy-start.2
  25.3 33.8 %conditional.1 = (f32[2,640,640]{2,1,0:T(8,128)S(1)}, f32[640,640]{1,0:T(8,128)}, f32[2,640,640]{2,1,0:T(8,128)}, f32[640,640]{1,0:T(8,128)}) conditional(s32[]{:T(128)} %convert_element_type.19, (f32[32]{0:T(128)}, f32[2,32]{1,0:T(2,128)}, f32[64,32]{0,1:T(8,128)}, f32[2,64,640]{2,1,0:T(8,128)}, s32[2,640]{1,0:T(2,128)}, /*index=5*/f32[2]{0:T(128)}, ...), branch_computations={%region_0.5_spmd, %region_5.10_spmd} | conditional | flops 9871785984 | bytes 66473128 | solution.py:327
  25.3 0.0 copy-start
  25.3 1.3 broadcast_select_fusion.1
  26.6 0.1 fusion.30
  26.7 0.0 copy-start.1
  26.7 0.0 copy-start.3
  26.8 0.0 copy-done
  26.8 0.1 multiply_reduce_fusion.2
  27.1 0.1 multiply_reduce_fusion.3
  27.2 0.2 slice_reduce_fusion
  27.4 0.2 slice_reduce_fusion.1
  27.5 0.2 copy.23
  27.7 0.1 pad_maximum_fusion.8
  27.9 0.1 copy.18
  28.0 0.0 copy-done.1
  28.0 0.0 copy-done.3
  28.0 0.7 fusion.15
  28.7 0.1 fusion.19
  28.8 0.1 fusion.18
  28.9 12.0 %add_multiply_fusion.1 = f32[6,640,640]{2,1,0:T(8,128)S(1)} fusion(f32[6,640]{1,0:T(8,128)S(1)} %multiply_reduce_fusion.2, f32[6,640]{1,0:T(8,128)S(1)} %multiply_reduce_fusion.3, f32[6]{0:T(128)S(1)} %pad_maximum_fusion.8, s32[6,640]{1,0:T(8,128)S(1)} %maximum_convert_fusion, f32[6,640]{1,0:T(8,128)S(1)} %fusion.18, ...), kind=kOutput, calls=%fused_computation.18 | convolution fusion | flops 1910046720 | bytes 11857944 | tf_op jit(solution)/shard_map/cond/branch_1_fun/vmap()/dot_general | solution.py:24
  40.9 0.2 slice.145
  41.1 7.3 %fusion.9 = f32[3,640,640]{2,1,0:T(8,128)S(1)} fusion(f32[6,640,640]{2,1,0:T(8,128)S(1)} %add_multiply_fusion.1), kind=kOutput, calls=%fused_computation.20 | convolution fusion | flops 4718592000 | bytes 14745600 | tf_op jit(solution)/shard_map/cond/branch_1_fun/dot_general | solution.py:302
  48.4 1.3 slice_bitcast_fusion.8
  49.7 1.9 %slice.147 = f32[2,640,640]{2,1,0:T(8,128)} slice(f32[3,640,640]{2,1,0:T(8,128)S(1)} %fusion.9), slice={[1:3], [0:640], [0:640]} | slice | bytes 6553600 | tf_op jit(solution)/shard_map/cond/branch_1_fun/slice | solution.py:310
  51.6 2.5 %fusion.12 = f32[640,640]{1,0:T(8,128)S(1)} fusion(f32[3,640,640]{2,1,0:T(8,128)S(1)} %fusion.9), kind=kOutput, calls=%fused_computation.24 | convolution fusion | flops 1572864000 | bytes 4915200 | tf_op jit(solution)/shard_map/cond/branch_1_fun/dot_general | solution.py:209
  54.0 5.0 %fusion.34 = f32[640,640]{1,0:T(8,128)} fusion(f32[640,640]{1,0:T(8,128)S(1)} %fusion.12, f32[640,640]{1,0:T(8,128)} %slice_bitcast_fusion.8), kind=kOutput, calls=%fused_computation.85 | convolution fusion | flops 1572864000 | bytes 4915200 | tf_op jit(solution)/shard_map/cond/branch_1_fun/dot_general | solution.py:209
  59.0 0.0 copy-done.2
  59.1 87.4 %shard_map.73 = f32[8,640]{1,0:T(8,128)S(1)} custom-call(f32[2,640,640]{2,1,0:T(8,128)S(1)} %get-tuple-element.57.refs_0_, f32[640,640]{1,0:T(8,128)} %get-tuple-element.58.refs_1_, f32[2,640,640]{2,1,0:T(8,128)} %get-tuple-element.59.refs_2_, f32[640,640]{1,0:T(8,128)} %get-tuple-element.60.refs_3_, f32[8,640]{1,0:T(8,128)S(1)} %broadcast_in_dim.26.refs_4_), custom_call_target="tpu_custom_call" | custom-call | tf_op jit(solution)/shard_map/pallas_call | solution.py:186
  146.5 0.6 fusion.27
  (28 shorter events, 0.3 us)
Async XLA Ops:
  3.4 8.3 %collective-permute-start.1 = (f32[72,640]{1,0:T(8,128)S(1)}, f32[72,640]{1,0:T(8,128)S(1)}, u32[]{:S(2)}, u32[]{:S(2)}) collective-permute-start(f32[72,640]{1,0:T(8,128)S(1)} %fusion.26), channel_id=1, source_target_pairs={{112,120},{120,128},{136,144},{144,152},{160,168},{168,176},{184,1... | collective-permute-start | bytes 552968 | tf_op jit(solution)/shard_map/ppermute | solution.py:248
  4.7 7.7 %collective-permute-start.2 = (f32[72,640]{1,0:T(8,128)S(1)}, f32[72,640]{1,0:T(8,128)S(1)}, u32[]{:S(2)}, u32[]{:S(2)}) collective-permute-start(f32[72,640]{1,0:T(8,128)S(1)} %fusion.26), channel_id=1, source_target_pairs={{112,128},{136,152},{160,176},{184,200},{208,224},{232,248},{256,2... | collective-permute-start | bytes 552968 | tf_op jit(solution)/shard_map/ppermute | solution.py:248
  6.3 7.2 %collective-permute-start.3 = (f32[32,640]{1,0:T(8,128)S(1)}, f32[32,640]{1,0:T(8,128)S(1)}, u32[]{:S(2)}, u32[]{:S(2)}) collective-permute-start(f32[32,640]{1,0:T(8,128)S(1)} %dynamic-slice_bitcast_fusion), channel_id=1, source_target_pairs={{104,120},{128,144},{152,168},{176,192},{200,216},{224,240},{248,2... | collective-permute-start | bytes 245768 | tf_op jit(solution)/shard_map/ppermute | solution.py:248
  7.6 6.6 %collective-permute-start.4 = (f32[32,640]{1,0:T(8,128)S(1)}, f32[32,640]{1,0:T(8,128)S(1)}, u32[]{:S(2)}, u32[]{:S(2)}) collective-permute-start(f32[32,640]{1,0:T(8,128)S(1)} %dynamic-slice_bitcast_fusion), channel_id=1, source_target_pairs={{104,128},{128,152},{152,176},{176,200},{200,224},{224,248},{248,2... | collective-permute-start | bytes 245768 | tf_op jit(solution)/shard_map/ppermute | solution.py:248
  14.8 10.4 %collective-permute-start.5 = (f32[208,640]{1,0:T(8,128)}, f32[208,640]{1,0:T(8,128)}, u32[]{:S(2)}, u32[]{:S(2)}) collective-permute-start(f32[208,640]{1,0:T(8,128)} %constant_dynamic-update-slice_fusion), channel_id=1, source_target_pairs={{0,1},{1,0},{2,3},{3,2},{4,5},{5,4},{6,7},{7,6},{8,9},{9,8},{10,11... | collective-permute-start | bytes 1597448 | tf_op jit(solution)/shard_map/ppermute | solution.py:260
  16.8 8.5 %collective-permute-start = (f32[64,640]{1,0:T(8,128)S(1)}, f32[64,640]{1,0:T(8,128)S(1)}, u32[]{:S(2)}, u32[]{:S(2)}) collective-permute-start(f32[64,640]{1,0:T(8,128)S(1)} %get-tuple-element.87), channel_id=1, source_target_pairs={{0,8},{8,16},{16,24},{24,32},{32,40},{40,48},{48,56},{56,64},{64,7... | collective-permute-start | bytes 491528 | tf_op jit(solution)/shard_map/ppermute | solution.py:248
  25.3 33.8 %copy-start.2 = (f32[640]{0:T(1024)S(1)}, f32[640]{0:T(1024)}, u32[]{:S(2)}) copy-start(f32[640]{0:T(1024)} %param.15) | copy-start | bytes 7684
  25.3 1.6 %copy-start = (f32[2,64,640]{2,1,0:T(8,128)S(1)}, f32[2,64,640]{2,1,0:T(8,128)}, u32[]{:S(2)}) copy-start(f32[2,64,640]{2,1,0:T(8,128)} %get-tuple-element.49) | copy-start | bytes 983044 | tf_op jit(solution)/shard_map/cond
  26.7 1.3 copy-start.1
  26.7 1.3 copy-start.3

commit v12 on v10

--- a/solution.py
+++ b/solution.py
@@ -9,7 +9,7 @@
 
 MESH = pl.DeviceIdType.MESH
 STRIDE = 3
-HEAD = 13
+HEAD = 12
 
 
 def shifted(block, axis, distance):

time: 143 us -> 141 us (0.986)
  Pallas kernels: 85.6 us -> 79.6 us
  waiting for transfers between devices: 4.9 us -> 8.48 us
    pallas_call x1, Pallas kernels: 85.6 us -> 79.6 us  [chain(): pl.pallas_call(functools.partial(chain_kernel, steps, stride, head), out_...]
    ppermute x5, waiting for transfers between devices: 4.9 us -> 8.48 us  [sent(): return lax.ppermute(block, 'tm', route)]
where the time goes in v12:
time: 141 us
  Pallas kernels  79.6 us (56%)
  matrix products  32.9 us (23%)
  waiting for transfers between devices  8.48 us (6%)
  starting transfers between devices  7.74 us (5%)
  other arithmetic  6.2 us (4%)
  local copies, waits for them, and re-layouts  5.22 us (4%)
    pallas_call x1, Pallas kernels, chain(): pl.pallas_call(functools.partial(chain_kernel, steps, stride, head), out_...  79.6 us
    dot_general x2, matrix products, transition(): lax.dot_general(previous, current, (((0,), (0,)), ((), ())), precision=hi...  12.9 us
    dot_general x3, matrix products, block_product(): jnp.dot(block, matrix, precision=lax.Precision.HIGH, preferred_element_ty...  11.6 us
    ppermute x5, waiting for transfers between devices, sent(): return lax.ppermute(block, 'tm', route)  8.48 us
    dot_general x1, matrix products, earlier(): lax.dot_general(weights_all[0::2], weights_all[1::2], (((2,), (1,)), ((0,...  6.65 us
    ppermute x5, starting transfers between devices, sent(): return lax.ppermute(block, 'tm', route)  5.83 us
  transfers between devices with their start and end apart: 6, of which 1 were waited for; matrix products, arithmetic and copies ran while one was open for 10% of the time, Pallas kernels for 0%

profile of v12, /device:TPU:504, one launch (start us, length us, event | category | flops | bytes accessed | tf_op | source)
XLA Modules:
  0.0 140.7 jit_solution(9826502748569181271)
XLA Ops:
  0.0 0.0 copy-start.6
  0.0 0.0 copy-start.3
  0.0 0.8 copy.12
  0.8 0.1 pad.26.clone
  0.9 0.8 maximum_bitcast_fusion.1
  1.7 0.7 convert_bitcast_fusion
  2.4 0.1 pad.23.clone
  2.4 1.0 fusion.20
  3.4 1.3 collective-permute-start.1
  4.7 1.3 collective-permute-start.2
  6.0 1.0 fusion.28
  7.1 0.7 collective-permute-start.3
  7.8 1.3 collective-permute-start.4
  9.1 1.3 collective-permute-start
  10.4 1.3 fusion.16
  11.7 0.1 fusion.23
  11.8 0.1 fusion.22
  11.9 1.0 multiply_reduce_fusion.2
  12.9 8.5 %collective-permute-done = f32[64,640]{1,0:T(8,128)S(1)} collective-permute-done((f32[64,640]{1,0:T(8,128)S(1)}, f32[64,640]{1,0:T(8,128)S(1)}, u32[]{:S(2)}, u32[]{:S(2)}) %collective-permute-start) | collective-permute-done | bytes 163872 | tf_op jit(solution)/shard_map/ppermute | solution.py:248
  21.4 0.0 copy-start.1
  21.4 0.0 collective-permute-done.1
  21.4 0.7 constant_dynamic-update-slice_fusion.3
  22.1 0.0 collective-permute-done.2
  22.1 0.7 constant_dynamic-update-slice_fusion.2
  22.8 0.0 collective-permute-done.3
  22.8 0.6 constant_dynamic-update-slice_fusion.1
  23.5 0.0 collective-permute-done.4
  23.5 0.6 constant_dynamic-update-slice_fusion
  24.1 0.0 copy-done.1
  24.1 1.9 %collective-permute-start.5 = (f32[208,640]{1,0:T(8,128)}, f32[208,640]{1,0:T(8,128)}, u32[]{:S(2)}, u32[]{:S(2)}) collective-permute-start(f32[208,640]{1,0:T(8,128)} %constant_dynamic-update-slice_fusion), channel_id=1, source_target_pairs={{0,1},{1,0},{2,3},{3,2},{4,5},{5,4},{6,7},{7,6},{8,9},{9,8},{10,11... | collective-permute-start | bytes 1597448 | tf_op jit(solution)/shard_map/ppermute | solution.py:260
  26.0 0.0 copy-done.6
  26.0 0.0 copy-done.3
  26.0 5.0 %add_multiply_fusion.1.refs_0_ = f32[2,640,640]{2,1,0:T(8,128)S(1)} fusion(f32[2,64,640]{2,1,0:T(8,128)} %param.9, f32[2,640]{1,0:T(2,128)S(1)} %multiply_reduce_fusion.2, f32[2,640]{1,0:T(2,128)S(1)} %multiply_reduce_fusion.3, f32[2]{0:T(128)S(1)} %copy-done.6, s32[2,640]{1,0:T(2,128)S(1)} %copy-done.3, f32[2,640]{1,0:T(2,128)S(1)} %fusion.22, ...), kind=kOutput, calls=%fused_computation.37 | convolution fusion | flops 636600320 | bytes 3952648 | tf_op jit(solution)/shard_map/vmap()/dot_general | solution.py:24
  31.0 0.0 copy-start.2
  31.0 0.0 copy-start.5
  31.0 3.5 %fusion.12.refs_1_ = f32[640,640]{1,0:T(8,128)} fusion(f32[2,640,640]{2,1,0:T(8,128)S(1)} %add_multiply_fusion.1.refs_0_), kind=kOutput, calls=%fused_computation.40 | convolution fusion | flops 1572864000 | bytes 4915200 | tf_op jit(solution)/shard_map/dot_general | solution.py:209
  34.5 0.0 collective-permute-done.5
  34.5 0.0 copy-done.2
  34.6 0.0 copy-done.5
  34.6 0.0 copy-start.4
  34.6 25.9 %conditional.1 = (f32[2,640,640]{2,1,0:T(8,128)}, f32[640,640]{1,0:T(8,128)}) conditional(s32[]{:T(128)} %convert_element_type.20, () %tuple.13, (f32[32]{0:T(128)S(1)}, s32[]{:T(128)}, f32[208,640]{1,0:T(8,128)}, f32[208,640]{1,0:T(8,128)}, f32[64,32]{0,1:T(8,128)S(1)}, /*index=5*/f32[640,640]{1,0:T(8,128)}) %tuple.30), branch_computations={%region_4.5_spmd, %region_5.10_spmd} | conditional | flops 7630446080 | bytes 44739368 | solution.py:329
  34.8 1.3 broadcast_select_fusion.1
  36.1 0.1 fusion.26
  36.3 0.5 fusion.6
  36.8 0.1 fusion.9
  36.9 0.1 fusion.8
  37.2 0.1 multiply_reduce_fusion.1
  37.2 0.1 multiply_reduce_fusion
  37.4 0.2 slice_reduce_fusion.1
  37.5 0.2 slice_reduce_fusion
  37.7 0.1 pad_maximum_fusion.8
  37.8 7.9 %add_multiply_fusion = f32[4,640,640]{2,1,0:T(8,128)S(1)} fusion(f32[4,640]{1,0:T(4,128)S(1)} %multiply_reduce_fusion, f32[4,640]{1,0:T(4,128)S(1)} %multiply_reduce_fusion.1, f32[4]{0:T(128)S(1)} %pad_maximum_fusion.8, s32[4,640]{1,0:T(4,128)S(1)} %maximum_convert_fusion, f32[4,640]{1,0:T(4,128)S(1)} %fusion.8, f32[2,64,640]{2,1,0:T(8,128)S(1)} %slice.107, ...), kind=kOutput, calls=%fused_computation | convolution fusion | flops 1273692160 | bytes 7905296 | tf_op jit(solution)/shard_map/cond/branch_1_fun/vmap()/dot_general | solution.py:24
  45.7 6.6 %fusion = f32[2,640,640]{2,1,0:T(8,128)} fusion(f32[4,640,640]{2,1,0:T(8,128)S(1)} %add_multiply_fusion), kind=kOutput, calls=%fused_computation.2 | convolution fusion | flops 3145728000 | bytes 9830400 | tf_op jit(solution)/shard_map/cond/branch_1_fun/dot_general | solution.py:313
  52.3 0.0 copy-start
  52.3 4.5 %fusion.3 = f32[640,640]{1,0:T(8,128)S(1)} fusion(f32[2,640,640]{2,1,0:T(8,128)} %fusion), kind=kOutput, calls=%fused_computation.6 | convolution fusion | flops 1572864000 | bytes 4915200 | tf_op jit(solution)/shard_map/cond/branch_1_fun/dot_general | solution.py:209
  56.8 0.0 copy-done
  56.8 3.6 %fusion.29 = f32[640,640]{1,0:T(8,128)} fusion(f32[640,640]{1,0:T(8,128)S(1)} %fusion.3, f32[640,640]{1,0:T(8,128)S(1)} %copy-done), kind=kOutput, calls=%fused_computation.75 | convolution fusion | flops 1572864000 | bytes 4915200 | tf_op jit(solution)/shard_map/cond/branch_1_fun/dot_general | solution.py:209
  60.4 0.0 copy-done.4
  60.4 79.6 %shard_map.73 = f32[8,640]{1,0:T(8,128)S(1)} custom-call(f32[2,640,640]{2,1,0:T(8,128)S(1)} %add_multiply_fusion.1.refs_0_, f32[640,640]{1,0:T(8,128)} %fusion.12.refs_1_, f32[2,640,640]{2,1,0:T(8,128)} %get-tuple-element.25.refs_2_, f32[640,640]{1,0:T(8,128)} %get-tuple-element.26.refs_3_, f32[8,640]{1,0:T(8,128)S(1)} %broadcast_in_dim.17.refs_4_), custom_call_target="tpu_custom_call" | custom-call | tf_op jit(solution)/shard_map/pallas_call | solution.py:186
  140.0 0.6 fusion.24
  (24 shorter events, 0.3 us)
Async XLA Ops:
  0.0 26.0 %copy-start.6 = (f32[2]{0:T(128)S(1)}, f32[2]{0:T(128)}, u32[]{:S(2)}) copy-start(f32[2]{0:T(128)} %param.12) | copy-start | bytes 28
  0.0 26.0 %copy-start.3 = (s32[2,640]{1,0:T(2,128)S(1)}, s32[2,640]{1,0:T(2,128)}, u32[]{:S(2)}) copy-start(s32[2,640]{1,0:T(2,128)} %param.10) | copy-start | bytes 15364
  3.4 18.0 %collective-permute-start.1 = (f32[72,640]{1,0:T(8,128)S(1)}, f32[72,640]{1,0:T(8,128)S(1)}, u32[]{:S(2)}, u32[]{:S(2)}) collective-permute-start(f32[72,640]{1,0:T(8,128)S(1)} %fusion.20), channel_id=1, source_target_pairs={{104,112},{112,120},{128,136},{136,144},{152,160},{160,168},{176,1... | collective-permute-start | bytes 552968 | tf_op jit(solution)/shard_map/ppermute | solution.py:248
  4.7 17.4 %collective-permute-start.2 = (f32[72,640]{1,0:T(8,128)S(1)}, f32[72,640]{1,0:T(8,128)S(1)}, u32[]{:S(2)}, u32[]{:S(2)}) collective-permute-start(f32[72,640]{1,0:T(8,128)S(1)} %fusion.20), channel_id=1, source_target_pairs={{104,120},{128,144},{152,168},{176,192},{200,216},{224,240},{248,2... | collective-permute-start | bytes 552968 | tf_op jit(solution)/shard_map/ppermute | solution.py:248
  7.1 15.7 %collective-permute-start.3 = (f32[32,640]{1,0:T(8,128)S(1)}, f32[32,640]{1,0:T(8,128)S(1)}, u32[]{:S(2)}, u32[]{:S(2)}) collective-permute-start(f32[32,640]{1,0:T(8,128)S(1)} %dynamic-slice_bitcast_fusion), channel_id=1, source_target_pairs={{96,112},{120,136},{144,160},{168,184},{192,208},{216,232},{240,25... | collective-permute-start | bytes 245768 | tf_op jit(solution)/shard_map/ppermute | solution.py:248
  7.8 15.7 %collective-permute-start.4 = (f32[32,640]{1,0:T(8,128)S(1)}, f32[32,640]{1,0:T(8,128)S(1)}, u32[]{:S(2)}, u32[]{:S(2)}) collective-permute-start(f32[32,640]{1,0:T(8,128)S(1)} %dynamic-slice_bitcast_fusion), channel_id=1, source_target_pairs={{96,120},{120,144},{144,168},{168,192},{192,216},{216,240},{240,26... | collective-permute-start | bytes 245768 | tf_op jit(solution)/shard_map/ppermute | solution.py:248
  9.1 12.3 %collective-permute-start = (f32[64,640]{1,0:T(8,128)S(1)}, f32[64,640]{1,0:T(8,128)S(1)}, u32[]{:S(2)}, u32[]{:S(2)}) collective-permute-start(f32[64,640]{1,0:T(8,128)S(1)} %get-tuple-element.44), channel_id=1, source_target_pairs={{0,8},{8,16},{16,24},{24,32},{32,40},{40,48},{48,56},{56,64},{64,7... | collective-permute-start | bytes 491528 | tf_op jit(solution)/shard_map/ppermute | solution.py:248
  21.4 2.7 %copy-start.1 = (f32[64,640]{1,0:T(8,128)}, f32[64,640]{1,0:T(8,128)S(1)}, u32[]{:S(2)}) copy-start(f32[64,640]{1,0:T(8,128)S(1)} %collective-permute-done) | copy-start | bytes 491524
  24.1 10.4 %collective-permute-start.5 = (f32[208,640]{1,0:T(8,128)}, f32[208,640]{1,0:T(8,128)}, u32[]{:S(2)}, u32[]{:S(2)}) collective-permute-start(f32[208,640]{1,0:T(8,128)} %constant_dynamic-update-slice_fusion), channel_id=1, source_target_pairs={{0,1},{1,0},{2,3},{3,2},{4,5},{5,4},{6,7},{7,6},{8,9},{9,8},{10,11... | collective-permute-start | bytes 1597448 | tf_op jit(solution)/shard_map/ppermute | solution.py:260
  31.0 3.5 %copy-start.2 = (f32[64,32]{0,1:T(8,128)S(1)}, f32[64,32]{0,1:T(8,128)}, u32[]{:S(2)}) copy-start(f32[64,32]{0,1:T(8,128)} %param.13) | copy-start | bytes 24580
  31.0 3.5 %copy-start.5 = (f32[32]{0:T(128)S(1)}, f32[32]{0:T(128)}, u32[]{:S(2)}) copy-start(f32[32]{0:T(128)} %param.14) | copy-start | bytes 388
  34.6 25.9 %copy-start.4 = (f32[640]{0:T(1024)S(1)}, f32[640]{0:T(1024)}, u32[]{:S(2)}) copy-start(f32[640]{0:T(1024)} %param.15) | copy-start | bytes 7684
  52.3 4.5 %copy-start = (f32[640,640]{1,0:T(8,128)S(1)}, f32[640,640]{1,0:T(8,128)}, u32[]{:S(2)}) copy-start(f32[640,640]{1,0:T(8,128)} %get-tuple-element.22) | copy-start | bytes 4915204 | tf_op jit(solution)/shard_map/cond

commit v13 on v12

--- a/solution.py
+++ b/solution.py
@@ -134,7 +134,10 @@
                 copies[d - 1].start()
 
     loads[0].wait()
-    loads[1].wait()
+
+    @pl.when(tail_node)
+    def _():
+        loads[1].wait()
 
     @pl.when(me == 0)
     def _():
@@ -152,6 +155,10 @@
     @pl.when(tail_node)
     def _():
         send_all(normalized(vec_mat(out_ref[...], combined_ref[...])))
+
+    @pl.when(jnp.logical_not(tail_node))
+    def _():
+        loads[1].wait()
 
     for load in loads[4:]:
         load.wait()
@@ -257,7 +264,6 @@
     fetched += [sent(rim_half, e, lambda i, e=e: need(i) + 1 == e) for e in range(2, stride + 1)]
     bundle = jnp.concatenate(fetched, axis=0)
     pairs = [(r, r ^ 1) for r in range(lax.axis_size("rows"))]
-    other = lax.ppermute(bundle, "rows", pairs)
 
     def own_matrices():
         return jax.vmap(transition, in_axes=(0, 0, 0, 0, 0, None, None))(
@@ -273,7 +279,8 @@
     weights_own = own_matrices()
     block_own = block_product([weights_own[0], weights_own[1]])
 
-    def earlier(bundle, other):
+    def earlier(bundle):
+        other = lax.ppermute(bundle, "rows", pairs)
         first_half = jnp.where(core == 0, bundle, other)
         second_half = jnp.where(core == 0, other, bundle)
         rows_of = [f.shape[0] for f in fetched]
@@ -320,13 +327,13 @@
         combined = block_product([products[d] for d in range(stride - 2, -1, -1)] + [block_own])
         return products, combined
 
-    def skipped(bundle, other):
+    def skipped(bundle):
         return (
             jnp.zeros((stride - 1, count, count), jnp.float32),
             jnp.zeros((count, count), jnp.float32),
         )
 
-    befores, combined = lax.cond(me > head, earlier, skipped, bundle, other)
+    befores, combined = lax.cond(me > head, earlier, skipped, bundle)
 
     prior8 = jnp.broadcast_to(prior_weights[None, :], (8, count))
     weights = chain(weights_own, block_own, befores, combined, prior8, steps, stride, head)

time: 141 us -> 147 us (1.043)
  waiting for transfers between devices: 8.48 us -> 11.6 us
  other arithmetic: 6.2 us -> 8.75 us
    ppermute x1, waiting for transfers between devices: 0.01 us -> 2.04 us  [earlier(): other = lax.ppermute(bundle, 'rows', pairs)]
    concatenate x0 -> x1, other arithmetic: none -> 1.89 us  [shards(): bundle = jnp.concatenate(fetched, axis=0)]
  transfers between devices with their start and end apart: 6 -> 6, of which waited for: 1 -> 2; matrix products, arithmetic and copies ran while one was open for 10% -> 10% of each run, Pallas kernels for 0% -> 0%
where the time goes in v13:
time: 147 us; the launch traced here: 146 us
  Pallas kernels  80.9 us (55%)
  matrix products  32.9 us (22%)
  waiting for transfers between devices  11.6 us (8%)
  other arithmetic  8.75 us (6%)
  starting transfers between devices  7.91 us (5%)
  local copies, waits for them, and re-layouts  3.79 us (3%)
    pallas_call x1, Pallas kernels, chain(): pl.pallas_call(functools.partial(chain_kernel, steps, stride, head), out_...  80.9 us
    dot_general x2, matrix products, transition(): lax.dot_general(previous, current, (((0,), (0,)), ((), ())), precision=hi...  12.8 us
    dot_general x3, matrix products, block_product(): jnp.dot(block, matrix, precision=lax.Precision.HIGH, preferred_element_ty...  11.6 us
    ppermute x5, waiting for transfers between devices, sent(): return lax.ppermute(block, 'tm', route)  9.53 us
    dot_general x1, matrix products, earlier(): lax.dot_general(weights_all[0::2], weights_all[1::2], (((2,), (1,)), ((0,...  6.65 us
    ppermute x5, starting transfers between devices, sent(): return lax.ppermute(block, 'tm', route)  5.81 us
  transfers between devices with their start and end apart: 6, of which 2 were waited for; matrix products, arithmetic and copies ran while one was open for 10% of the time, Pallas kernels for 0%

profile of v13, /device:TPU:504, one launch (start us, length us, event | category | flops | bytes accessed | tf_op | source)
XLA Modules:
  0.0 146.1 jit_solution(13500501247246265196)
XLA Ops:
  0.0 1.0 fusion.28
  1.0 0.7 dynamic-slice_bitcast_fusion
  1.7 0.7 collective-permute-start.4
  2.4 1.3 collective-permute-start.5
  3.7 0.7 copy.12
  4.4 0.1 pad.30.clone
  4.5 0.8 maximum_bitcast_fusion.1
  5.2 0.7 convert_bitcast_fusion
  6.0 0.1 pad.27.clone
  6.0 1.7 %fusion.20 = f32[72,640]{1,0:T(8,128)} fusion(s32[]{:T(128)S(6)} %select_n.30, f32[2,64,640]{2,1,0:T(8,128)} %param.9, f32[2,1,640]{2,1,0:T(1,128)S(1)} %copy.13, f32[2,1,640]{2,1,0:T(1,128)S(1)} %copy.14, f32[72]{0:T(128)S(1)} %pad.27.clone), kind=kLoop, calls=%fused_computation.57 | loop fusion | flops 138240 | bytes 522532 | tf_op jit(solution)/shard_map/jit(dynamic_index_in_dim)/squeeze | solution.py:261
  7.7 1.3 collective-permute-start.2
  9.0 1.3 collective-permute-start.3
  10.3 1.3 collective-permute-start.1
  11.6 1.3 fusion.16
  12.9 0.1 fusion.23
  13.0 0.1 fusion.22
  13.1 1.0 multiply_reduce_fusion.2
  14.1 9.5 %collective-permute-done.1 = f32[64,640]{1,0:T(8,128)S(1)} collective-permute-done((f32[64,640]{1,0:T(8,128)S(1)}, f32[64,640]{1,0:T(8,128)S(1)}, u32[]{:S(2)}, u32[]{:S(2)}) %collective-permute-start.1) | collective-permute-done | bytes 163872 | tf_op jit(solution)/shard_map/ppermute | solution.py:255
  23.6 0.0 copy-start.1
  23.6 0.7 copy-done.1
  24.3 4.9 %add_multiply_fusion.1.refs_0_ = f32[2,640,640]{2,1,0:T(8,128)S(1)} fusion(f32[2,64,640]{2,1,0:T(8,128)} %param.9, f32[2,640]{1,0:T(2,128)S(1)} %multiply_reduce_fusion.2, f32[2,640]{1,0:T(2,128)S(1)} %multiply_reduce_fusion.3, f32[2]{0:T(128)} %param.12, s32[2,640]{1,0:T(2,128)} %param.10, f32[2,640]{1,0:T(2,128)S(1)} %fusion.22, ...), kind=kOutput, calls=%fused_computation.37 | convolution fusion | flops 636600320 | bytes 3952648 | tf_op jit(solution)/shard_map/vmap()/dot_general | solution.py:24
  29.3 0.0 copy-start.2
  29.3 0.0 copy-start.4
  29.3 3.5 %fusion.12.refs_1_ = f32[640,640]{1,0:T(8,128)} fusion(f32[2,640,640]{2,1,0:T(8,128)S(1)} %add_multiply_fusion.1.refs_0_), kind=kOutput, calls=%fused_computation.40 | convolution fusion | flops 1572864000 | bytes 4915200 | tf_op jit(solution)/shard_map/dot_general | solution.py:216
  32.8 0.0 collective-permute-done.4
  32.8 0.0 collective-permute-done.5
  32.8 0.0 collective-permute-done.2
  32.8 0.0 collective-permute-done.3
  32.8 1.9 %pad_maximum_fusion.9 = f32[208,640]{1,0:T(8,128)} fusion(f32[32,640]{1,0:T(8,128)} %collective-permute-done.5, f32[32,640]{1,0:T(8,128)S(1)} %collective-permute-done.4, f32[72,640]{1,0:T(8,128)} %collective-permute-done.3, f32[72,640]{1,0:T(8,128)} %collective-permute-done.2), kind=kLoop, calls=%fused_computation.47 | loop fusion | flops 399360 | bytes 1064960 | tf_op jit(solution)/shard_map/concatenate | solution.py:265
  34.7 0.0 copy-done.2
  34.7 0.0 copy-done.4
  34.7 0.0 copy-start.3
  34.7 29.8 %conditional.1 = (f32[2,640,640]{2,1,0:T(8,128)}, f32[640,640]{1,0:T(8,128)}) conditional(s32[]{:T(128)} %convert_element_type.20, () %tuple.13, (f32[32]{0:T(128)S(1)}, s32[]{:T(128)}, f32[208,640]{1,0:T(8,128)}, f32[64,32]{0,1:T(8,128)S(1)}, f32[640,640]{1,0:T(8,128)}) %tuple.30), branch_computations={%region_4.5_spmd, %region_5.10_spmd} | conditional | flops 7630446080 | bytes 46869324 | solution.py:336
  34.7 2.1 %collective-permute-start = (f32[208,640]{1,0:T(8,128)}, f32[208,640]{1,0:T(8,128)}, u32[]{:S(2)}, u32[]{:S(2)}) collective-permute-start(f32[208,640]{1,0:T(8,128)} %get-tuple-element.17), channel_id=1, source_target_pairs={{0,1},{1,0},{2,3},{3,2},{4,5},{5,4},{6,7},{7,6},{8,9},{9,8},{10,11... | collective-permute-start | bytes 1597448 | tf_op jit(solution)/shard_map/cond/branch_1_fun/ppermute | solution.py:283
  36.9 2.0 %collective-permute-done = f32[208,640]{1,0:T(8,128)} collective-permute-done((f32[208,640]{1,0:T(8,128)}, f32[208,640]{1,0:T(8,128)}, u32[]{:S(2)}, u32[]{:S(2)}) %collective-permute-start) | collective-permute-done | bytes 532512 | tf_op jit(solution)/shard_map/cond/branch_1_fun/ppermute | solution.py:283
  38.9 1.3 broadcast_select_fusion.1
  40.2 0.1 fusion.26
  40.5 0.2 slice_reduce_fusion.1
  40.6 0.2 slice_reduce_fusion
  40.8 0.1 multiply_reduce_fusion
  40.9 0.5 fusion.6
  41.4 0.1 fusion.9
  41.6 0.1 fusion.8
  41.7 0.1 pad_maximum_fusion.8
  41.8 0.1 multiply_reduce_fusion.1
  41.9 7.9 %add_multiply_fusion = f32[4,640,640]{2,1,0:T(8,128)S(1)} fusion(f32[4,640]{1,0:T(4,128)S(1)} %multiply_reduce_fusion, f32[4,640]{1,0:T(4,128)S(1)} %multiply_reduce_fusion.1, f32[4]{0:T(128)S(1)} %pad_maximum_fusion.8, s32[4,640]{1,0:T(4,128)S(1)} %maximum_convert_fusion, f32[4,640]{1,0:T(4,128)S(1)} %fusion.8, f32[2,64,640]{2,1,0:T(8,128)S(1)} %slice.107, ...), kind=kOutput, calls=%fused_computation | convolution fusion | flops 1273692160 | bytes 7905296 | tf_op jit(solution)/shard_map/cond/branch_1_fun/vmap()/dot_general | solution.py:24
  49.8 6.7 %fusion = f32[2,640,640]{2,1,0:T(8,128)} fusion(f32[4,640,640]{2,1,0:T(8,128)S(1)} %add_multiply_fusion), kind=kOutput, calls=%fused_computation.2 | convolution fusion | flops 3145728000 | bytes 9830400 | tf_op jit(solution)/shard_map/cond/branch_1_fun/dot_general | solution.py:320
  56.4 0.0 copy-start
  56.4 4.5 %fusion.3 = f32[640,640]{1,0:T(8,128)S(1)} fusion(f32[2,640,640]{2,1,0:T(8,128)} %fusion), kind=kOutput, calls=%fused_computation.6 | convolution fusion | flops 1572864000 | bytes 4915200 | tf_op jit(solution)/shard_map/cond/branch_1_fun/dot_general | solution.py:216
  60.9 0.0 copy-done
  60.9 3.6 %fusion.29 = f32[640,640]{1,0:T(8,128)} fusion(f32[640,640]{1,0:T(8,128)S(1)} %fusion.3, f32[640,640]{1,0:T(8,128)S(1)} %copy-done), kind=kOutput, calls=%fused_computation.72 | convolution fusion | flops 1572864000 | bytes 4915200 | tf_op jit(solution)/shard_map/cond/branch_1_fun/dot_general | solution.py:216
  64.5 0.0 copy-done.3
  64.5 80.9 %shard_map.73 = f32[8,640]{1,0:T(8,128)S(1)} custom-call(f32[2,640,640]{2,1,0:T(8,128)S(1)} %add_multiply_fusion.1.refs_0_, f32[640,640]{1,0:T(8,128)} %fusion.12.refs_1_, f32[2,640,640]{2,1,0:T(8,128)} %get-tuple-element.22.refs_2_, f32[640,640]{1,0:T(8,128)} %get-tuple-element.23.refs_3_, f32[8,640]{1,0:T(8,128)S(1)} %broadcast_in_dim.17.refs_4_), custom_call_target="tpu_custom_call" | custom-call | tf_op jit(solution)/shard_map/pallas_call | solution.py:193
  145.5 0.6 fusion.24
  (23 shorter events, 0.3 us)
Async XLA Ops:
  1.7 31.1 %collective-permute-start.4 = (f32[32,640]{1,0:T(8,128)}, f32[32,640]{1,0:T(8,128)S(1)}, u32[]{:S(2)}, u32[]{:S(2)}) collective-permute-start(f32[32,640]{1,0:T(8,128)} %dynamic-slice_bitcast_fusion), channel_id=1, source_target_pairs={{96,112},{120,136},{144,160},{168,184},{192,208},{216,232},{240,25... | collective-permute-start | bytes 245768 | tf_op jit(solution)/shard_map/ppermute | solution.py:255
  2.4 30.5 %collective-permute-start.5 = (f32[32,640]{1,0:T(8,128)}, f32[32,640]{1,0:T(8,128)}, u32[]{:S(2)}, u32[]{:S(2)}) collective-permute-start(f32[32,640]{1,0:T(8,128)} %dynamic-slice_bitcast_fusion), channel_id=1, source_target_pairs={{96,120},{120,144},{144,168},{168,192},{192,216},{216,240},{240,26... | collective-permute-start | bytes 245768 | tf_op jit(solution)/shard_map/ppermute | solution.py:255
  7.7 25.1 %collective-permute-start.2 = (f32[72,640]{1,0:T(8,128)}, f32[72,640]{1,0:T(8,128)}, u32[]{:S(2)}, u32[]{:S(2)}) collective-permute-start(f32[72,640]{1,0:T(8,128)} %fusion.20), channel_id=1, source_target_pairs={{104,112},{112,120},{128,136},{136,144},{152,160},{160,168},{176,1... | collective-permute-start | bytes 552968 | tf_op jit(solution)/shard_map/ppermute | solution.py:255
  9.0 23.8 %collective-permute-start.3 = (f32[72,640]{1,0:T(8,128)}, f32[72,640]{1,0:T(8,128)}, u32[]{:S(2)}, u32[]{:S(2)}) collective-permute-start(f32[72,640]{1,0:T(8,128)} %fusion.20), channel_id=1, source_target_pairs={{104,120},{128,144},{152,168},{176,192},{200,216},{224,240},{248,2... | collective-permute-start | bytes 552968 | tf_op jit(solution)/shard_map/ppermute | solution.py:255
  10.3 13.3 %collective-permute-start.1 = (f32[64,640]{1,0:T(8,128)S(1)}, f32[64,640]{1,0:T(8,128)S(1)}, u32[]{:S(2)}, u32[]{:S(2)}) collective-permute-start(f32[64,640]{1,0:T(8,128)S(1)} %get-tuple-element.41), channel_id=1, source_target_pairs={{0,8},{8,16},{16,24},{24,32},{32,40},{40,48},{48,56},{56,64},{64,7... | collective-permute-start | bytes 491528 | tf_op jit(solution)/shard_map/ppermute | solution.py:255
  23.6 0.7 copy-start.1
  29.3 5.5 %copy-start.2 = (f32[64,32]{0,1:T(8,128)S(1)}, f32[64,32]{0,1:T(8,128)}, u32[]{:S(2)}) copy-start(f32[64,32]{0,1:T(8,128)} %param.13) | copy-start | bytes 24580
  29.3 5.4 %copy-start.4 = (f32[32]{0:T(128)S(1)}, f32[32]{0:T(128)}, u32[]{:S(2)}) copy-start(f32[32]{0:T(128)} %param.14) | copy-start | bytes 388
  34.7 29.8 %copy-start.3 = (f32[640]{0:T(1024)S(1)}, f32[640]{0:T(1024)}, u32[]{:S(2)}) copy-start(f32[640]{0:T(1024)} %param.15) | copy-start | bytes 7684
  34.7 4.2 %collective-permute-start = (f32[208,640]{1,0:T(8,128)}, f32[208,640]{1,0:T(8,128)}, u32[]{:S(2)}, u32[]{:S(2)}) collective-permute-start(f32[208,640]{1,0:T(8,128)} %get-tuple-element.17), channel_id=1, source_target_pairs={{0,1},{1,0},{2,3},{3,2},{4,5},{5,4},{6,7},{7,6},{8,9},{9,8},{10,11... | collective-permute-start | bytes 1597448 | tf_op jit(solution)/shard_map/cond/branch_1_fun/ppermute | solution.py:283
  56.4 4.5 %copy-start = (f32[640,640]{1,0:T(8,128)S(1)}, f32[640,640]{1,0:T(8,128)}, u32[]{:S(2)}) copy-start(f32[640,640]{1,0:T(8,128)} %get-tuple-element.19) | copy-start | bytes 4915204 | tf_op jit(solution)/shard_map/cond

commit v14 on v12

--- a/solution.py
+++ b/solution.py
@@ -249,16 +249,6 @@
 
     rim_own = sent(states[-1], 1, lambda i: True)
 
-    core = lax.axis_index("rows") % 2
-    half_rows = dims // 2
-    packed_half = lax.dynamic_index_in_dim(packed, core, 0, keepdims=False)
-    rim_half = lax.dynamic_slice_in_dim(states[-1], core * half_rows, half_rows, 0)
-    fetched = [sent(packed_half, d, lambda i, d=d: need(i) >= d) for d in range(1, stride)]
-    fetched += [sent(rim_half, e, lambda i, e=e: need(i) + 1 == e) for e in range(2, stride + 1)]
-    bundle = jnp.concatenate(fetched, axis=0)
-    pairs = [(r, r ^ 1) for r in range(lax.axis_size("rows"))]
-    other = lax.ppermute(bundle, "rows", pairs)
-
     def own_matrices():
         return jax.vmap(transition, in_axes=(0, 0, 0, 0, 0, None, None))(
             jnp.stack([rim_own, states[0]]),
@@ -272,6 +262,19 @@
 
     weights_own = own_matrices()
     block_own = block_product([weights_own[0], weights_own[1]])
+
+    core = lax.axis_index("rows") % 2
+    half_rows = dims // 2
+    packed_half = lax.dynamic_index_in_dim(packed, core, 0, keepdims=False)
+    rim_half = lax.dynamic_slice_in_dim(states[-1], core * half_rows, half_rows, 0)
+    weights_own, block_own, packed_half, rim_half = lax.optimization_barrier(
+        (weights_own, block_own, packed_half, rim_half)
+    )
+    fetched = [sent(packed_half, d, lambda i, d=d: need(i) >= d) for d in range(1, stride)]
+    fetched += [sent(rim_half, e, lambda i, e=e: need(i) + 1 == e) for e in range(2, stride + 1)]
+    bundle = jnp.concatenate(fetched, axis=0)
+    pairs = [(r, r ^ 1) for r in range(lax.axis_size("rows"))]
+    other = lax.ppermute(bundle, "rows", pairs)
 
     def earlier(bundle, other):
         first_half = jnp.where(core == 0, bundle, other)

time: 141 us -> 145 us (1.028)
  waiting for transfers between devices: 8.48 us -> 14.5 us
  Pallas kernels: 79.6 us -> 77.5 us
    ppermute x5, waiting for transfers between devices: 8.48 us -> 12.3 us  [sent(): return lax.ppermute(block, 'tm', route)]
    ppermute x1, waiting for transfers between devices: 0.01 us -> 2.22 us  [shards(): other = lax.ppermute(bundle, 'rows', pairs)]
    pallas_call x1, Pallas kernels: 79.6 us -> 77.5 us  [chain(): pl.pallas_call(functools.partial(chain_kernel, steps, stride, head), out_...]
  transfers between devices with their start and end apart: 6 -> 6, of which waited for: 1 -> 4; matrix products, arithmetic and copies ran while one was open for 10% -> 5% of each run, Pallas kernels for 0% -> 0%
where the time goes in v14:
time: 145 us
  Pallas kernels  77.5 us (53%)
  matrix products  32.9 us (23%)
  waiting for transfers between devices  14.5 us (10%)
  starting transfers between devices  7.73 us (5%)
  other arithmetic  6.18 us (4%)
  local copies, waits for them, and re-layouts  5.78 us (4%)
    pallas_call x1, Pallas kernels, chain(): pl.pallas_call(functools.partial(chain_kernel, steps, stride, head), out_...  77.5 us
    dot_general x2, matrix products, transition(): lax.dot_general(previous, current, (((0,), (0,)), ((), ())), precision=hi...  12.8 us
    ppermute x5, waiting for transfers between devices, sent(): return lax.ppermute(block, 'tm', route)  12.3 us
    dot_general x3, matrix products, block_product(): jnp.dot(block, matrix, precision=lax.Precision.HIGH, preferred_element_ty...  11.6 us
    dot_general x1, matrix products, earlier(): lax.dot_general(weights_all[0::2], weights_all[1::2], (((2,), (1,)), ((0,...  6.65 us
    ppermute x5, starting transfers between devices, sent(): return lax.ppermute(block, 'tm', route)  5.82 us
  transfers between devices with their start and end apart: 6, of which 4 were waited for; matrix products, arithmetic and copies ran while one was open for 5% of the time, Pallas kernels for 0%

profile of v14, /device:TPU:504, one launch (start us, length us, event | category | flops | bytes accessed | tf_op | source)
XLA Modules:
  0.0 145.0 jit_solution(13265872393115849416)
XLA Ops:
  0.0 1.0 fusion.28
  1.0 1.3 collective-permute-start
  2.3 1.3 fusion.16
  3.6 0.1 fusion.23
  3.8 0.1 fusion.22
  3.8 0.7 convert_bitcast_fusion
  4.6 0.7 copy.12
  5.3 0.1 pad.26.clone
  5.4 0.8 maximum_bitcast_fusion.1
  6.1 0.1 pad.23.clone
  6.2 1.0 fusion.20
  7.2 1.0 multiply_reduce_fusion.2
  8.3 0.6 collective-permute-done
  8.9 0.0 copy-start.1
  8.9 0.7 copy-done.1
  9.6 4.9 %add_multiply_fusion.1.refs_0_ = f32[2,640,640]{2,1,0:T(8,128)S(1)} fusion(f32[2,64,640]{2,1,0:T(8,128)} %param.9, f32[2,640]{1,0:T(2,128)S(1)} %multiply_reduce_fusion.2, f32[2,640]{1,0:T(2,128)S(1)} %multiply_reduce_fusion.3, f32[2]{0:T(128)} %param.12, s32[2,640]{1,0:T(2,128)} %param.10, f32[2,640]{1,0:T(2,128)S(1)} %fusion.22, ...), kind=kOutput, calls=%fused_computation.37 | convolution fusion | flops 636600320 | bytes 3952648 | tf_op jit(solution)/shard_map/vmap()/dot_general | solution.py:24
  14.5 0.0 copy-start.2
  14.5 0.0 copy-start.4
  14.5 3.5 %fusion.12.refs_1_ = f32[640,640]{1,0:T(8,128)} fusion(f32[2,640,640]{2,1,0:T(8,128)S(1)} %add_multiply_fusion.1.refs_0_), kind=kOutput, calls=%fused_computation.40 | convolution fusion | flops 1572864000 | bytes 4915200 | tf_op jit(solution)/shard_map/dot_general | solution.py:209
  18.0 1.3 collective-permute-start.1
  19.3 1.3 collective-permute-start.2
  20.6 0.7 collective-permute-start.3
  21.3 1.3 collective-permute-start.4
  22.6 4.0 %collective-permute-done.1 = f32[72,640]{1,0:T(8,128)S(1)} collective-permute-done((f32[72,640]{1,0:T(8,128)S(1)}, f32[72,640]{1,0:T(8,128)S(1)}, u32[]{:S(2)}, u32[]{:S(2)}) %collective-permute-start.1) | collective-permute-done | bytes 184352 | tf_op jit(solution)/shard_map/ppermute | solution.py:248
  26.6 0.7 constant_dynamic-update-slice_fusion.3
  27.3 7.6 %collective-permute-done.2 = f32[72,640]{1,0:T(8,128)S(1)} collective-permute-done((f32[72,640]{1,0:T(8,128)S(1)}, f32[72,640]{1,0:T(8,128)S(1)}, u32[]{:S(2)}, u32[]{:S(2)}) %collective-permute-start.2) | collective-permute-done | bytes 184352 | tf_op jit(solution)/shard_map/ppermute | solution.py:248
  34.9 0.7 constant_dynamic-update-slice_fusion.2
  35.6 0.0 collective-permute-done.3
  35.6 0.6 constant_dynamic-update-slice_fusion.1
  36.3 0.0 collective-permute-done.4
  36.3 0.6 constant_dynamic-update-slice_fusion
  36.9 1.9 %collective-permute-start.5 = (f32[208,640]{1,0:T(8,128)}, f32[208,640]{1,0:T(8,128)}, u32[]{:S(2)}, u32[]{:S(2)}) collective-permute-start(f32[208,640]{1,0:T(8,128)} %constant_dynamic-update-slice_fusion), channel_id=1, source_target_pairs={{0,1},{1,0},{2,3},{3,2},{4,5},{5,4},{6,7},{7,6},{8,9},{9,8},{10,11... | collective-permute-start | bytes 1597448 | tf_op jit(solution)/shard_map/ppermute | solution.py:277
  38.8 2.2 %collective-permute-done.5 = f32[208,640]{1,0:T(8,128)} collective-permute-done((f32[208,640]{1,0:T(8,128)}, f32[208,640]{1,0:T(8,128)}, u32[]{:S(2)}, u32[]{:S(2)}) %collective-permute-start.5) | collective-permute-done | bytes 532512 | tf_op jit(solution)/shard_map/ppermute | solution.py:277
  41.1 0.0 copy-done.2
  41.1 0.0 copy-done.4
  41.1 0.0 copy-start.3
  41.1 25.8 %conditional.1 = (f32[2,640,640]{2,1,0:T(8,128)}, f32[640,640]{1,0:T(8,128)}) conditional(s32[]{:T(128)} %convert_element_type.21, () %tuple.15, (f32[32]{0:T(128)S(1)}, s32[]{:T(128)}, f32[208,640]{1,0:T(8,128)}, f32[208,640]{1,0:T(8,128)}, f32[64,32]{0,1:T(8,128)S(1)}, /*index=5*/f32[640,640]{1,0:T(8,128)}) %tuple.32), branch_computations={%region_4.5_spmd, %region_5.10_spmd} | conditional | flops 7630446080 | bytes 44739368 | solution.py:332
  41.3 1.3 broadcast_select_fusion.1
  42.5 0.1 fusion.26
  42.7 0.1 multiply_reduce_fusion
  42.9 0.1 multiply_reduce_fusion.1
  43.0 0.2 slice_reduce_fusion
  43.2 0.2 slice_reduce_fusion.1
  43.3 0.1 pad_maximum_fusion.8
  43.5 0.5 fusion.6
  44.0 0.1 fusion.9
  44.2 0.1 fusion.8
  44.2 7.9 %add_multiply_fusion = f32[4,640,640]{2,1,0:T(8,128)S(1)} fusion(f32[4,640]{1,0:T(4,128)S(1)} %multiply_reduce_fusion, f32[4,640]{1,0:T(4,128)S(1)} %multiply_reduce_fusion.1, f32[4]{0:T(128)S(1)} %pad_maximum_fusion.8, s32[4,640]{1,0:T(4,128)S(1)} %maximum_convert_fusion, f32[4,640]{1,0:T(4,128)S(1)} %fusion.8, f32[2,64,640]{2,1,0:T(8,128)S(1)} %slice.107, ...), kind=kOutput, calls=%fused_computation | convolution fusion | flops 1273692160 | bytes 7905296 | tf_op jit(solution)/shard_map/cond/branch_1_fun/vmap()/dot_general | solution.py:24
  52.1 6.6 %fusion = f32[2,640,640]{2,1,0:T(8,128)} fusion(f32[4,640,640]{2,1,0:T(8,128)S(1)} %add_multiply_fusion), kind=kOutput, calls=%fused_computation.2 | convolution fusion | flops 3145728000 | bytes 9830400 | tf_op jit(solution)/shard_map/cond/branch_1_fun/dot_general | solution.py:316
  58.8 0.0 copy-start
  58.8 4.5 %fusion.3 = f32[640,640]{1,0:T(8,128)S(1)} fusion(f32[2,640,640]{2,1,0:T(8,128)} %fusion), kind=kOutput, calls=%fused_computation.6 | convolution fusion | flops 1572864000 | bytes 4915200 | tf_op jit(solution)/shard_map/cond/branch_1_fun/dot_general | solution.py:209
  63.3 0.0 copy-done
  63.3 3.6 %fusion.29 = f32[640,640]{1,0:T(8,128)} fusion(f32[640,640]{1,0:T(8,128)S(1)} %fusion.3, f32[640,640]{1,0:T(8,128)S(1)} %copy-done), kind=kOutput, calls=%fused_computation.75 | convolution fusion | flops 1572864000 | bytes 4915200 | tf_op jit(solution)/shard_map/cond/branch_1_fun/dot_general | solution.py:209
  66.9 0.0 copy-done.3
  66.9 77.5 %shard_map.73 = f32[8,640]{1,0:T(8,128)S(1)} custom-call(f32[2,640,640]{2,1,0:T(8,128)S(1)} %add_multiply_fusion.1.refs_0_, f32[640,640]{1,0:T(8,128)} %fusion.12.refs_1_, f32[2,640,640]{2,1,0:T(8,128)} %get-tuple-element.33.refs_2_, f32[640,640]{1,0:T(8,128)} %get-tuple-element.34.refs_3_, f32[8,640]{1,0:T(8,128)S(1)} %broadcast_in_dim.17.refs_4_), custom_call_target="tpu_custom_call" | custom-call | tf_op jit(solution)/shard_map/pallas_call | solution.py:186
  144.4 0.6 fusion.24
  (24 shorter events, 0.3 us)
Async XLA Ops:
  1.0 7.8 %collective-permute-start = (f32[64,640]{1,0:T(8,128)S(1)}, f32[64,640]{1,0:T(8,128)S(1)}, u32[]{:S(2)}, u32[]{:S(2)}) collective-permute-start(f32[64,640]{1,0:T(8,128)S(1)} %get-tuple-element.52), channel_id=1, source_target_pairs={{0,8},{8,16},{16,24},{24,32},{32,40},{40,48},{48,56},{56,64},{64,7... | collective-permute-start | bytes 491528 | tf_op jit(solution)/shard_map/ppermute | solution.py:248
  8.9 0.7 copy-start.1
  14.5 26.6 %copy-start.2 = (f32[64,32]{0,1:T(8,128)S(1)}, f32[64,32]{0,1:T(8,128)}, u32[]{:S(2)}) copy-start(f32[64,32]{0,1:T(8,128)} %param.13) | copy-start | bytes 24580
  14.5 26.6 %copy-start.4 = (f32[32]{0:T(128)S(1)}, f32[32]{0:T(128)}, u32[]{:S(2)}) copy-start(f32[32]{0:T(128)} %param.14) | copy-start | bytes 388
  18.0 8.6 %collective-permute-start.1 = (f32[72,640]{1,0:T(8,128)S(1)}, f32[72,640]{1,0:T(8,128)S(1)}, u32[]{:S(2)}, u32[]{:S(2)}) collective-permute-start(f32[72,640]{1,0:T(8,128)S(1)} %fusion.20), channel_id=1, source_target_pairs={{104,112},{112,120},{128,136},{136,144},{152,160},{160,168},{176,1... | collective-permute-start | bytes 552968 | tf_op jit(solution)/shard_map/ppermute | solution.py:248
  19.3 15.6 %collective-permute-start.2 = (f32[72,640]{1,0:T(8,128)S(1)}, f32[72,640]{1,0:T(8,128)S(1)}, u32[]{:S(2)}, u32[]{:S(2)}) collective-permute-start(f32[72,640]{1,0:T(8,128)S(1)} %fusion.20), channel_id=1, source_target_pairs={{104,120},{128,144},{152,168},{176,192},{200,216},{224,240},{248,2... | collective-permute-start | bytes 552968 | tf_op jit(solution)/shard_map/ppermute | solution.py:248
  20.6 15.0 %collective-permute-start.3 = (f32[32,640]{1,0:T(8,128)S(1)}, f32[32,640]{1,0:T(8,128)S(1)}, u32[]{:S(2)}, u32[]{:S(2)}) collective-permute-start(f32[32,640]{1,0:T(8,128)S(1)} %dynamic-slice_bitcast_fusion), channel_id=1, source_target_pairs={{96,112},{120,136},{144,160},{168,184},{192,208},{216,232},{240,25... | collective-permute-start | bytes 245768 | tf_op jit(solution)/shard_map/ppermute | solution.py:248
  21.3 15.0 %collective-permute-start.4 = (f32[32,640]{1,0:T(8,128)S(1)}, f32[32,640]{1,0:T(8,128)S(1)}, u32[]{:S(2)}, u32[]{:S(2)}) collective-permute-start(f32[32,640]{1,0:T(8,128)S(1)} %dynamic-slice_bitcast_fusion), channel_id=1, source_target_pairs={{96,120},{120,144},{144,168},{168,192},{192,216},{216,240},{240,26... | collective-permute-start | bytes 245768 | tf_op jit(solution)/shard_map/ppermute | solution.py:248
  36.9 4.1 %collective-permute-start.5 = (f32[208,640]{1,0:T(8,128)}, f32[208,640]{1,0:T(8,128)}, u32[]{:S(2)}, u32[]{:S(2)}) collective-permute-start(f32[208,640]{1,0:T(8,128)} %constant_dynamic-update-slice_fusion), channel_id=1, source_target_pairs={{0,1},{1,0},{2,3},{3,2},{4,5},{5,4},{6,7},{7,6},{8,9},{9,8},{10,11... | collective-permute-start | bytes 1597448 | tf_op jit(solution)/shard_map/ppermute | solution.py:277
  41.1 25.8 %copy-start.3 = (f32[640]{0:T(1024)S(1)}, f32[640]{0:T(1024)}, u32[]{:S(2)}) copy-start(f32[640]{0:T(1024)} %param.15) | copy-start | bytes 7684
  58.8 4.5 %copy-start = (f32[640,640]{1,0:T(8,128)S(1)}, f32[640,640]{1,0:T(8,128)}, u32[]{:S(2)}) copy-start(f32[640,640]{1,0:T(8,128)} %get-tuple-element.22) | copy-start | bytes 4915204 | tf_op jit(solution)/shard_map/cond

commit v15 on v12

--- a/solution.py
+++ b/solution.py
@@ -253,8 +253,8 @@
     half_rows = dims // 2
     packed_half = lax.dynamic_index_in_dim(packed, core, 0, keepdims=False)
     rim_half = lax.dynamic_slice_in_dim(states[-1], core * half_rows, half_rows, 0)
-    fetched = [sent(packed_half, d, lambda i, d=d: need(i) >= d) for d in range(1, stride)]
-    fetched += [sent(rim_half, e, lambda i, e=e: need(i) + 1 == e) for e in range(2, stride + 1)]
+    fetched = [sent(packed_half, d, lambda i: need(i) >= 1) for d in range(1, stride)]
+    fetched += [sent(rim_half, stride, lambda i: need(i) == stride - 1)]
     bundle = jnp.concatenate(fetched, axis=0)
     pairs = [(r, r ^ 1) for r in range(lax.axis_size("rows"))]
     other = lax.ppermute(bundle, "rows", pairs)
@@ -284,11 +284,8 @@
             return jnp.concatenate([first_half[lo:hi], second_half[lo:hi]], axis=0)
 
         packs = [packed] + [joined(i).reshape(packed.shape) for i in range(stride - 1)]
-        rim_parts = [joined(stride - 1 + i) for i in range(stride - 1)]
-        rims = [None] + [
-            (packs[d + 1][-1, :dims, :] if d + 1 < stride else 0.0) + rim_parts[d - 1]
-            for d in range(1, stride)
-        ]
+        rims = [None] + [packs[d + 1][-1, :dims, :] for d in range(1, stride - 1)]
+        rims.append(joined(stride - 1))
         previous = []
         current = []
         parents = []

time: 141 us -> 144 us (1.021)
  Pallas kernels: 79.6 us -> 82.1 us
  waiting for transfers between devices: 8.48 us -> 10 us
    pallas_call x1, Pallas kernels: 79.6 us -> 82.1 us  [chain(): pl.pallas_call(functools.partial(chain_kernel, steps, stride, head), out_...]
    ppermute x5 -> x4, waiting for transfers between devices: 8.48 us -> 10 us  [sent(): return lax.ppermute(block, 'tm', route)]
    ppermute x5 -> x4, starting transfers between devices: 5.83 us -> 5.17 us  [sent(): return lax.ppermute(block, 'tm', route)]
  transfers between devices with their start and end apart: 6 -> 5, of which waited for: 1 -> 2; matrix products, arithmetic and copies ran while one was open for 10% -> 9% of each run, Pallas kernels for 0% -> 0%
where the time goes in v15:
time: 144 us; the launch traced here: 143 us
  Pallas kernels  82.1 us (57%)
  matrix products  32.9 us (23%)
  waiting for transfers between devices  10 us (7%)
  starting transfers between devices  7.08 us (5%)
  other arithmetic  6.09 us (4%)
  local copies, waits for them, and re-layouts  4.59 us (3%)
    pallas_call x1, Pallas kernels, chain(): pl.pallas_call(functools.partial(chain_kernel, steps, stride, head), out_...  82.1 us
    dot_general x2, matrix products, transition(): lax.dot_general(previous, current, (((0,), (0,)), ((), ())), precision=hi...  12.9 us
    dot_general x3, matrix products, block_product(): jnp.dot(block, matrix, precision=lax.Precision.HIGH, preferred_element_ty...  11.6 us
    ppermute x4, waiting for transfers between devices, sent(): return lax.ppermute(block, 'tm', route)  10 us
    dot_general x1, matrix products, earlier(): lax.dot_general(weights_all[0::2], weights_all[1::2], (((2,), (1,)), ((0,...  6.65 us
    ppermute x4, starting transfers between devices, sent(): return lax.ppermute(block, 'tm', route)  5.17 us
  transfers between devices with their start and end apart: 5, of which 2 were waited for; matrix products, arithmetic and copies ran while one was open for 9% of the time, Pallas kernels for 0%

profile of v15, /device:TPU:504, one launch (start us, length us, event | category | flops | bytes accessed | tf_op | source)
XLA Modules:
  0.0 143.3 jit_solution(7633095471454746459)
XLA Ops:
  0.0 0.0 copy-start.6
  0.0 0.0 copy-start.3
  0.0 0.8 copy.12
  0.8 0.1 pad.24.clone
  0.9 0.8 maximum_bitcast_fusion.1
  1.7 0.7 convert_bitcast_fusion
  2.4 0.1 pad.21.clone
  2.4 1.0 fusion.20
  3.4 1.3 collective-permute-start.1
  4.7 1.3 collective-permute-start.2
  6.0 1.0 fusion.29
  7.1 1.3 collective-permute-start.3
  8.4 1.3 collective-permute-start
  9.7 1.3 fusion.16
  11.0 0.1 fusion.23
  11.1 0.1 fusion.22
  11.2 1.0 multiply_reduce_fusion.2
  12.2 6.2 %collective-permute-done = f32[64,640]{1,0:T(8,128)S(1)} collective-permute-done((f32[64,640]{1,0:T(8,128)S(1)}, f32[64,640]{1,0:T(8,128)S(1)}, u32[]{:S(2)}, u32[]{:S(2)}) %collective-permute-start) | collective-permute-done | bytes 163872 | tf_op jit(solution)/shard_map/ppermute | solution.py:248
  18.4 0.0 copy-start.1
  18.5 0.0 collective-permute-done.1
  18.5 0.7 constant_dynamic-update-slice_fusion.2
  19.2 3.8 %collective-permute-done.2 = f32[72,640]{1,0:T(8,128)S(1)} collective-permute-done((f32[72,640]{1,0:T(8,128)S(1)}, f32[72,640]{1,0:T(8,128)S(1)}, u32[]{:S(2)}, u32[]{:S(2)}) %collective-permute-start.2) | collective-permute-done | bytes 184352 | tf_op jit(solution)/shard_map/ppermute | solution.py:248
  23.0 0.7 constant_dynamic-update-slice_fusion.1
  23.7 0.0 collective-permute-done.3
  23.7 0.6 constant_dynamic-update-slice_fusion
  24.3 0.0 copy-done.1
  24.3 1.9 %collective-permute-start.4 = (f32[176,640]{1,0:T(8,128)}, f32[176,640]{1,0:T(8,128)}, u32[]{:S(2)}, u32[]{:S(2)}) collective-permute-start(f32[176,640]{1,0:T(8,128)} %constant_dynamic-update-slice_fusion), channel_id=1, source_target_pairs={{0,1},{1,0},{2,3},{3,2},{4,5},{5,4},{6,7},{7,6},{8,9},{9,8},{10,11... | collective-permute-start | bytes 1351688 | tf_op jit(solution)/shard_map/ppermute | solution.py:260
  26.2 0.0 copy-done.6
  26.2 0.0 copy-done.3
  26.2 5.0 %add_multiply_fusion.1.refs_0_ = f32[2,640,640]{2,1,0:T(8,128)S(1)} fusion(f32[2,64,640]{2,1,0:T(8,128)} %param.9, f32[2,640]{1,0:T(2,128)S(1)} %multiply_reduce_fusion.2, f32[2,640]{1,0:T(2,128)S(1)} %multiply_reduce_fusion.3, f32[2]{0:T(128)S(1)} %copy-done.6, s32[2,640]{1,0:T(2,128)S(1)} %copy-done.3, f32[2,640]{1,0:T(2,128)S(1)} %fusion.22, ...), kind=kOutput, calls=%fused_computation.34 | convolution fusion | flops 636600320 | bytes 3952648 | tf_op jit(solution)/shard_map/vmap()/dot_general | solution.py:24
  31.2 0.0 copy-start.2
  31.2 0.0 copy-start.5
  31.2 3.5 %fusion.12.refs_1_ = f32[640,640]{1,0:T(8,128)} fusion(f32[2,640,640]{2,1,0:T(8,128)S(1)} %add_multiply_fusion.1.refs_0_), kind=kOutput, calls=%fused_computation.37 | convolution fusion | flops 1572864000 | bytes 4915200 | tf_op jit(solution)/shard_map/dot_general | solution.py:209
  34.8 0.0 collective-permute-done.4
  34.8 0.0 copy-done.2
  34.8 0.0 copy-done.5
  34.8 0.0 copy-start.4
  34.8 25.8 %conditional.1 = (f32[2,640,640]{2,1,0:T(8,128)}, f32[640,640]{1,0:T(8,128)}) conditional(s32[]{:T(128)} %convert_element_type.20, () %tuple.13, (f32[32]{0:T(128)S(1)}, s32[]{:T(128)}, f32[176,640]{1,0:T(8,128)}, f32[176,640]{1,0:T(8,128)}, f32[64,32]{0,1:T(8,128)S(1)}, /*index=5*/f32[640,640]{1,0:T(8,128)}) %tuple.26), branch_computations={%region_4.5_spmd, %region_5.10_spmd} | conditional | flops 7630323200 | bytes 43920168 | solution.py:326
  35.0 1.2 broadcast_select_fusion.1
  36.2 0.1 fusion.26
  36.4 0.5 fusion.6
  37.0 0.1 fusion.9
  37.1 0.1 fusion.8
  37.3 0.1 multiply_reduce_fusion.1
  37.4 0.1 multiply_reduce_fusion
  37.5 0.2 slice_reduce_fusion.1
  37.7 0.2 slice_reduce_fusion
  37.8 0.1 pad_maximum_fusion.8
  37.9 7.9 %add_multiply_fusion = f32[4,640,640]{2,1,0:T(8,128)S(1)} fusion(f32[4,640]{1,0:T(4,128)S(1)} %multiply_reduce_fusion, f32[4,640]{1,0:T(4,128)S(1)} %multiply_reduce_fusion.1, f32[4]{0:T(128)S(1)} %pad_maximum_fusion.8, s32[4,640]{1,0:T(4,128)S(1)} %maximum_convert_fusion, f32[4,640]{1,0:T(4,128)S(1)} %fusion.8, f32[2,64,640]{2,1,0:T(8,128)S(1)} %slice.101, ...), kind=kOutput, calls=%fused_computation | convolution fusion | flops 1273692160 | bytes 7905296 | tf_op jit(solution)/shard_map/cond/branch_1_fun/vmap()/dot_general | solution.py:24
  45.8 6.6 %fusion = f32[2,640,640]{2,1,0:T(8,128)} fusion(f32[4,640,640]{2,1,0:T(8,128)S(1)} %add_multiply_fusion), kind=kOutput, calls=%fused_computation.2 | convolution fusion | flops 3145728000 | bytes 9830400 | tf_op jit(solution)/shard_map/cond/branch_1_fun/dot_general | solution.py:310
  52.5 0.0 copy-start
  52.5 4.5 %fusion.3 = f32[640,640]{1,0:T(8,128)S(1)} fusion(f32[2,640,640]{2,1,0:T(8,128)} %fusion), kind=kOutput, calls=%fused_computation.6 | convolution fusion | flops 1572864000 | bytes 4915200 | tf_op jit(solution)/shard_map/cond/branch_1_fun/dot_general | solution.py:209
  56.9 0.0 copy-done
  56.9 3.6 %fusion.30 = f32[640,640]{1,0:T(8,128)} fusion(f32[640,640]{1,0:T(8,128)S(1)} %fusion.3, f32[640,640]{1,0:T(8,128)S(1)} %copy-done), kind=kOutput, calls=%fused_computation.72 | convolution fusion | flops 1572864000 | bytes 4915200 | tf_op jit(solution)/shard_map/cond/branch_1_fun/dot_general | solution.py:209
  60.6 0.0 copy-done.4
  60.6 82.1 %shard_map.73 = f32[8,640]{1,0:T(8,128)S(1)} custom-call(f32[2,640,640]{2,1,0:T(8,128)S(1)} %add_multiply_fusion.1.refs_0_, f32[640,640]{1,0:T(8,128)} %fusion.12.refs_1_, f32[2,640,640]{2,1,0:T(8,128)} %get-tuple-element.25.refs_2_, f32[640,640]{1,0:T(8,128)} %get-tuple-element.26.refs_3_, f32[8,640]{1,0:T(8,128)S(1)} %broadcast_in_dim.17.refs_4_), custom_call_target="tpu_custom_call" | custom-call | tf_op jit(solution)/shard_map/pallas_call | solution.py:186
  142.7 0.6 fusion.24
  (25 shorter events, 0.3 us)
Async XLA Ops:
  0.0 26.2 %copy-start.6 = (f32[2]{0:T(128)S(1)}, f32[2]{0:T(128)}, u32[]{:S(2)}) copy-start(f32[2]{0:T(128)} %param.12) | copy-start | bytes 28
  0.0 26.2 %copy-start.3 = (s32[2,640]{1,0:T(2,128)S(1)}, s32[2,640]{1,0:T(2,128)}, u32[]{:S(2)}) copy-start(s32[2,640]{1,0:T(2,128)} %param.10) | copy-start | bytes 15364
  3.4 15.0 %collective-permute-start.1 = (f32[72,640]{1,0:T(8,128)S(1)}, f32[72,640]{1,0:T(8,128)S(1)}, u32[]{:S(2)}, u32[]{:S(2)}) collective-permute-start(f32[72,640]{1,0:T(8,128)S(1)} %fusion.20), channel_id=1, source_target_pairs={{104,112},{112,120},{128,136},{136,144},{152,160},{160,168},{176,1... | collective-permute-start | bytes 552968 | tf_op jit(solution)/shard_map/ppermute | solution.py:248
  4.7 18.2 %collective-permute-start.2 = (f32[72,640]{1,0:T(8,128)S(1)}, f32[72,640]{1,0:T(8,128)S(1)}, u32[]{:S(2)}, u32[]{:S(2)}) collective-permute-start(f32[72,640]{1,0:T(8,128)S(1)} %fusion.20), channel_id=1, source_target_pairs={{96,112},{104,120},{120,136},{128,144},{144,160},{152,168},{168,18... | collective-permute-start | bytes 552968 | tf_op jit(solution)/shard_map/ppermute | solution.py:248
  7.1 16.6 %collective-permute-start.3 = (f32[32,640]{1,0:T(8,128)S(1)}, f32[32,640]{1,0:T(8,128)S(1)}, u32[]{:S(2)}, u32[]{:S(2)}) collective-permute-start(f32[32,640]{1,0:T(8,128)S(1)} %dynamic-slice_bitcast_fusion), channel_id=1, source_target_pairs={{96,120},{120,144},{144,168},{168,192},{192,216},{216,240},{240,26... | collective-permute-start | bytes 245768 | tf_op jit(solution)/shard_map/ppermute | solution.py:248
  8.4 10.0 %collective-permute-start = (f32[64,640]{1,0:T(8,128)S(1)}, f32[64,640]{1,0:T(8,128)S(1)}, u32[]{:S(2)}, u32[]{:S(2)}) collective-permute-start(f32[64,640]{1,0:T(8,128)S(1)} %get-tuple-element.38), channel_id=1, source_target_pairs={{0,8},{8,16},{16,24},{24,32},{32,40},{40,48},{48,56},{56,64},{64,7... | collective-permute-start | bytes 491528 | tf_op jit(solution)/shard_map/ppermute | solution.py:248
  18.4 5.9 %copy-start.1 = (f32[64,640]{1,0:T(8,128)}, f32[64,640]{1,0:T(8,128)S(1)}, u32[]{:S(2)}) copy-start(f32[64,640]{1,0:T(8,128)S(1)} %collective-permute-done) | copy-start | bytes 491524
  24.3 10.5 %collective-permute-start.4 = (f32[176,640]{1,0:T(8,128)}, f32[176,640]{1,0:T(8,128)}, u32[]{:S(2)}, u32[]{:S(2)}) collective-permute-start(f32[176,640]{1,0:T(8,128)} %constant_dynamic-update-slice_fusion), channel_id=1, source_target_pairs={{0,1},{1,0},{2,3},{3,2},{4,5},{5,4},{6,7},{7,6},{8,9},{9,8},{10,11... | collective-permute-start | bytes 1351688 | tf_op jit(solution)/shard_map/ppermute | solution.py:260
  31.2 3.5 %copy-start.2 = (f32[64,32]{0,1:T(8,128)S(1)}, f32[64,32]{0,1:T(8,128)}, u32[]{:S(2)}) copy-start(f32[64,32]{0,1:T(8,128)} %param.13) | copy-start | bytes 24580
  31.2 3.5 %copy-start.5 = (f32[32]{0:T(128)S(1)}, f32[32]{0:T(128)}, u32[]{:S(2)}) copy-start(f32[32]{0:T(128)} %param.14) | copy-start | bytes 388
  34.8 25.8 %copy-start.4 = (f32[640]{0:T(1024)S(1)}, f32[640]{0:T(1024)}, u32[]{:S(2)}) copy-start(f32[640]{0:T(1024)} %param.15) | copy-start | bytes 7684
  52.5 4.5 %copy-start = (f32[640,640]{1,0:T(8,128)S(1)}, f32[640,640]{1,0:T(8,128)}, u32[]{:S(2)}) copy-start(f32[640,640]{1,0:T(8,128)} %get-tuple-element.22) | copy-start | bytes 4915204 | tf_op jit(solution)/shard_map/cond

commit v16 on v12

--- a/solution.py
+++ b/solution.py
@@ -128,7 +128,7 @@
 
     def send_all(v):
         send_buf[...] = v
-        for d in range(1, stride + 1):
+        for d in range(stride, 0, -1):
             @pl.when(d <= sends)
             def _():
                 copies[d - 1].start()

time: 141 us -> 140 us (level)
  no operation moved by 1% of the time
where the time goes in v16:
time: 140 us
  Pallas kernels  78.7 us (56%)
  matrix products  32.9 us (24%)
  waiting for transfers between devices  8.48 us (6%)
  starting transfers between devices  7.74 us (6%)
  other arithmetic  6.2 us (4%)
  local copies, waits for them, and re-layouts  5.22 us (4%)
    pallas_call x1, Pallas kernels, chain(): pl.pallas_call(functools.partial(chain_kernel, steps, stride, head), out_...  78.7 us
    dot_general x2, matrix products, transition(): lax.dot_general(previous, current, (((0,), (0,)), ((), ())), precision=hi...  12.9 us
    dot_general x3, matrix products, block_product(): jnp.dot(block, matrix, precision=lax.Precision.HIGH, preferred_element_ty...  11.6 us
    ppermute x5, waiting for transfers between devices, sent(): return lax.ppermute(block, 'tm', route)  8.48 us
    dot_general x1, matrix products, earlier(): lax.dot_general(weights_all[0::2], weights_all[1::2], (((2,), (1,)), ((0,...  6.65 us
    ppermute x5, starting transfers between devices, sent(): return lax.ppermute(block, 'tm', route)  5.83 us
  transfers between devices with their start and end apart: 6, of which 1 were waited for; matrix products, arithmetic and copies ran while one was open for 10% of the time, Pallas kernels for 0%

profile of v16, /device:TPU:504, one launch (start us, length us, event | category | flops | bytes accessed | tf_op | source)
XLA Modules:
  0.0 139.8 jit_solution(6493165508425129409)
XLA Ops:
  0.0 0.0 copy-start.6
  0.0 0.0 copy-start.3
  0.0 0.8 copy.12
  0.8 0.1 pad.26.clone
  0.9 0.8 maximum_bitcast_fusion.1
  1.7 0.7 convert_bitcast_fusion
  2.4 0.1 pad.23.clone
  2.4 1.0 fusion.20
  3.4 1.3 collective-permute-start.1
  4.7 1.3 collective-permute-start.2
  6.0 1.0 fusion.28
  7.1 0.7 collective-permute-start.3
  7.8 1.3 collective-permute-start.4
  9.1 1.3 collective-permute-start
  10.4 1.3 fusion.16
  11.7 0.1 fusion.23
  11.8 0.1 fusion.22
  11.9 1.0 multiply_reduce_fusion.2
  12.9 8.5 %collective-permute-done = f32[64,640]{1,0:T(8,128)S(1)} collective-permute-done((f32[64,640]{1,0:T(8,128)S(1)}, f32[64,640]{1,0:T(8,128)S(1)}, u32[]{:S(2)}, u32[]{:S(2)}) %collective-permute-start) | collective-permute-done | bytes 163872 | tf_op jit(solution)/shard_map/ppermute | solution.py:248
  21.4 0.0 copy-start.1
  21.4 0.0 collective-permute-done.1
  21.4 0.7 constant_dynamic-update-slice_fusion.3
  22.1 0.0 collective-permute-done.2
  22.1 0.7 constant_dynamic-update-slice_fusion.2
  22.8 0.0 collective-permute-done.3
  22.8 0.6 constant_dynamic-update-slice_fusion.1
  23.5 0.0 collective-permute-done.4
  23.5 0.6 constant_dynamic-update-slice_fusion
  24.1 0.0 copy-done.1
  24.1 1.9 %collective-permute-start.5 = (f32[208,640]{1,0:T(8,128)}, f32[208,640]{1,0:T(8,128)}, u32[]{:S(2)}, u32[]{:S(2)}) collective-permute-start(f32[208,640]{1,0:T(8,128)} %constant_dynamic-update-slice_fusion), channel_id=1, source_target_pairs={{0,1},{1,0},{2,3},{3,2},{4,5},{5,4},{6,7},{7,6},{8,9},{9,8},{10,11... | collective-permute-start | bytes 1597448 | tf_op jit(solution)/shard_map/ppermute | solution.py:260
  26.0 0.0 copy-done.6
  26.0 0.0 copy-done.3
  26.0 5.0 %add_multiply_fusion.1.refs_0_ = f32[2,640,640]{2,1,0:T(8,128)S(1)} fusion(f32[2,64,640]{2,1,0:T(8,128)} %param.9, f32[2,640]{1,0:T(2,128)S(1)} %multiply_reduce_fusion.2, f32[2,640]{1,0:T(2,128)S(1)} %multiply_reduce_fusion.3, f32[2]{0:T(128)S(1)} %copy-done.6, s32[2,640]{1,0:T(2,128)S(1)} %copy-done.3, f32[2,640]{1,0:T(2,128)S(1)} %fusion.22, ...), kind=kOutput, calls=%fused_computation.37 | convolution fusion | flops 636600320 | bytes 3952648 | tf_op jit(solution)/shard_map/vmap()/dot_general | solution.py:24
  31.0 0.0 copy-start.2
  31.0 0.0 copy-start.5
  31.0 3.5 %fusion.12.refs_1_ = f32[640,640]{1,0:T(8,128)} fusion(f32[2,640,640]{2,1,0:T(8,128)S(1)} %add_multiply_fusion.1.refs_0_), kind=kOutput, calls=%fused_computation.40 | convolution fusion | flops 1572864000 | bytes 4915200 | tf_op jit(solution)/shard_map/dot_general | solution.py:209
  34.5 0.0 collective-permute-done.5
  34.5 0.0 copy-done.2
  34.6 0.0 copy-done.5
  34.6 0.0 copy-start.4
  34.6 25.9 %conditional.1 = (f32[2,640,640]{2,1,0:T(8,128)}, f32[640,640]{1,0:T(8,128)}) conditional(s32[]{:T(128)} %convert_element_type.20, () %tuple.13, (f32[32]{0:T(128)S(1)}, s32[]{:T(128)}, f32[208,640]{1,0:T(8,128)}, f32[208,640]{1,0:T(8,128)}, f32[64,32]{0,1:T(8,128)S(1)}, /*index=5*/f32[640,640]{1,0:T(8,128)}) %tuple.30), branch_computations={%region_4.5_spmd, %region_5.10_spmd} | conditional | flops 7630446080 | bytes 44739368 | solution.py:329
  34.8 1.3 broadcast_select_fusion.1
  36.1 0.1 fusion.26
  36.3 0.5 fusion.6
  36.8 0.1 fusion.9
  36.9 0.1 fusion.8
  37.2 0.1 multiply_reduce_fusion.1
  37.2 0.1 multiply_reduce_fusion
  37.4 0.2 slice_reduce_fusion.1
  37.5 0.2 slice_reduce_fusion
  37.7 0.1 pad_maximum_fusion.8
  37.8 7.9 %add_multiply_fusion = f32[4,640,640]{2,1,0:T(8,128)S(1)} fusion(f32[4,640]{1,0:T(4,128)S(1)} %multiply_reduce_fusion, f32[4,640]{1,0:T(4,128)S(1)} %multiply_reduce_fusion.1, f32[4]{0:T(128)S(1)} %pad_maximum_fusion.8, s32[4,640]{1,0:T(4,128)S(1)} %maximum_convert_fusion, f32[4,640]{1,0:T(4,128)S(1)} %fusion.8, f32[2,64,640]{2,1,0:T(8,128)S(1)} %slice.107, ...), kind=kOutput, calls=%fused_computation | convolution fusion | flops 1273692160 | bytes 7905296 | tf_op jit(solution)/shard_map/cond/branch_1_fun/vmap()/dot_general | solution.py:24
  45.7 6.6 %fusion = f32[2,640,640]{2,1,0:T(8,128)} fusion(f32[4,640,640]{2,1,0:T(8,128)S(1)} %add_multiply_fusion), kind=kOutput, calls=%fused_computation.2 | convolution fusion | flops 3145728000 | bytes 9830400 | tf_op jit(solution)/shard_map/cond/branch_1_fun/dot_general | solution.py:313
  52.3 0.0 copy-start
  52.3 4.5 %fusion.3 = f32[640,640]{1,0:T(8,128)S(1)} fusion(f32[2,640,640]{2,1,0:T(8,128)} %fusion), kind=kOutput, calls=%fused_computation.6 | convolution fusion | flops 1572864000 | bytes 4915200 | tf_op jit(solution)/shard_map/cond/branch_1_fun/dot_general | solution.py:209
  56.8 0.0 copy-done
  56.8 3.6 %fusion.29 = f32[640,640]{1,0:T(8,128)} fusion(f32[640,640]{1,0:T(8,128)S(1)} %fusion.3, f32[640,640]{1,0:T(8,128)S(1)} %copy-done), kind=kOutput, calls=%fused_computation.75 | convolution fusion | flops 1572864000 | bytes 4915200 | tf_op jit(solution)/shard_map/cond/branch_1_fun/dot_general | solution.py:209
  60.4 0.0 copy-done.4
  60.4 78.7 %shard_map.73 = f32[8,640]{1,0:T(8,128)S(1)} custom-call(f32[2,640,640]{2,1,0:T(8,128)S(1)} %add_multiply_fusion.1.refs_0_, f32[640,640]{1,0:T(8,128)} %fusion.12.refs_1_, f32[2,640,640]{2,1,0:T(8,128)} %get-tuple-element.25.refs_2_, f32[640,640]{1,0:T(8,128)} %get-tuple-element.26.refs_3_, f32[8,640]{1,0:T(8,128)S(1)} %broadcast_in_dim.17.refs_4_), custom_call_target="tpu_custom_call" | custom-call | tf_op jit(solution)/shard_map/pallas_call | solution.py:186
  139.2 0.6 fusion.24
  (24 shorter events, 0.3 us)
Async XLA Ops:
  0.0 26.0 %copy-start.6 = (f32[2]{0:T(128)S(1)}, f32[2]{0:T(128)}, u32[]{:S(2)}) copy-start(f32[2]{0:T(128)} %param.12) | copy-start | bytes 28
  0.0 26.0 %copy-start.3 = (s32[2,640]{1,0:T(2,128)S(1)}, s32[2,640]{1,0:T(2,128)}, u32[]{:S(2)}) copy-start(s32[2,640]{1,0:T(2,128)} %param.10) | copy-start | bytes 15364
  3.4 18.0 %collective-permute-start.1 = (f32[72,640]{1,0:T(8,128)S(1)}, f32[72,640]{1,0:T(8,128)S(1)}, u32[]{:S(2)}, u32[]{:S(2)}) collective-permute-start(f32[72,640]{1,0:T(8,128)S(1)} %fusion.20), channel_id=1, source_target_pairs={{104,112},{112,120},{128,136},{136,144},{152,160},{160,168},{176,1... | collective-permute-start | bytes 552968 | tf_op jit(solution)/shard_map/ppermute | solution.py:248
  4.7 17.4 %collective-permute-start.2 = (f32[72,640]{1,0:T(8,128)S(1)}, f32[72,640]{1,0:T(8,128)S(1)}, u32[]{:S(2)}, u32[]{:S(2)}) collective-permute-start(f32[72,640]{1,0:T(8,128)S(1)} %fusion.20), channel_id=1, source_target_pairs={{104,120},{128,144},{152,168},{176,192},{200,216},{224,240},{248,2... | collective-permute-start | bytes 552968 | tf_op jit(solution)/shard_map/ppermute | solution.py:248
  7.1 15.7 %collective-permute-start.3 = (f32[32,640]{1,0:T(8,128)S(1)}, f32[32,640]{1,0:T(8,128)S(1)}, u32[]{:S(2)}, u32[]{:S(2)}) collective-permute-start(f32[32,640]{1,0:T(8,128)S(1)} %dynamic-slice_bitcast_fusion), channel_id=1, source_target_pairs={{96,112},{120,136},{144,160},{168,184},{192,208},{216,232},{240,25... | collective-permute-start | bytes 245768 | tf_op jit(solution)/shard_map/ppermute | solution.py:248
  7.8 15.7 %collective-permute-start.4 = (f32[32,640]{1,0:T(8,128)S(1)}, f32[32,640]{1,0:T(8,128)S(1)}, u32[]{:S(2)}, u32[]{:S(2)}) collective-permute-start(f32[32,640]{1,0:T(8,128)S(1)} %dynamic-slice_bitcast_fusion), channel_id=1, source_target_pairs={{96,120},{120,144},{144,168},{168,192},{192,216},{216,240},{240,26... | collective-permute-start | bytes 245768 | tf_op jit(solution)/shard_map/ppermute | solution.py:248
  9.1 12.3 %collective-permute-start = (f32[64,640]{1,0:T(8,128)S(1)}, f32[64,640]{1,0:T(8,128)S(1)}, u32[]{:S(2)}, u32[]{:S(2)}) collective-permute-start(f32[64,640]{1,0:T(8,128)S(1)} %get-tuple-element.44), channel_id=1, source_target_pairs={{0,8},{8,16},{16,24},{24,32},{32,40},{40,48},{48,56},{56,64},{64,7... | collective-permute-start | bytes 491528 | tf_op jit(solution)/shard_map/ppermute | solution.py:248
  21.4 2.7 %copy-start.1 = (f32[64,640]{1,0:T(8,128)}, f32[64,640]{1,0:T(8,128)S(1)}, u32[]{:S(2)}) copy-start(f32[64,640]{1,0:T(8,128)S(1)} %collective-permute-done) | copy-start | bytes 491524
  24.1 10.4 %collective-permute-start.5 = (f32[208,640]{1,0:T(8,128)}, f32[208,640]{1,0:T(8,128)}, u32[]{:S(2)}, u32[]{:S(2)}) collective-permute-start(f32[208,640]{1,0:T(8,128)} %constant_dynamic-update-slice_fusion), channel_id=1, source_target_pairs={{0,1},{1,0},{2,3},{3,2},{4,5},{5,4},{6,7},{7,6},{8,9},{9,8},{10,11... | collective-permute-start | bytes 1597448 | tf_op jit(solution)/shard_map/ppermute | solution.py:260
  31.0 3.5 %copy-start.2 = (f32[64,32]{0,1:T(8,128)S(1)}, f32[64,32]{0,1:T(8,128)}, u32[]{:S(2)}) copy-start(f32[64,32]{0,1:T(8,128)} %param.13) | copy-start | bytes 24580
  31.0 3.5 %copy-start.5 = (f32[32]{0:T(128)S(1)}, f32[32]{0:T(128)}, u32[]{:S(2)}) copy-start(f32[32]{0:T(128)} %param.14) | copy-start | bytes 388
  34.6 25.9 %copy-start.4 = (f32[640]{0:T(1024)S(1)}, f32[640]{0:T(1024)}, u32[]{:S(2)}) copy-start(f32[640]{0:T(1024)} %param.15) | copy-start | bytes 7684
  52.3 4.5 %copy-start = (f32[640,640]{1,0:T(8,128)S(1)}, f32[640,640]{1,0:T(8,128)}, u32[]{:S(2)}) copy-start(f32[640,640]{1,0:T(8,128)} %get-tuple-element.22) | copy-start | bytes 4915204 | tf_op jit(solution)/shard_map/cond

commit v17 on v16

--- a/solution.py
+++ b/solution.py
@@ -9,7 +9,7 @@
 
 MESH = pl.DeviceIdType.MESH
 STRIDE = 3
-HEAD = 12
+HEAD = 11
 
 
 def shifted(block, axis, distance):

time: 140 us -> 143 us (1.021)
  Pallas kernels: 78.7 us -> 86.4 us
  waiting for transfers between devices: 8.48 us -> 5.16 us
  starting transfers between devices: 7.74 us -> 5.88 us
    pallas_call x1, Pallas kernels: 78.7 us -> 86.4 us  [chain(): pl.pallas_call(functools.partial(chain_kernel, steps, stride, head), out_...]
    ppermute x5, waiting for transfers between devices: 8.48 us -> 5.15 us  [sent(): return lax.ppermute(block, 'tm', route)]
    ppermute x5, starting transfers between devices: 5.83 us -> 3.97 us  [sent(): return lax.ppermute(block, 'tm', route)]
where the time goes in v17:
time: 143 us; the launch traced here: 142 us
  Pallas kernels  86.4 us (60%)
  matrix products  32.9 us (23%)
  other arithmetic  6.2 us (4%)
  starting transfers between devices  5.88 us (4%)
  local copies, waits for them, and re-layouts  5.22 us (4%)
  waiting for transfers between devices  5.16 us (4%)
    pallas_call x1, Pallas kernels, chain(): pl.pallas_call(functools.partial(chain_kernel, steps, stride, head), out_...  86.4 us
    dot_general x2, matrix products, transition(): lax.dot_general(previous, current, (((0,), (0,)), ((), ())), precision=hi...  12.9 us
    dot_general x3, matrix products, block_product(): jnp.dot(block, matrix, precision=lax.Precision.HIGH, preferred_element_ty...  11.6 us
    dot_general x1, matrix products, earlier(): lax.dot_general(weights_all[0::2], weights_all[1::2], (((2,), (1,)), ((0,...  6.65 us
    ppermute x5, waiting for transfers between devices, sent(): return lax.ppermute(block, 'tm', route)  5.15 us
    ppermute x5, starting transfers between devices, sent(): return lax.ppermute(block, 'tm', route)  3.97 us
  transfers between devices with their start and end apart: 6, of which 1 were waited for; matrix products, arithmetic and copies ran while one was open for 10% of the time, Pallas kernels for 0%

profile of v17, /device:TPU:504, one launch (start us, length us, event | category | flops | bytes accessed | tf_op | source)
XLA Modules:
  0.0 142.4 jit_solution(18297033924774316413)
XLA Ops:
  0.0 0.0 copy-start.6
  0.0 0.0 copy-start.3
  0.0 0.8 copy.12
  0.8 0.1 pad.26.clone
  0.9 0.8 maximum_bitcast_fusion.1
  1.7 0.7 convert_bitcast_fusion
  2.4 0.1 pad.23.clone
  2.4 1.0 fusion.20
  3.4 0.7 collective-permute-start.1
  4.1 0.7 collective-permute-start.2
  4.8 1.0 fusion.28
  5.9 0.7 collective-permute-start.3
  6.5 0.7 collective-permute-start.4
  7.2 1.3 collective-permute-start
  8.5 1.3 fusion.16
  9.8 0.1 fusion.23
  9.9 0.1 fusion.22
  10.0 1.0 multiply_reduce_fusion.2
  11.1 5.1 %collective-permute-done = f32[64,640]{1,0:T(8,128)S(1)} collective-permute-done((f32[64,640]{1,0:T(8,128)S(1)}, f32[64,640]{1,0:T(8,128)S(1)}, u32[]{:S(2)}, u32[]{:S(2)}) %collective-permute-start) | collective-permute-done | bytes 163872 | tf_op jit(solution)/shard_map/ppermute | solution.py:248
  16.2 0.0 copy-start.1
  16.2 0.0 collective-permute-done.1
  16.2 0.7 constant_dynamic-update-slice_fusion.3
  16.9 0.0 collective-permute-done.2
  16.9 0.7 constant_dynamic-update-slice_fusion.2
  17.6 0.0 collective-permute-done.3
  17.6 0.6 constant_dynamic-update-slice_fusion.1
  18.3 0.0 collective-permute-done.4
  18.3 0.6 constant_dynamic-update-slice_fusion
  18.9 0.0 copy-done.1
  18.9 1.9 %collective-permute-start.5 = (f32[208,640]{1,0:T(8,128)}, f32[208,640]{1,0:T(8,128)}, u32[]{:S(2)}, u32[]{:S(2)}) collective-permute-start(f32[208,640]{1,0:T(8,128)} %constant_dynamic-update-slice_fusion), channel_id=1, source_target_pairs={{0,1},{1,0},{2,3},{3,2},{4,5},{5,4},{6,7},{7,6},{8,9},{9,8},{10,11... | collective-permute-start | bytes 1597448 | tf_op jit(solution)/shard_map/ppermute | solution.py:260
  20.8 0.0 copy-done.6
  20.8 0.0 copy-done.3
  20.8 5.0 %add_multiply_fusion.1.refs_0_ = f32[2,640,640]{2,1,0:T(8,128)S(1)} fusion(f32[2,64,640]{2,1,0:T(8,128)} %param.9, f32[2,640]{1,0:T(2,128)S(1)} %multiply_reduce_fusion.2, f32[2,640]{1,0:T(2,128)S(1)} %multiply_reduce_fusion.3, f32[2]{0:T(128)S(1)} %copy-done.6, s32[2,640]{1,0:T(2,128)S(1)} %copy-done.3, f32[2,640]{1,0:T(2,128)S(1)} %fusion.22, ...), kind=kOutput, calls=%fused_computation.37 | convolution fusion | flops 636600320 | bytes 3952648 | tf_op jit(solution)/shard_map/vmap()/dot_general | solution.py:24
  25.8 0.0 copy-start.2
  25.8 0.0 copy-start.5
  25.8 3.5 %fusion.12.refs_1_ = f32[640,640]{1,0:T(8,128)} fusion(f32[2,640,640]{2,1,0:T(8,128)S(1)} %add_multiply_fusion.1.refs_0_), kind=kOutput, calls=%fused_computation.40 | convolution fusion | flops 1572864000 | bytes 4915200 | tf_op jit(solution)/shard_map/dot_general | solution.py:209
  29.4 0.0 collective-permute-done.5
  29.4 0.0 copy-done.2
  29.4 0.0 copy-done.5
  29.4 0.0 copy-start.4
  29.4 25.9 %conditional.1 = (f32[2,640,640]{2,1,0:T(8,128)}, f32[640,640]{1,0:T(8,128)}) conditional(s32[]{:T(128)} %convert_element_type.20, () %tuple.13, (f32[32]{0:T(128)S(1)}, s32[]{:T(128)}, f32[208,640]{1,0:T(8,128)}, f32[208,640]{1,0:T(8,128)}, f32[64,32]{0,1:T(8,128)S(1)}, /*index=5*/f32[640,640]{1,0:T(8,128)}) %tuple.30), branch_computations={%region_4.5_spmd, %region_5.10_spmd} | conditional | flops 7630446080 | bytes 44739368 | solution.py:329
  29.6 1.3 broadcast_select_fusion.1
  30.9 0.1 fusion.26
  31.1 0.5 fusion.6
  31.6 0.1 fusion.9
  31.8 0.1 fusion.8
  32.0 0.1 multiply_reduce_fusion.1
  32.0 0.1 multiply_reduce_fusion
  32.2 0.2 slice_reduce_fusion.1
  32.4 0.2 slice_reduce_fusion
  32.5 0.1 pad_maximum_fusion.8
  32.6 7.9 %add_multiply_fusion = f32[4,640,640]{2,1,0:T(8,128)S(1)} fusion(f32[4,640]{1,0:T(4,128)S(1)} %multiply_reduce_fusion, f32[4,640]{1,0:T(4,128)S(1)} %multiply_reduce_fusion.1, f32[4]{0:T(128)S(1)} %pad_maximum_fusion.8, s32[4,640]{1,0:T(4,128)S(1)} %maximum_convert_fusion, f32[4,640]{1,0:T(4,128)S(1)} %fusion.8, f32[2,64,640]{2,1,0:T(8,128)S(1)} %slice.107, ...), kind=kOutput, calls=%fused_computation | convolution fusion | flops 1273692160 | bytes 7905296 | tf_op jit(solution)/shard_map/cond/branch_1_fun/vmap()/dot_general | solution.py:24
  40.5 6.6 %fusion = f32[2,640,640]{2,1,0:T(8,128)} fusion(f32[4,640,640]{2,1,0:T(8,128)S(1)} %add_multiply_fusion), kind=kOutput, calls=%fused_computation.2 | convolution fusion | flops 3145728000 | bytes 9830400 | tf_op jit(solution)/shard_map/cond/branch_1_fun/dot_general | solution.py:313
  47.1 0.0 copy-start
  47.1 4.5 %fusion.3 = f32[640,640]{1,0:T(8,128)S(1)} fusion(f32[2,640,640]{2,1,0:T(8,128)} %fusion), kind=kOutput, calls=%fused_computation.6 | convolution fusion | flops 1572864000 | bytes 4915200 | tf_op jit(solution)/shard_map/cond/branch_1_fun/dot_general | solution.py:209
  51.6 0.0 copy-done
  51.6 3.6 %fusion.29 = f32[640,640]{1,0:T(8,128)} fusion(f32[640,640]{1,0:T(8,128)S(1)} %fusion.3, f32[640,640]{1,0:T(8,128)S(1)} %copy-done), kind=kOutput, calls=%fused_computation.75 | convolution fusion | flops 1572864000 | bytes 4915200 | tf_op jit(solution)/shard_map/cond/branch_1_fun/dot_general | solution.py:209
  55.2 0.0 copy-done.4
  55.2 86.4 %shard_map.73 = f32[8,640]{1,0:T(8,128)S(1)} custom-call(f32[2,640,640]{2,1,0:T(8,128)S(1)} %add_multiply_fusion.1.refs_0_, f32[640,640]{1,0:T(8,128)} %fusion.12.refs_1_, f32[2,640,640]{2,1,0:T(8,128)} %get-tuple-element.25.refs_2_, f32[640,640]{1,0:T(8,128)} %get-tuple-element.26.refs_3_, f32[8,640]{1,0:T(8,128)S(1)} %broadcast_in_dim.17.refs_4_), custom_call_target="tpu_custom_call" | custom-call | tf_op jit(solution)/shard_map/pallas_call | solution.py:186
  141.7 0.6 fusion.24
  (24 shorter events, 0.3 us)
Async XLA Ops:
  0.0 20.8 %copy-start.6 = (f32[2]{0:T(128)S(1)}, f32[2]{0:T(128)}, u32[]{:S(2)}) copy-start(f32[2]{0:T(128)} %param.12) | copy-start | bytes 28
  0.0 20.8 %copy-start.3 = (s32[2,640]{1,0:T(2,128)S(1)}, s32[2,640]{1,0:T(2,128)}, u32[]{:S(2)}) copy-start(s32[2,640]{1,0:T(2,128)} %param.10) | copy-start | bytes 15364
  3.4 12.8 %collective-permute-start.1 = (f32[72,640]{1,0:T(8,128)S(1)}, f32[72,640]{1,0:T(8,128)S(1)}, u32[]{:S(2)}, u32[]{:S(2)}) collective-permute-start(f32[72,640]{1,0:T(8,128)S(1)} %fusion.20), channel_id=1, source_target_pairs={{96,104},{104,112},{120,128},{128,136},{144,152},{152,160},{168,17... | collective-permute-start | bytes 552968 | tf_op jit(solution)/shard_map/ppermute | solution.py:248
  4.1 12.8 %collective-permute-start.2 = (f32[72,640]{1,0:T(8,128)S(1)}, f32[72,640]{1,0:T(8,128)S(1)}, u32[]{:S(2)}, u32[]{:S(2)}) collective-permute-start(f32[72,640]{1,0:T(8,128)S(1)} %fusion.20), channel_id=1, source_target_pairs={{96,112},{120,136},{144,160},{168,184},{192,208},{216,232},{240,25... | collective-permute-start | bytes 552968 | tf_op jit(solution)/shard_map/ppermute | solution.py:248
  5.9 11.8 %collective-permute-start.3 = (f32[32,640]{1,0:T(8,128)S(1)}, f32[32,640]{1,0:T(8,128)S(1)}, u32[]{:S(2)}, u32[]{:S(2)}) collective-permute-start(f32[32,640]{1,0:T(8,128)S(1)} %dynamic-slice_bitcast_fusion), channel_id=1, source_target_pairs={{88,104},{112,128},{136,152},{160,176},{184,200},{208,224},{232,24... | collective-permute-start | bytes 245768 | tf_op jit(solution)/shard_map/ppermute | solution.py:248
  6.5 11.7 %collective-permute-start.4 = (f32[32,640]{1,0:T(8,128)S(1)}, f32[32,640]{1,0:T(8,128)S(1)}, u32[]{:S(2)}, u32[]{:S(2)}) collective-permute-start(f32[32,640]{1,0:T(8,128)S(1)} %dynamic-slice_bitcast_fusion), channel_id=1, source_target_pairs={{88,112},{112,136},{136,160},{160,184},{184,208},{208,232},{232,25... | collective-permute-start | bytes 245768 | tf_op jit(solution)/shard_map/ppermute | solution.py:248
  7.2 9.0 %collective-permute-start = (f32[64,640]{1,0:T(8,128)S(1)}, f32[64,640]{1,0:T(8,128)S(1)}, u32[]{:S(2)}, u32[]{:S(2)}) collective-permute-start(f32[64,640]{1,0:T(8,128)S(1)} %get-tuple-element.44), channel_id=1, source_target_pairs={{0,8},{8,16},{16,24},{24,32},{32,40},{40,48},{48,56},{56,64},{64,7... | collective-permute-start | bytes 491528 | tf_op jit(solution)/shard_map/ppermute | solution.py:248
  16.2 2.7 %copy-start.1 = (f32[64,640]{1,0:T(8,128)}, f32[64,640]{1,0:T(8,128)S(1)}, u32[]{:S(2)}) copy-start(f32[64,640]{1,0:T(8,128)S(1)} %collective-permute-done) | copy-start | bytes 491524
  18.9 10.4 %collective-permute-start.5 = (f32[208,640]{1,0:T(8,128)}, f32[208,640]{1,0:T(8,128)}, u32[]{:S(2)}, u32[]{:S(2)}) collective-permute-start(f32[208,640]{1,0:T(8,128)} %constant_dynamic-update-slice_fusion), channel_id=1, source_target_pairs={{0,1},{1,0},{2,3},{3,2},{4,5},{5,4},{6,7},{7,6},{8,9},{9,8},{10,11... | collective-permute-start | bytes 1597448 | tf_op jit(solution)/shard_map/ppermute | solution.py:260
  25.8 3.5 %copy-start.2 = (f32[64,32]{0,1:T(8,128)S(1)}, f32[64,32]{0,1:T(8,128)}, u32[]{:S(2)}) copy-start(f32[64,32]{0,1:T(8,128)} %param.13) | copy-start | bytes 24580
  25.8 3.5 %copy-start.5 = (f32[32]{0:T(128)S(1)}, f32[32]{0:T(128)}, u32[]{:S(2)}) copy-start(f32[32]{0:T(128)} %param.14) | copy-start | bytes 388
  29.4 25.9 %copy-start.4 = (f32[640]{0:T(1024)S(1)}, f32[640]{0:T(1024)}, u32[]{:S(2)}) copy-start(f32[640]{0:T(1024)} %param.15) | copy-start | bytes 7684
  47.1 4.5 %copy-start = (f32[640,640]{1,0:T(8,128)S(1)}, f32[640,640]{1,0:T(8,128)}, u32[]{:S(2)}) copy-start(f32[640,640]{1,0:T(8,128)} %get-tuple-element.22) | copy-start | bytes 4915204 | tf_op jit(solution)/shard_map/cond

commit v18 on v16

--- a/solution.py
+++ b/solution.py
@@ -134,7 +134,10 @@
                 copies[d - 1].start()
 
     loads[0].wait()
-    loads[1].wait()
+
+    @pl.when(tail_node)
+    def _():
+        loads[1].wait()
 
     @pl.when(me == 0)
     def _():
@@ -152,6 +155,10 @@
     @pl.when(tail_node)
     def _():
         send_all(normalized(vec_mat(out_ref[...], combined_ref[...])))
+
+    @pl.when(jnp.logical_not(tail_node))
+    def _():
+        loads[1].wait()
 
     for load in loads[4:]:
         load.wait()

time: 140 us -> 140 us (level)
  no operation moved by 1% of the time
where the time goes in v18:
time: 140 us
  Pallas kernels  78.7 us (56%)
  matrix products  32.9 us (24%)
  waiting for transfers between devices  8.48 us (6%)
  starting transfers between devices  7.74 us (6%)
  other arithmetic  6.2 us (4%)
  local copies, waits for them, and re-layouts  5.22 us (4%)
    pallas_call x1, Pallas kernels, chain(): pl.pallas_call(functools.partial(chain_kernel, steps, stride, head), out_...  78.7 us
    dot_general x2, matrix products, transition(): lax.dot_general(previous, current, (((0,), (0,)), ((), ())), precision=hi...  12.9 us
    dot_general x3, matrix products, block_product(): jnp.dot(block, matrix, precision=lax.Precision.HIGH, preferred_element_ty...  11.6 us
    ppermute x5, waiting for transfers between devices, sent(): return lax.ppermute(block, 'tm', route)  8.48 us
    dot_general x1, matrix products, earlier(): lax.dot_general(weights_all[0::2], weights_all[1::2], (((2,), (1,)), ((0,...  6.65 us
    ppermute x5, starting transfers between devices, sent(): return lax.ppermute(block, 'tm', route)  5.83 us
  transfers between devices with their start and end apart: 6, of which 1 were waited for; matrix products, arithmetic and copies ran while one was open for 10% of the time, Pallas kernels for 0%

profile of v18, /device:TPU:504, one launch (start us, length us, event | category | flops | bytes accessed | tf_op | source)
XLA Modules:
  0.0 139.8 jit_solution(16312186830828214781)
XLA Ops:
  0.0 0.0 copy-start.6
  0.0 0.0 copy-start.3
  0.0 0.8 copy.12
  0.8 0.1 pad.26.clone
  0.9 0.8 maximum_bitcast_fusion.1
  1.7 0.7 convert_bitcast_fusion
  2.4 0.1 pad.23.clone
  2.4 1.0 fusion.20
  3.4 1.3 collective-permute-start.1
  4.7 1.3 collective-permute-start.2
  6.0 1.0 fusion.28
  7.1 0.7 collective-permute-start.3
  7.8 1.3 collective-permute-start.4
  9.1 1.3 collective-permute-start
  10.4 1.3 fusion.16
  11.7 0.1 fusion.23
  11.8 0.1 fusion.22
  11.9 1.0 multiply_reduce_fusion.2
  12.9 8.5 %collective-permute-done = f32[64,640]{1,0:T(8,128)S(1)} collective-permute-done((f32[64,640]{1,0:T(8,128)S(1)}, f32[64,640]{1,0:T(8,128)S(1)}, u32[]{:S(2)}, u32[]{:S(2)}) %collective-permute-start) | collective-permute-done | bytes 163872 | tf_op jit(solution)/shard_map/ppermute | solution.py:255
  21.4 0.0 copy-start.1
  21.4 0.0 collective-permute-done.1
  21.4 0.7 constant_dynamic-update-slice_fusion.3
  22.1 0.0 collective-permute-done.2
  22.1 0.7 constant_dynamic-update-slice_fusion.2
  22.8 0.0 collective-permute-done.3
  22.8 0.6 constant_dynamic-update-slice_fusion.1
  23.5 0.0 collective-permute-done.4
  23.5 0.6 constant_dynamic-update-slice_fusion
  24.1 0.0 copy-done.1
  24.1 1.9 %collective-permute-start.5 = (f32[208,640]{1,0:T(8,128)}, f32[208,640]{1,0:T(8,128)}, u32[]{:S(2)}, u32[]{:S(2)}) collective-permute-start(f32[208,640]{1,0:T(8,128)} %constant_dynamic-update-slice_fusion), channel_id=1, source_target_pairs={{0,1},{1,0},{2,3},{3,2},{4,5},{5,4},{6,7},{7,6},{8,9},{9,8},{10,11... | collective-permute-start | bytes 1597448 | tf_op jit(solution)/shard_map/ppermute | solution.py:267
  26.0 0.0 copy-done.6
  26.0 0.0 copy-done.3
  26.0 5.0 %add_multiply_fusion.1.refs_0_ = f32[2,640,640]{2,1,0:T(8,128)S(1)} fusion(f32[2,64,640]{2,1,0:T(8,128)} %param.9, f32[2,640]{1,0:T(2,128)S(1)} %multiply_reduce_fusion.2, f32[2,640]{1,0:T(2,128)S(1)} %multiply_reduce_fusion.3, f32[2]{0:T(128)S(1)} %copy-done.6, s32[2,640]{1,0:T(2,128)S(1)} %copy-done.3, f32[2,640]{1,0:T(2,128)S(1)} %fusion.22, ...), kind=kOutput, calls=%fused_computation.37 | convolution fusion | flops 636600320 | bytes 3952648 | tf_op jit(solution)/shard_map/vmap()/dot_general | solution.py:24
  31.0 0.0 copy-start.2
  31.0 0.0 copy-start.5
  31.0 3.5 %fusion.12.refs_1_ = f32[640,640]{1,0:T(8,128)} fusion(f32[2,640,640]{2,1,0:T(8,128)S(1)} %add_multiply_fusion.1.refs_0_), kind=kOutput, calls=%fused_computation.40 | convolution fusion | flops 1572864000 | bytes 4915200 | tf_op jit(solution)/shard_map/dot_general | solution.py:216
  34.5 0.0 collective-permute-done.5
  34.5 0.0 copy-done.2
  34.6 0.0 copy-done.5
  34.6 0.0 copy-start.4
  34.6 25.9 %conditional.1 = (f32[2,640,640]{2,1,0:T(8,128)}, f32[640,640]{1,0:T(8,128)}) conditional(s32[]{:T(128)} %convert_element_type.20, () %tuple.13, (f32[32]{0:T(128)S(1)}, s32[]{:T(128)}, f32[208,640]{1,0:T(8,128)}, f32[208,640]{1,0:T(8,128)}, f32[64,32]{0,1:T(8,128)S(1)}, /*index=5*/f32[640,640]{1,0:T(8,128)}) %tuple.30), branch_computations={%region_4.5_spmd, %region_5.10_spmd} | conditional | flops 7630446080 | bytes 44739368 | solution.py:336
  34.8 1.3 broadcast_select_fusion.1
  36.1 0.1 fusion.26
  36.3 0.5 fusion.6
  36.8 0.1 fusion.9
  36.9 0.1 fusion.8
  37.2 0.1 multiply_reduce_fusion.1
  37.2 0.1 multiply_reduce_fusion
  37.4 0.2 slice_reduce_fusion.1
  37.5 0.2 slice_reduce_fusion
  37.7 0.1 pad_maximum_fusion.8
  37.8 7.9 %add_multiply_fusion = f32[4,640,640]{2,1,0:T(8,128)S(1)} fusion(f32[4,640]{1,0:T(4,128)S(1)} %multiply_reduce_fusion, f32[4,640]{1,0:T(4,128)S(1)} %multiply_reduce_fusion.1, f32[4]{0:T(128)S(1)} %pad_maximum_fusion.8, s32[4,640]{1,0:T(4,128)S(1)} %maximum_convert_fusion, f32[4,640]{1,0:T(4,128)S(1)} %fusion.8, f32[2,64,640]{2,1,0:T(8,128)S(1)} %slice.107, ...), kind=kOutput, calls=%fused_computation | convolution fusion | flops 1273692160 | bytes 7905296 | tf_op jit(solution)/shard_map/cond/branch_1_fun/vmap()/dot_general | solution.py:24
  45.7 6.6 %fusion = f32[2,640,640]{2,1,0:T(8,128)} fusion(f32[4,640,640]{2,1,0:T(8,128)S(1)} %add_multiply_fusion), kind=kOutput, calls=%fused_computation.2 | convolution fusion | flops 3145728000 | bytes 9830400 | tf_op jit(solution)/shard_map/cond/branch_1_fun/dot_general | solution.py:320
  52.3 0.0 copy-start
  52.3 4.5 %fusion.3 = f32[640,640]{1,0:T(8,128)S(1)} fusion(f32[2,640,640]{2,1,0:T(8,128)} %fusion), kind=kOutput, calls=%fused_computation.6 | convolution fusion | flops 1572864000 | bytes 4915200 | tf_op jit(solution)/shard_map/cond/branch_1_fun/dot_general | solution.py:216
  56.8 0.0 copy-done
  56.8 3.6 %fusion.29 = f32[640,640]{1,0:T(8,128)} fusion(f32[640,640]{1,0:T(8,128)S(1)} %fusion.3, f32[640,640]{1,0:T(8,128)S(1)} %copy-done), kind=kOutput, calls=%fused_computation.75 | convolution fusion | flops 1572864000 | bytes 4915200 | tf_op jit(solution)/shard_map/cond/branch_1_fun/dot_general | solution.py:216
  60.4 0.0 copy-done.4
  60.4 78.7 %shard_map.73 = f32[8,640]{1,0:T(8,128)S(1)} custom-call(f32[2,640,640]{2,1,0:T(8,128)S(1)} %add_multiply_fusion.1.refs_0_, f32[640,640]{1,0:T(8,128)} %fusion.12.refs_1_, f32[2,640,640]{2,1,0:T(8,128)} %get-tuple-element.25.refs_2_, f32[640,640]{1,0:T(8,128)} %get-tuple-element.26.refs_3_, f32[8,640]{1,0:T(8,128)S(1)} %broadcast_in_dim.17.refs_4_), custom_call_target="tpu_custom_call" | custom-call | tf_op jit(solution)/shard_map/pallas_call | solution.py:193
  139.2 0.6 fusion.24
  (24 shorter events, 0.3 us)
Async XLA Ops:
  0.0 26.0 %copy-start.6 = (f32[2]{0:T(128)S(1)}, f32[2]{0:T(128)}, u32[]{:S(2)}) copy-start(f32[2]{0:T(128)} %param.12) | copy-start | bytes 28
  0.0 26.0 %copy-start.3 = (s32[2,640]{1,0:T(2,128)S(1)}, s32[2,640]{1,0:T(2,128)}, u32[]{:S(2)}) copy-start(s32[2,640]{1,0:T(2,128)} %param.10) | copy-start | bytes 15364
  3.4 18.0 %collective-permute-start.1 = (f32[72,640]{1,0:T(8,128)S(1)}, f32[72,640]{1,0:T(8,128)S(1)}, u32[]{:S(2)}, u32[]{:S(2)}) collective-permute-start(f32[72,640]{1,0:T(8,128)S(1)} %fusion.20), channel_id=1, source_target_pairs={{104,112},{112,120},{128,136},{136,144},{152,160},{160,168},{176,1... | collective-permute-start | bytes 552968 | tf_op jit(solution)/shard_map/ppermute | solution.py:255
  4.7 17.4 %collective-permute-start.2 = (f32[72,640]{1,0:T(8,128)S(1)}, f32[72,640]{1,0:T(8,128)S(1)}, u32[]{:S(2)}, u32[]{:S(2)}) collective-permute-start(f32[72,640]{1,0:T(8,128)S(1)} %fusion.20), channel_id=1, source_target_pairs={{104,120},{128,144},{152,168},{176,192},{200,216},{224,240},{248,2... | collective-permute-start | bytes 552968 | tf_op jit(solution)/shard_map/ppermute | solution.py:255
  7.1 15.7 %collective-permute-start.3 = (f32[32,640]{1,0:T(8,128)S(1)}, f32[32,640]{1,0:T(8,128)S(1)}, u32[]{:S(2)}, u32[]{:S(2)}) collective-permute-start(f32[32,640]{1,0:T(8,128)S(1)} %dynamic-slice_bitcast_fusion), channel_id=1, source_target_pairs={{96,112},{120,136},{144,160},{168,184},{192,208},{216,232},{240,25... | collective-permute-start | bytes 245768 | tf_op jit(solution)/shard_map/ppermute | solution.py:255
  7.8 15.7 %collective-permute-start.4 = (f32[32,640]{1,0:T(8,128)S(1)}, f32[32,640]{1,0:T(8,128)S(1)}, u32[]{:S(2)}, u32[]{:S(2)}) collective-permute-start(f32[32,640]{1,0:T(8,128)S(1)} %dynamic-slice_bitcast_fusion), channel_id=1, source_target_pairs={{96,120},{120,144},{144,168},{168,192},{192,216},{216,240},{240,26... | collective-permute-start | bytes 245768 | tf_op jit(solution)/shard_map/ppermute | solution.py:255
  9.1 12.3 %collective-permute-start = (f32[64,640]{1,0:T(8,128)S(1)}, f32[64,640]{1,0:T(8,128)S(1)}, u32[]{:S(2)}, u32[]{:S(2)}) collective-permute-start(f32[64,640]{1,0:T(8,128)S(1)} %get-tuple-element.44), channel_id=1, source_target_pairs={{0,8},{8,16},{16,24},{24,32},{32,40},{40,48},{48,56},{56,64},{64,7... | collective-permute-start | bytes 491528 | tf_op jit(solution)/shard_map/ppermute | solution.py:255
  21.4 2.7 %copy-start.1 = (f32[64,640]{1,0:T(8,128)}, f32[64,640]{1,0:T(8,128)S(1)}, u32[]{:S(2)}) copy-start(f32[64,640]{1,0:T(8,128)S(1)} %collective-permute-done) | copy-start | bytes 491524
  24.1 10.4 %collective-permute-start.5 = (f32[208,640]{1,0:T(8,128)}, f32[208,640]{1,0:T(8,128)}, u32[]{:S(2)}, u32[]{:S(2)}) collective-permute-start(f32[208,640]{1,0:T(8,128)} %constant_dynamic-update-slice_fusion), channel_id=1, source_target_pairs={{0,1},{1,0},{2,3},{3,2},{4,5},{5,4},{6,7},{7,6},{8,9},{9,8},{10,11... | collective-permute-start | bytes 1597448 | tf_op jit(solution)/shard_map/ppermute | solution.py:267
  31.0 3.5 %copy-start.2 = (f32[64,32]{0,1:T(8,128)S(1)}, f32[64,32]{0,1:T(8,128)}, u32[]{:S(2)}) copy-start(f32[64,32]{0,1:T(8,128)} %param.13) | copy-start | bytes 24580
  31.0 3.5 %copy-start.5 = (f32[32]{0:T(128)S(1)}, f32[32]{0:T(128)}, u32[]{:S(2)}) copy-start(f32[32]{0:T(128)} %param.14) | copy-start | bytes 388
  34.6 25.9 %copy-start.4 = (f32[640]{0:T(1024)S(1)}, f32[640]{0:T(1024)}, u32[]{:S(2)}) copy-start(f32[640]{0:T(1024)} %param.15) | copy-start | bytes 7684
  52.3 4.5 %copy-start = (f32[640,640]{1,0:T(8,128)S(1)}, f32[640,640]{1,0:T(8,128)}, u32[]{:S(2)}) copy-start(f32[640,640]{1,0:T(8,128)} %get-tuple-element.22) | copy-start | bytes 4915204 | tf_op jit(solution)/shard_map/cond

commit v19 on v18

--- a/solution.py
+++ b/solution.py
@@ -143,18 +143,28 @@
     def _():
         out_ref[...] = spread(normalized(prior_ref[0:1, :]), out_ref)
 
-    @pl.when(me > 0)
+    @pl.when(jnp.logical_and(me > 0, me <= head))
+    def _():
+        copies[0].wait_recv()
+        received = recv_buf[...]
+        send_all(normalized(vec_mat(received, block_ref[...])))
+        out_ref[...] = spread(received, out_ref)
+
+    @pl.when(me == 0)
+    def _():
+        send_all(normalized(vec_mat(out_ref[...], block_ref[...])))
+
+    @pl.when(tail_node)
+    def _():
+        copies[0].wait_recv()
+        received = recv_buf[...]
+        send_all(normalized(vec_mat(received, combined_ref[...])))
+        out_ref[...] = spread(received, out_ref)
+
+    @pl.when(jnp.logical_and(tail, jnp.logical_not(tail_node)))
     def _():
         copies[0].wait_recv()
         out_ref[...] = spread(recv_buf[...], out_ref)
-
-    @pl.when(me <= head)
-    def _():
-        send_all(normalized(vec_mat(out_ref[...], block_ref[...])))
-
-    @pl.when(tail_node)
-    def _():
-        send_all(normalized(vec_mat(out_ref[...], combined_ref[...])))
 
     @pl.when(jnp.logical_not(tail_node))
     def _():

time: 140 us -> 140 us (level)
  no operation moved by 1% of the time
where the time goes in v19:
time: 140 us
  Pallas kernels  78.5 us (56%)
  matrix products  32.9 us (24%)
  waiting for transfers between devices  8.48 us (6%)
  starting transfers between devices  7.74 us (6%)
  other arithmetic  6.2 us (4%)
  local copies, waits for them, and re-layouts  5.22 us (4%)
    pallas_call x1, Pallas kernels, chain(): pl.pallas_call(functools.partial(chain_kernel, steps, stride, head), out_...  78.5 us
    dot_general x2, matrix products, transition(): lax.dot_general(previous, current, (((0,), (0,)), ((), ())), precision=hi...  12.9 us
    dot_general x3, matrix products, block_product(): jnp.dot(block, matrix, precision=lax.Precision.HIGH, preferred_element_ty...  11.6 us
    ppermute x5, waiting for transfers between devices, sent(): return lax.ppermute(block, 'tm', route)  8.48 us
    dot_general x1, matrix products, earlier(): lax.dot_general(weights_all[0::2], weights_all[1::2], (((2,), (1,)), ((0,...  6.65 us
    ppermute x5, starting transfers between devices, sent(): return lax.ppermute(block, 'tm', route)  5.83 us
  transfers between devices with their start and end apart: 6, of which 1 were waited for; matrix products, arithmetic and copies ran while one was open for 10% of the time, Pallas kernels for 0%

profile of v19, /device:TPU:504, one launch (start us, length us, event | category | flops | bytes accessed | tf_op | source)
XLA Modules:
  0.0 139.6 jit_solution(3522183801740032050)
XLA Ops:
  0.0 0.0 copy-start.6
  0.0 0.0 copy-start.3
  0.0 0.8 copy.12
  0.8 0.1 pad.26.clone
  0.9 0.8 maximum_bitcast_fusion.1
  1.7 0.7 convert_bitcast_fusion
  2.4 0.1 pad.23.clone
  2.4 1.0 fusion.20
  3.4 1.3 collective-permute-start.1
  4.7 1.3 collective-permute-start.2
  6.0 1.0 fusion.28
  7.1 0.7 collective-permute-start.3
  7.8 1.3 collective-permute-start.4
  9.1 1.3 collective-permute-start
  10.4 1.3 fusion.16
  11.7 0.1 fusion.23
  11.8 0.1 fusion.22
  11.9 1.0 multiply_reduce_fusion.2
  12.9 8.5 %collective-permute-done = f32[64,640]{1,0:T(8,128)S(1)} collective-permute-done((f32[64,640]{1,0:T(8,128)S(1)}, f32[64,640]{1,0:T(8,128)S(1)}, u32[]{:S(2)}, u32[]{:S(2)}) %collective-permute-start) | collective-permute-done | bytes 163872 | tf_op jit(solution)/shard_map/ppermute | solution.py:265
  21.4 0.0 copy-start.1
  21.4 0.0 collective-permute-done.1
  21.4 0.7 constant_dynamic-update-slice_fusion.3
  22.1 0.0 collective-permute-done.2
  22.1 0.7 constant_dynamic-update-slice_fusion.2
  22.8 0.0 collective-permute-done.3
  22.8 0.6 constant_dynamic-update-slice_fusion.1
  23.5 0.0 collective-permute-done.4
  23.5 0.6 constant_dynamic-update-slice_fusion
  24.1 0.0 copy-done.1
  24.1 1.9 %collective-permute-start.5 = (f32[208,640]{1,0:T(8,128)}, f32[208,640]{1,0:T(8,128)}, u32[]{:S(2)}, u32[]{:S(2)}) collective-permute-start(f32[208,640]{1,0:T(8,128)} %constant_dynamic-update-slice_fusion), channel_id=1, source_target_pairs={{0,1},{1,0},{2,3},{3,2},{4,5},{5,4},{6,7},{7,6},{8,9},{9,8},{10,11... | collective-permute-start | bytes 1597448 | tf_op jit(solution)/shard_map/ppermute | solution.py:277
  26.0 0.0 copy-done.6
  26.0 0.0 copy-done.3
  26.0 5.0 %add_multiply_fusion.1.refs_0_ = f32[2,640,640]{2,1,0:T(8,128)S(1)} fusion(f32[2,64,640]{2,1,0:T(8,128)} %param.9, f32[2,640]{1,0:T(2,128)S(1)} %multiply_reduce_fusion.2, f32[2,640]{1,0:T(2,128)S(1)} %multiply_reduce_fusion.3, f32[2]{0:T(128)S(1)} %copy-done.6, s32[2,640]{1,0:T(2,128)S(1)} %copy-done.3, f32[2,640]{1,0:T(2,128)S(1)} %fusion.22, ...), kind=kOutput, calls=%fused_computation.37 | convolution fusion | flops 636600320 | bytes 3952648 | tf_op jit(solution)/shard_map/vmap()/dot_general | solution.py:24
  31.0 0.0 copy-start.2
  31.0 0.0 copy-start.5
  31.0 3.5 %fusion.12.refs_1_ = f32[640,640]{1,0:T(8,128)} fusion(f32[2,640,640]{2,1,0:T(8,128)S(1)} %add_multiply_fusion.1.refs_0_), kind=kOutput, calls=%fused_computation.40 | convolution fusion | flops 1572864000 | bytes 4915200 | tf_op jit(solution)/shard_map/dot_general | solution.py:226
  34.5 0.0 collective-permute-done.5
  34.5 0.0 copy-done.2
  34.6 0.0 copy-done.5
  34.6 0.0 copy-start.4
  34.6 25.9 %conditional.1 = (f32[2,640,640]{2,1,0:T(8,128)}, f32[640,640]{1,0:T(8,128)}) conditional(s32[]{:T(128)} %convert_element_type.20, () %tuple.13, (f32[32]{0:T(128)S(1)}, s32[]{:T(128)}, f32[208,640]{1,0:T(8,128)}, f32[208,640]{1,0:T(8,128)}, f32[64,32]{0,1:T(8,128)S(1)}, /*index=5*/f32[640,640]{1,0:T(8,128)}) %tuple.30), branch_computations={%region_4.5_spmd, %region_5.10_spmd} | conditional | flops 7630446080 | bytes 44739368 | solution.py:346
  34.8 1.3 broadcast_select_fusion.1
  36.1 0.1 fusion.26
  36.3 0.5 fusion.6
  36.8 0.1 fusion.9
  36.9 0.1 fusion.8
  37.2 0.1 multiply_reduce_fusion.1
  37.2 0.1 multiply_reduce_fusion
  37.4 0.2 slice_reduce_fusion.1
  37.5 0.2 slice_reduce_fusion
  37.7 0.1 pad_maximum_fusion.8
  37.8 7.9 %add_multiply_fusion = f32[4,640,640]{2,1,0:T(8,128)S(1)} fusion(f32[4,640]{1,0:T(4,128)S(1)} %multiply_reduce_fusion, f32[4,640]{1,0:T(4,128)S(1)} %multiply_reduce_fusion.1, f32[4]{0:T(128)S(1)} %pad_maximum_fusion.8, s32[4,640]{1,0:T(4,128)S(1)} %maximum_convert_fusion, f32[4,640]{1,0:T(4,128)S(1)} %fusion.8, f32[2,64,640]{2,1,0:T(8,128)S(1)} %slice.107, ...), kind=kOutput, calls=%fused_computation | convolution fusion | flops 1273692160 | bytes 7905296 | tf_op jit(solution)/shard_map/cond/branch_1_fun/vmap()/dot_general | solution.py:24
  45.7 6.6 %fusion = f32[2,640,640]{2,1,0:T(8,128)} fusion(f32[4,640,640]{2,1,0:T(8,128)S(1)} %add_multiply_fusion), kind=kOutput, calls=%fused_computation.2 | convolution fusion | flops 3145728000 | bytes 9830400 | tf_op jit(solution)/shard_map/cond/branch_1_fun/dot_general | solution.py:330
  52.3 0.0 copy-start
  52.3 4.5 %fusion.3 = f32[640,640]{1,0:T(8,128)S(1)} fusion(f32[2,640,640]{2,1,0:T(8,128)} %fusion), kind=kOutput, calls=%fused_computation.6 | convolution fusion | flops 1572864000 | bytes 4915200 | tf_op jit(solution)/shard_map/cond/branch_1_fun/dot_general | solution.py:226
  56.8 0.0 copy-done
  56.8 3.6 %fusion.29 = f32[640,640]{1,0:T(8,128)} fusion(f32[640,640]{1,0:T(8,128)S(1)} %fusion.3, f32[640,640]{1,0:T(8,128)S(1)} %copy-done), kind=kOutput, calls=%fused_computation.75 | convolution fusion | flops 1572864000 | bytes 4915200 | tf_op jit(solution)/shard_map/cond/branch_1_fun/dot_general | solution.py:226
  60.4 0.0 copy-done.4
  60.4 78.5 %shard_map.73 = f32[8,640]{1,0:T(8,128)S(1)} custom-call(f32[2,640,640]{2,1,0:T(8,128)S(1)} %add_multiply_fusion.1.refs_0_, f32[640,640]{1,0:T(8,128)} %fusion.12.refs_1_, f32[2,640,640]{2,1,0:T(8,128)} %get-tuple-element.25.refs_2_, f32[640,640]{1,0:T(8,128)} %get-tuple-element.26.refs_3_, f32[8,640]{1,0:T(8,128)S(1)} %broadcast_in_dim.17.refs_4_), custom_call_target="tpu_custom_call" | custom-call | tf_op jit(solution)/shard_map/pallas_call | solution.py:203
  139.0 0.6 fusion.24
  (24 shorter events, 0.3 us)
Async XLA Ops:
  0.0 26.0 %copy-start.6 = (f32[2]{0:T(128)S(1)}, f32[2]{0:T(128)}, u32[]{:S(2)}) copy-start(f32[2]{0:T(128)} %param.12) | copy-start | bytes 28
  0.0 26.0 %copy-start.3 = (s32[2,640]{1,0:T(2,128)S(1)}, s32[2,640]{1,0:T(2,128)}, u32[]{:S(2)}) copy-start(s32[2,640]{1,0:T(2,128)} %param.10) | copy-start | bytes 15364
  3.4 18.0 %collective-permute-start.1 = (f32[72,640]{1,0:T(8,128)S(1)}, f32[72,640]{1,0:T(8,128)S(1)}, u32[]{:S(2)}, u32[]{:S(2)}) collective-permute-start(f32[72,640]{1,0:T(8,128)S(1)} %fusion.20), channel_id=1, source_target_pairs={{104,112},{112,120},{128,136},{136,144},{152,160},{160,168},{176,1... | collective-permute-start | bytes 552968 | tf_op jit(solution)/shard_map/ppermute | solution.py:265
  4.7 17.4 %collective-permute-start.2 = (f32[72,640]{1,0:T(8,128)S(1)}, f32[72,640]{1,0:T(8,128)S(1)}, u32[]{:S(2)}, u32[]{:S(2)}) collective-permute-start(f32[72,640]{1,0:T(8,128)S(1)} %fusion.20), channel_id=1, source_target_pairs={{104,120},{128,144},{152,168},{176,192},{200,216},{224,240},{248,2... | collective-permute-start | bytes 552968 | tf_op jit(solution)/shard_map/ppermute | solution.py:265
  7.1 15.7 %collective-permute-start.3 = (f32[32,640]{1,0:T(8,128)S(1)}, f32[32,640]{1,0:T(8,128)S(1)}, u32[]{:S(2)}, u32[]{:S(2)}) collective-permute-start(f32[32,640]{1,0:T(8,128)S(1)} %dynamic-slice_bitcast_fusion), channel_id=1, source_target_pairs={{96,112},{120,136},{144,160},{168,184},{192,208},{216,232},{240,25... | collective-permute-start | bytes 245768 | tf_op jit(solution)/shard_map/ppermute | solution.py:265
  7.8 15.7 %collective-permute-start.4 = (f32[32,640]{1,0:T(8,128)S(1)}, f32[32,640]{1,0:T(8,128)S(1)}, u32[]{:S(2)}, u32[]{:S(2)}) collective-permute-start(f32[32,640]{1,0:T(8,128)S(1)} %dynamic-slice_bitcast_fusion), channel_id=1, source_target_pairs={{96,120},{120,144},{144,168},{168,192},{192,216},{216,240},{240,26... | collective-permute-start | bytes 245768 | tf_op jit(solution)/shard_map/ppermute | solution.py:265
  9.1 12.3 %collective-permute-start = (f32[64,640]{1,0:T(8,128)S(1)}, f32[64,640]{1,0:T(8,128)S(1)}, u32[]{:S(2)}, u32[]{:S(2)}) collective-permute-start(f32[64,640]{1,0:T(8,128)S(1)} %get-tuple-element.44), channel_id=1, source_target_pairs={{0,8},{8,16},{16,24},{24,32},{32,40},{40,48},{48,56},{56,64},{64,7... | collective-permute-start | bytes 491528 | tf_op jit(solution)/shard_map/ppermute | solution.py:265
  21.4 2.7 %copy-start.1 = (f32[64,640]{1,0:T(8,128)}, f32[64,640]{1,0:T(8,128)S(1)}, u32[]{:S(2)}) copy-start(f32[64,640]{1,0:T(8,128)S(1)} %collective-permute-done) | copy-start | bytes 491524
  24.1 10.4 %collective-permute-start.5 = (f32[208,640]{1,0:T(8,128)}, f32[208,640]{1,0:T(8,128)}, u32[]{:S(2)}, u32[]{:S(2)}) collective-permute-start(f32[208,640]{1,0:T(8,128)} %constant_dynamic-update-slice_fusion), channel_id=1, source_target_pairs={{0,1},{1,0},{2,3},{3,2},{4,5},{5,4},{6,7},{7,6},{8,9},{9,8},{10,11... | collective-permute-start | bytes 1597448 | tf_op jit(solution)/shard_map/ppermute | solution.py:277
  31.0 3.5 %copy-start.2 = (f32[64,32]{0,1:T(8,128)S(1)}, f32[64,32]{0,1:T(8,128)}, u32[]{:S(2)}) copy-start(f32[64,32]{0,1:T(8,128)} %param.13) | copy-start | bytes 24580
  31.0 3.5 %copy-start.5 = (f32[32]{0:T(128)S(1)}, f32[32]{0:T(128)}, u32[]{:S(2)}) copy-start(f32[32]{0:T(128)} %param.14) | copy-start | bytes 388
  34.6 25.9 %copy-start.4 = (f32[640]{0:T(1024)S(1)}, f32[640]{0:T(1024)}, u32[]{:S(2)}) copy-start(f32[640]{0:T(1024)} %param.15) | copy-start | bytes 7684
  52.3 4.5 %copy-start = (f32[640,640]{1,0:T(8,128)S(1)}, f32[640,640]{1,0:T(8,128)}, u32[]{:S(2)}) copy-start(f32[640,640]{1,0:T(8,128)} %get-tuple-element.22) | copy-start | bytes 4915204 | tf_op jit(solution)/shard_map/cond

commit v20 on v18

--- a/solution.py
+++ b/solution.py
@@ -327,13 +327,15 @@
         combined = block_product([products[d] for d in range(stride - 2, -1, -1)] + [block_own])
         return products, combined
 
-    def skipped(bundle, other):
-        return (
-            jnp.zeros((stride - 1, count, count), jnp.float32),
-            jnp.zeros((count, count), jnp.float32),
-        )
-
-    befores, combined = lax.cond(me > head, earlier, skipped, bundle, other)
+    def skipped(bundle, other, weights_own, block_own):
+        return weights_own, block_own
+
+    def tail_branch(bundle, other, weights_own, block_own):
+        return earlier(bundle, other)
+
+    befores, combined = lax.cond(
+        me > head, tail_branch, skipped, bundle, other, weights_own, block_own
+    )
 
     prior8 = jnp.broadcast_to(prior_weights[None, :], (8, count))
     weights = chain(weights_own, block_own, befores, combined, prior8, steps, stride, head)

time: 140 us -> 142 us (1.014)
  no operation moved by 1% of the time
where the time goes in v20:
time: 142 us; the launch traced here: 141 us
  Pallas kernels  78.7 us (55%)
  matrix products  34.2 us (24%)
  waiting for transfers between devices  8.48 us (6%)
  starting transfers between devices  7.74 us (5%)
  other arithmetic  6.2 us (4%)
  local copies, waits for them, and re-layouts  5.22 us (4%)
    pallas_call x1, Pallas kernels, chain(): pl.pallas_call(functools.partial(chain_kernel, steps, stride, head), out_...  78.7 us
    dot_general x3, matrix products, block_product(): jnp.dot(block, matrix, precision=lax.Precision.HIGH, preferred_element_ty...  12.9 us
    dot_general x2, matrix products, transition(): lax.dot_general(previous, current, (((0,), (0,)), ((), ())), precision=hi...  12.9 us
    ppermute x5, waiting for transfers between devices, sent(): return lax.ppermute(block, 'tm', route)  8.48 us
    dot_general x1, matrix products, earlier(): lax.dot_general(weights_all[0::2], weights_all[1::2], (((2,), (1,)), ((0,...  6.65 us
    ppermute x5, starting transfers between devices, sent(): return lax.ppermute(block, 'tm', route)  5.83 us
  transfers between devices with their start and end apart: 6, of which 1 were waited for; matrix products, arithmetic and copies ran while one was open for 10% of the time, Pallas kernels for 0%

profile of v20, /device:TPU:504, one launch (start us, length us, event | category | flops | bytes accessed | tf_op | source)
XLA Modules:
  0.0 141.1 jit_solution(10572810471536416349)
XLA Ops:
  0.0 0.0 copy-start.5
  0.0 0.0 copy-start.2
  0.0 0.8 copy.12
  0.8 0.1 pad.26.clone
  0.9 0.8 maximum_bitcast_fusion.1
  1.7 0.7 convert_bitcast_fusion
  2.4 0.1 pad.23.clone
  2.4 1.0 fusion.20
  3.4 1.3 collective-permute-start.1
  4.7 1.3 collective-permute-start.2
  6.0 1.0 fusion.28
  7.1 0.7 collective-permute-start.3
  7.8 1.3 collective-permute-start.4
  9.1 1.3 collective-permute-start
  10.4 1.3 fusion.16
  11.7 0.1 fusion.23
  11.8 0.1 fusion.22
  11.9 1.0 multiply_reduce_fusion.2
  12.9 8.5 %collective-permute-done = f32[64,640]{1,0:T(8,128)S(1)} collective-permute-done((f32[64,640]{1,0:T(8,128)S(1)}, f32[64,640]{1,0:T(8,128)S(1)}, u32[]{:S(2)}, u32[]{:S(2)}) %collective-permute-start) | collective-permute-done | bytes 163872 | tf_op jit(solution)/shard_map/ppermute | solution.py:255
  21.4 0.0 copy-start
  21.4 0.0 collective-permute-done.1
  21.4 0.7 constant_dynamic-update-slice_fusion.3
  22.1 0.0 collective-permute-done.2
  22.1 0.7 constant_dynamic-update-slice_fusion.2
  22.8 0.0 collective-permute-done.3
  22.8 0.6 constant_dynamic-update-slice_fusion.1
  23.5 0.0 collective-permute-done.4
  23.5 0.6 constant_dynamic-update-slice_fusion
  24.1 0.0 copy-done
  24.1 1.9 %collective-permute-start.5 = (f32[208,640]{1,0:T(8,128)}, f32[208,640]{1,0:T(8,128)}, u32[]{:S(2)}, u32[]{:S(2)}) collective-permute-start(f32[208,640]{1,0:T(8,128)} %constant_dynamic-update-slice_fusion), channel_id=1, source_target_pairs={{0,1},{1,0},{2,3},{3,2},{4,5},{5,4},{6,7},{7,6},{8,9},{9,8},{10,11... | collective-permute-start | bytes 1597448 | tf_op jit(solution)/shard_map/ppermute | solution.py:267
  26.0 0.0 copy-done.5
  26.0 0.0 copy-done.2
  26.0 5.0 %add_multiply_fusion.1.refs_0_ = f32[2,640,640]{2,1,0:T(8,128)S(1)} fusion(f32[2,64,640]{2,1,0:T(8,128)} %param.9, f32[2,640]{1,0:T(2,128)S(1)} %multiply_reduce_fusion.2, f32[2,640]{1,0:T(2,128)S(1)} %multiply_reduce_fusion.3, f32[2]{0:T(128)S(1)} %copy-done.5, s32[2,640]{1,0:T(2,128)S(1)} %copy-done.2, f32[2,640]{1,0:T(2,128)S(1)} %fusion.22, ...), kind=kOutput, calls=%fused_computation.37 | convolution fusion | flops 636600320 | bytes 3952648 | tf_op jit(solution)/shard_map/vmap()/dot_general | solution.py:24
  31.0 0.0 copy-start.1
  31.0 0.0 copy-start.4
  31.0 3.5 %fusion.12.refs_1_ = f32[640,640]{1,0:T(8,128)} fusion(f32[2,640,640]{2,1,0:T(8,128)S(1)} %add_multiply_fusion.1.refs_0_), kind=kOutput, calls=%fused_computation.40 | convolution fusion | flops 1572864000 | bytes 4915200 | tf_op jit(solution)/shard_map/dot_general | solution.py:216
  34.5 0.0 collective-permute-done.5
  34.5 0.0 copy-done.1
  34.6 0.0 copy-done.4
  34.6 0.0 copy-start.3
  34.6 27.1 %conditional.1 = (f32[2,640,640]{2,1,0:T(8,128)}, f32[640,640]{1,0:T(8,128)}) conditional(s32[]{:T(128)} %convert_element_type.20, (f32[2,640,640]{2,1,0:T(8,128)S(1)}, f32[640,640]{1,0:T(8,128)}) %tuple.12, (f32[32]{0:T(128)S(1)}, s32[]{:T(128)}, f32[208,640]{1,0:T(8,128)}, f32[208,640]{1,0:T(8,128)}, f32[64,32]{0,1:T(8,128)S(1)}, ...), branch_computations={%region_4.5_spmd, %region_5.10_spmd} | conditional | flops 7630446080 | bytes 38185736 | solution.py:336
  34.8 1.3 broadcast_select_fusion.1
  36.1 0.1 fusion.26
  36.3 0.5 fusion.6
  36.8 0.1 fusion.9
  36.9 0.1 fusion.8
  37.2 0.1 multiply_reduce_fusion.1
  37.2 0.1 multiply_reduce_fusion
  37.4 0.2 slice_reduce_fusion.1
  37.5 0.2 slice_reduce_fusion
  37.7 0.1 pad_maximum_fusion.8
  37.8 7.9 %add_multiply_fusion = f32[4,640,640]{2,1,0:T(8,128)S(1)} fusion(f32[4,640]{1,0:T(4,128)S(1)} %multiply_reduce_fusion, f32[4,640]{1,0:T(4,128)S(1)} %multiply_reduce_fusion.1, f32[4]{0:T(128)S(1)} %pad_maximum_fusion.8, s32[4,640]{1,0:T(4,128)S(1)} %maximum_convert_fusion, f32[4,640]{1,0:T(4,128)S(1)} %fusion.8, f32[2,64,640]{2,1,0:T(8,128)S(1)} %slice.107, ...), kind=kOutput, calls=%fused_computation | convolution fusion | flops 1273692160 | bytes 7905296 | tf_op jit(solution)/shard_map/cond/branch_1_fun/vmap()/dot_general | solution.py:24
  45.7 6.6 %fusion = f32[2,640,640]{2,1,0:T(8,128)} fusion(f32[4,640,640]{2,1,0:T(8,128)S(1)} %add_multiply_fusion), kind=kOutput, calls=%fused_computation.2 | convolution fusion | flops 3145728000 | bytes 9830400 | tf_op jit(solution)/shard_map/cond/branch_1_fun/dot_general | solution.py:320
  52.3 4.3 %fusion.3 = f32[640,640]{1,0:T(8,128)S(1)} fusion(f32[2,640,640]{2,1,0:T(8,128)} %fusion), kind=kOutput, calls=%fused_computation.6 | convolution fusion | flops 1572864000 | bytes 4915200 | tf_op jit(solution)/shard_map/cond/branch_1_fun/dot_general | solution.py:216
  56.7 5.0 %fusion.29 = f32[640,640]{1,0:T(8,128)} fusion(f32[640,640]{1,0:T(8,128)S(1)} %fusion.3, f32[640,640]{1,0:T(8,128)} %get-tuple-element.26), kind=kOutput, calls=%fused_computation.75 | convolution fusion | flops 1572864000 | bytes 4915200 | tf_op jit(solution)/shard_map/cond/branch_1_fun/dot_general | solution.py:216
  61.7 0.0 copy-done.3
  61.7 78.7 %shard_map.73 = f32[8,640]{1,0:T(8,128)S(1)} custom-call(f32[2,640,640]{2,1,0:T(8,128)S(1)} %add_multiply_fusion.1.refs_0_, f32[640,640]{1,0:T(8,128)} %fusion.12.refs_1_, f32[2,640,640]{2,1,0:T(8,128)} %get-tuple-element.29.refs_2_, f32[640,640]{1,0:T(8,128)} %get-tuple-element.30.refs_3_, f32[8,640]{1,0:T(8,128)S(1)} %broadcast_in_dim.17.refs_4_), custom_call_target="tpu_custom_call" | custom-call | tf_op jit(solution)/shard_map/pallas_call | solution.py:193
  140.4 0.6 fusion.24
  (24 shorter events, 0.3 us)
Async XLA Ops:
  0.0 26.0 %copy-start.5 = (f32[2]{0:T(128)S(1)}, f32[2]{0:T(128)}, u32[]{:S(2)}) copy-start(f32[2]{0:T(128)} %param.12) | copy-start | bytes 28
  0.0 26.0 %copy-start.2 = (s32[2,640]{1,0:T(2,128)S(1)}, s32[2,640]{1,0:T(2,128)}, u32[]{:S(2)}) copy-start(s32[2,640]{1,0:T(2,128)} %param.10) | copy-start | bytes 15364
  3.4 18.0 %collective-permute-start.1 = (f32[72,640]{1,0:T(8,128)S(1)}, f32[72,640]{1,0:T(8,128)S(1)}, u32[]{:S(2)}, u32[]{:S(2)}) collective-permute-start(f32[72,640]{1,0:T(8,128)S(1)} %fusion.20), channel_id=1, source_target_pairs={{104,112},{112,120},{128,136},{136,144},{152,160},{160,168},{176,1... | collective-permute-start | bytes 552968 | tf_op jit(solution)/shard_map/ppermute | solution.py:255
  4.7 17.4 %collective-permute-start.2 = (f32[72,640]{1,0:T(8,128)S(1)}, f32[72,640]{1,0:T(8,128)S(1)}, u32[]{:S(2)}, u32[]{:S(2)}) collective-permute-start(f32[72,640]{1,0:T(8,128)S(1)} %fusion.20), channel_id=1, source_target_pairs={{104,120},{128,144},{152,168},{176,192},{200,216},{224,240},{248,2... | collective-permute-start | bytes 552968 | tf_op jit(solution)/shard_map/ppermute | solution.py:255
  7.1 15.7 %collective-permute-start.3 = (f32[32,640]{1,0:T(8,128)S(1)}, f32[32,640]{1,0:T(8,128)S(1)}, u32[]{:S(2)}, u32[]{:S(2)}) collective-permute-start(f32[32,640]{1,0:T(8,128)S(1)} %dynamic-slice_bitcast_fusion), channel_id=1, source_target_pairs={{96,112},{120,136},{144,160},{168,184},{192,208},{216,232},{240,25... | collective-permute-start | bytes 245768 | tf_op jit(solution)/shard_map/ppermute | solution.py:255
  7.8 15.7 %collective-permute-start.4 = (f32[32,640]{1,0:T(8,128)S(1)}, f32[32,640]{1,0:T(8,128)S(1)}, u32[]{:S(2)}, u32[]{:S(2)}) collective-permute-start(f32[32,640]{1,0:T(8,128)S(1)} %dynamic-slice_bitcast_fusion), channel_id=1, source_target_pairs={{96,120},{120,144},{144,168},{168,192},{192,216},{216,240},{240,26... | collective-permute-start | bytes 245768 | tf_op jit(solution)/shard_map/ppermute | solution.py:255
  9.1 12.3 %collective-permute-start = (f32[64,640]{1,0:T(8,128)S(1)}, f32[64,640]{1,0:T(8,128)S(1)}, u32[]{:S(2)}, u32[]{:S(2)}) collective-permute-start(f32[64,640]{1,0:T(8,128)S(1)} %get-tuple-element.48), channel_id=1, source_target_pairs={{0,8},{8,16},{16,24},{24,32},{32,40},{40,48},{48,56},{56,64},{64,7... | collective-permute-start | bytes 491528 | tf_op jit(solution)/shard_map/ppermute | solution.py:255
  21.4 2.7 %copy-start = (f32[64,640]{1,0:T(8,128)}, f32[64,640]{1,0:T(8,128)S(1)}, u32[]{:S(2)}) copy-start(f32[64,640]{1,0:T(8,128)S(1)} %collective-permute-done) | copy-start | bytes 491524
  24.1 10.4 %collective-permute-start.5 = (f32[208,640]{1,0:T(8,128)}, f32[208,640]{1,0:T(8,128)}, u32[]{:S(2)}, u32[]{:S(2)}) collective-permute-start(f32[208,640]{1,0:T(8,128)} %constant_dynamic-update-slice_fusion), channel_id=1, source_target_pairs={{0,1},{1,0},{2,3},{3,2},{4,5},{5,4},{6,7},{7,6},{8,9},{9,8},{10,11... | collective-permute-start | bytes 1597448 | tf_op jit(solution)/shard_map/ppermute | solution.py:267
  31.0 3.5 %copy-start.1 = (f32[64,32]{0,1:T(8,128)S(1)}, f32[64,32]{0,1:T(8,128)}, u32[]{:S(2)}) copy-start(f32[64,32]{0,1:T(8,128)} %param.13) | copy-start | bytes 24580
  31.0 3.5 %copy-start.4 = (f32[32]{0:T(128)S(1)}, f32[32]{0:T(128)}, u32[]{:S(2)}) copy-start(f32[32]{0:T(128)} %param.14) | copy-start | bytes 388
  34.6 27.1 %copy-start.3 = (f32[640]{0:T(1024)S(1)}, f32[640]{0:T(1024)}, u32[]{:S(2)}) copy-start(f32[640]{0:T(1024)} %param.15) | copy-start | bytes 7684
